TPU v7x, 32 devices: a whole 2x2x4 slice. The times are simulated.
32 devices in a mesh: band: 4 (over z), tile: 8 (over y, x, core).
Axes of the slice: x: 2, y: 2, z: 4, core: 2. Of those that a mesh axis runs over, the one named last changes fastest.
Arguments:
- anomalies: bfloat16 [4, 8, 18, 80, 256], P('band', 'tile'), may hold values from -6 to 6
- forcing: float32 [4, 8, 18, 256], P('band', 'tile'), may hold values from -6 to 6
- pair_code: int32 [4, 8, 8], P('band', 'tile'), may hold values from 0 to 4, as said below
- kernel: float32 [63, 63], replicated, may hold values from 0 to 1
- tile_taper: float32 [4], replicated, may hold values from 0.03 to 0.22
Outputs:
- increment: float32 [4, 8, 18, 256], P('band', 'tile')
- residual: float32 [4, 8, 18, 256], P('band', 'tile')
Inputs may be any that keep to these rules, and one draw needn't show every extreme that they name: pair_code[b, l, k] names the pair of tile (b, l) with its neighbour in direction k; the partner's entry for the opposite direction holds the same code; no listed pair crosses the first or the last band.
All inputs are finite; a program needn't handle non-finite values.
Results may differ from a plain program's by a relative error of at most 0.014.
Values may be sent and summed in bfloat16 or wider, within the bound.
No kernel may reach another device: no remote copies, remote signals or barrier semaphores. Data moves between devices by JAX's collectives and lax.ppermute only.
A program may use at most 64 MiB of HBM per device.

v0:
```python
import jax
import jax.numpy as jnp
import numpy as np
from jax import lax
from jax.sharding import PartitionSpec as P

SIDE = 16
ITERS = 2


DIRECTIONS = ((-1, -1), (-1, 0), (-1, 1), (0, -1), (0, 1), (1, -1), (1, 0), (1, 1))


def padded(block, sides, width):
    for axis, dim in sides:
        count = lax.axis_size(axis)
        forward = [(i, i + 1) for i in range(count - 1)]
        forward.append((count - 1, 0))
        backward = [(target, source) for source, target in forward]
        low = lax.ppermute(
            lax.slice_in_dim(block, block.shape[dim] - width, None, axis=dim), axis, forward
        )
        high = lax.ppermute(lax.slice_in_dim(block, 0, width, axis=dim), axis, backward)
        block = jnp.concatenate([low, block, high], axis=dim)
    return block


def selector(tile_side, offset):
    first_index = np.arange(tile_side)[:, None]
    second_index = np.arange(tile_side)[None, :]
    target = 2 * tile_side - 1 + offset * tile_side + second_index - first_index
    return (np.arange(4 * tile_side - 1)[None, None, :] == target[:, :, None]).astype(np.float32)


def local_map(kernel, row_step, col_step):
    by_lat = jnp.einsum(
        "abp,pq->abq", selector(SIDE, row_step), kernel, precision=lax.Precision.HIGHEST
    )
    full_map = jnp.einsum(
        "abq,cdq->acbd", by_lat, selector(SIDE, col_step), precision=lax.Precision.HIGHEST
    )
    return full_map.reshape(SIDE * SIDE, SIDE * SIDE).astype(jnp.bfloat16)


def all_maps(kernel):
    return [local_map(kernel, 0, 0)] + [
        local_map(kernel, row_step, col_step) for row_step, col_step in DIRECTIONS
    ]


def taper_lookup(tile_taper, code):
    entries = jnp.arange(1, tile_taper.shape[0] + 1, dtype=jnp.int32)
    return jnp.sum(jnp.where(entries == code, tile_taper, jnp.zeros_like(tile_taper)))


def weighted_block(block, field):
    return (block.astype(jnp.float32) * field[:, None, :]).astype(jnp.bfloat16)


def pair_term(own_block, weighted, matrix, weight):
    levels, members, columns = weighted.shape
    spread = lax.dot_general(
        weighted.reshape(levels * members, columns),
        matrix,
        (((1,), (1,)), ((), ())),
        preferred_element_type=jnp.float32,
    )
    summed = jnp.sum(
        own_block.astype(jnp.float32) * spread.reshape(levels, members, columns), axis=1
    )
    return summed * (weight / (members - 1))


def masked_term(code, weight, own_block, weighted, matrix):

    def active():
        return pair_term(own_block, weighted, matrix, weight)

    def inactive():
        return jnp.zeros((weighted.shape[0], weighted.shape[2]), jnp.float32)

    return lax.cond(code > 0, active, inactive)


def covariance_all(blocks, neighbours, pair_codes, tile_taper, local_maps):
    own_block = blocks[1, 1]
    summed_terms = pair_term(
        own_block, weighted_block(own_block, neighbours[1, 1]), local_maps[0], 1.0
    )
    for position, (row_step, col_step) in enumerate(DIRECTIONS):
        code = pair_codes[position]
        weight = taper_lookup(tile_taper, code)
        other_weighted = weighted_block(
            blocks[1 + row_step, 1 + col_step], neighbours[1 + row_step, 1 + col_step]
        )
        summed_terms = summed_terms + masked_term(
            code, weight, own_block, other_weighted, local_maps[position + 1]
        )
    return summed_terms


def global_total(factor_one, factor_two):
    return lax.psum(jnp.sum(factor_one * factor_two), ("band", "tile"))


def on_device(anomalies, forcing, pair_code, kernel, tile_taper):
    pair_codes = pair_code[0, 0]
    kept_maps = all_maps(kernel)
    residual = forcing[0, 0]
    increment = jnp.zeros_like(residual)
    direction = residual
    norm_now = global_total(residual, residual)
    for iteration in range(ITERS):
        blocks = padded(anomalies, (("band", 0), ("tile", 1)), 1)
        neighbours = padded(direction[None, None], (("band", 0), ("tile", 1)), 1)
        mapped = direction + covariance_all(blocks, neighbours, pair_codes, tile_taper, kept_maps)
        step_length = norm_now / global_total(direction, mapped)
        increment = increment + step_length * direction
        residual = residual - step_length * mapped
        norm_next = global_total(residual, residual)
        direction = residual + norm_next / norm_now * direction
        norm_now = norm_next
    return (increment[None, None], residual[None, None])


def solution(mesh):
    return jax.shard_map(
        on_device,
        mesh=mesh,
        in_specs=(
            P("band", "tile", None, None, None),
            P("band", "tile", None, None),
            P("band", "tile", None),
            P(),
            P(),
        ),
        out_specs=(P("band", "tile", None, None), P("band", "tile", None, None)),
        check_vma=False,
    )
```

profile of v0, /device:TPU:0, one launch (start us, length us, event | category | flops | bytes accessed | tf_op | source)
XLA Modules:
  0.0 272.6 jit_solution(5299002742823642487)
XLA Ops:
  0.7 3.1 %collective-permute-start.3 = (f32[1,1,18,256]{3,1,2,0:T(1,128)}, f32[1,1,18,256]{3,1,2,0:T(1,128)S(1)}, u32[]{:S(2)}, u32[]{:S(2)}) collective-permute-start(f32[1,1,18,256]{3,1,2,0:T(1,128)} %param.56), channel_id=1, source_target_pairs={{0,8},{8,16},{16,24},{24,0},{1,9},{9,17},{17,25},{25,1},{2,10},{10... | collective-permute-start | bytes 55304 | tf_op jit(solution)/shard_map/ppermute | solution.py:20
  3.8 2.1 collective-permute-start.4
  5.9 3.8 %collective-permute-start.1 = (bf16[1,1,18,80,256]{4,3,2,1,0:T(8,128)(2,1)}, bf16[1,1,18,80,256]{4,3,2,1,0:T(8,128)(2,1)S(1)}, u32[]{:S(2)}, u32[]{:S(2)}) collective-permute-start(bf16[1,1,18,80,256]{4,3,2,1,0:T(8,128)(2,1)} %param.55), channel_id=1, source_target_pairs={{8,0},{16,8},{24,16},{0,24},{9,1},{17,9},{25,17},{1,25},{10,2},{18... | collective-permute-start | bytes 2211848 | tf_op jit(solution)/shard_map/ppermute | solution.py:23
  12.1 3.7 %fusion.44 = bf16[16,16,16,16]{3,2,1,0:T(8,128)(2,1)} fusion(f32[16,16,63,1]{2,1,3,0:T(8,128)S(1)} %convolution_bitcast_fusion, f32[16,16,63,1]{2,1,0,3:T(8,128)} %constant.135), kind=kOutput, calls=%fused_computation.105 | convolution fusion | flops 49610752 | bytes 260096 | tf_op jit(solution)/shard_map/abq,cdq->acbd/dot_general | solution.py:39
  15.8 2.8 %fusion.43 = bf16[16,16,16,16]{3,2,1,0:T(8,128)(2,1)} fusion(f32[16,16,63,1]{2,1,3,0:T(8,128)S(1)} %convolution_bitcast_fusion, f32[16,16,63,1]{2,1,0,3:T(8,128)S(1)} %copy-done.3), kind=kOutput, calls=%fused_computation.104 | convolution fusion | flops 49610752 | bytes 260096 | tf_op jit(solution)/shard_map/abq,cdq->acbd/dot_general | solution.py:39
  18.5 2.8 %fusion.39 = bf16[16,16,16,16]{3,2,1,0:T(8,128)(2,1)} fusion(f32[16,16,63,1]{2,1,3,0:T(8,128)S(1)} %convolution_bitcast_fusion.1, f32[16,16,63,1]{2,1,0,3:T(8,128)S(1)} %copy-done.4), kind=kOutput, calls=%fused_computation.100 | convolution fusion | flops 49610752 | bytes 260096 | tf_op jit(solution)/shard_map/abq,cdq->acbd/dot_general | solution.py:39
  21.3 2.8 %fusion.38 = bf16[16,16,16,16]{3,2,1,0:T(8,128)(2,1)} fusion(f32[16,16,63,1]{2,1,3,0:T(8,128)S(1)} %convolution_bitcast_fusion.1, f32[16,16,63,1]{2,1,0,3:T(8,128)S(1)} %copy-done.3), kind=kOutput, calls=%fused_computation.99 | convolution fusion | flops 49610752 | bytes 260096 | tf_op jit(solution)/shard_map/abq,cdq->acbd/dot_general | solution.py:39
  24.4 2.8 %fusion.42 = bf16[16,16,16,16]{3,2,1,0:T(8,128)(2,1)} fusion(f32[16,16,63,1]{2,1,3,0:T(8,128)S(1)} %convolution_bitcast_fusion, f32[16,16,63,1]{2,1,0,3:T(8,128)S(1)} %copy-done.5), kind=kOutput, calls=%fused_computation.103 | convolution fusion | flops 49610752 | bytes 260096 | tf_op jit(solution)/shard_map/abq,cdq->acbd/dot_general | solution.py:39
  27.2 2.9 %fusion.37 = bf16[16,16,16,16]{3,2,1,0:T(8,128)(2,1)} fusion(f32[16,16,63,1]{2,1,3,0:T(8,128)S(1)} %convolution_bitcast_fusion.1, f32[16,16,63,1]{2,1,0,3:T(8,128)S(1)} %copy-done.5), kind=kOutput, calls=%fused_computation.98 | convolution fusion | flops 49610752 | bytes 260096 | tf_op jit(solution)/shard_map/abq,cdq->acbd/dot_general | solution.py:39
  30.1 2.8 %fusion.41 = bf16[16,16,16,16]{3,2,1,0:T(8,128)(2,1)} fusion(f32[16,16,63,1]{2,1,3,0:T(8,128)S(1)} %convolution_bitcast_fusion.2, f32[16,16,63,1]{2,1,0,3:T(8,128)S(1)} %copy-done.4), kind=kOutput, calls=%fused_computation.102 | convolution fusion | flops 49610752 | bytes 260096 | tf_op jit(solution)/shard_map/abq,cdq->acbd/dot_general | solution.py:39
  32.9 2.8 %fusion.40 = bf16[16,16,16,16]{3,2,1,0:T(8,128)(2,1)} fusion(f32[16,16,63,1]{2,1,3,0:T(8,128)S(1)} %convolution_bitcast_fusion.2, f32[16,16,63,1]{2,1,0,3:T(8,128)S(1)} %copy-done.5), kind=kOutput, calls=%fused_computation.101 | convolution fusion | flops 49610752 | bytes 260096 | tf_op jit(solution)/shard_map/abq,cdq->acbd/dot_general | solution.py:39
  37.7 2.1 collective-permute-done.1
  41.4 1.8 fusion.36
  44.9 2.4 fusion.16
  49.8 2.6 collective-permute-start.7
  52.5 5.8 %fusion.54 = (f32[]{:T(128)}, f32[]{:T(128)}, f32[]{:T(128)}, f32[]{:T(128)}, f32[]{:T(128)}, /*index=5*/f32[]{:T(128)}, f32[]{:T(128)}, f32[]{:T(128)}) fusion(f32[4]{0:T(128)S(1)} %copy-done.24, s32[]{:T(128)} %bitcast.23, s32[]{:T(128)} %bitcast.44, s32[]{:T(128)} %bitcast.41, s32[]{:T(128)} %bitcast.37, s32[]{:T(128)} %bitcast.33, s32[]{:T(128)} %bitcast.29, ...), kind=kLoop, calls=%fused_computation.162 | loop fusion | flops 92 | bytes 80 | tf_op jit(solution)/shard_map/reduce_sum | solution.py:53
  63.3 2.8 %convert_element_type.358 = bf16[256,256]{1,0:T(8,128)(2,1)} reshape(bf16[16,16,16,16]{3,2,1,0:T(8,128)(2,1)} %fusion.44) | data formatting | bytes 262144 | tf_op jit(solution)/shard_map/convert_element_type | solution.py:42
  66.1 2.8 %convert_element_type.351 = bf16[256,256]{1,0:T(8,128)(2,1)} reshape(bf16[16,16,16,16]{3,2,1,0:T(8,128)(2,1)} %fusion.43) | data formatting | bytes 262144 | tf_op jit(solution)/shard_map/convert_element_type | solution.py:42
  69.0 2.2 convert_element_type.344
  71.2 2.8 %convert_element_type.323 = bf16[256,256]{1,0:T(8,128)(2,1)} reshape(bf16[16,16,16,16]{3,2,1,0:T(8,128)(2,1)} %fusion.39) | data formatting | bytes 262144 | tf_op jit(solution)/shard_map/convert_element_type | solution.py:42
  74.0 2.8 %convert_element_type.316 = bf16[256,256]{1,0:T(8,128)(2,1)} reshape(bf16[16,16,16,16]{3,2,1,0:T(8,128)(2,1)} %fusion.38) | data formatting | bytes 262144 | tf_op jit(solution)/shard_map/convert_element_type | solution.py:42
  76.9 2.2 convert_element_type.309
  79.1 2.8 %convert_element_type.337 = bf16[256,256]{1,0:T(8,128)(2,1)} reshape(bf16[16,16,16,16]{3,2,1,0:T(8,128)(2,1)} %fusion.41) | data formatting | bytes 262144 | tf_op jit(solution)/shard_map/convert_element_type | solution.py:42
  81.9 2.2 convert_element_type.330
  85.2 8.4 %collective-permute-done.5 = f32[3,1,18,256]{3,1,2,0:T(1,128)S(1)} collective-permute-done((f32[3,1,18,256]{3,1,2,0:T(1,128)}, f32[3,1,18,256]{3,1,2,0:T(1,128)S(1)}, u32[]{:S(2)}, u32[]{:S(2)}) %collective-permute-start.5) | collective-permute-done | bytes 55328 | tf_op jit(solution)/shard_map/ppermute | solution.py:20
  93.6 2.1 fusion.32
  95.8 3.1 %conditional.22 = (f32[18,256]{1,0:T(8,128)}) conditional(s32[]{:T(128)} %convert_element_type.345, () %tuple.116, (bf16[18,80,256]{2,1,0:T(8,128)(2,1)}, bf16[18,80,256]{2,1,0:T(8,128)(2,1)}, bf16[256,256]{1,0:T(8,128)(2,1)}, f32[]{:T(128)}) %tuple.205), branch_computations={%region_28.29_spmd, %region_29.31_spmd} | conditional | flops 189849600 | bytes 1660952 | solution.py:82
  96.4 1.8 multiply_reduce_fusion.6
  98.8 1.8 fusion.22
  101.2 3.2 %fusion.24 = (bf16[18,80,256]{2,1,0:T(8,128)(2,1)}, bf16[18,80,256]{2,1,0:T(8,128)(2,1)}, bf16[18,80,256]{2,1,0:T(8,128)(2,1)}) fusion(f32[18,256]{1,0:T(8,128)S(1)} %bitcast.289, bf16[3,1,18,80,256]{4,3,2,1,0:T(8,128)(2,1)} %collective-permute-done.6, f32[18,256]{1,0:T(8,128)S(1)} %get-tuple-element.291, f32[18,256]{1,0:T(8,128)S(1)} %get-tuple-element.292), kind=kLoop, calls=%fused_computation.85 | loop fusion | flops 3317760 | bytes 4478976 | tf_op jit(solution)/shard_map/convert_element_type | solution.py:57
  104.4 2.5 conditional.23
  105.0 1.8 multiply_reduce_fusion.7
  106.9 2.5 conditional.20
  107.5 1.8 multiply_reduce_fusion.4
  109.4 1.6 fusion.20
  111.6 3.0 %conditional.21 = (f32[18,256]{1,0:T(8,128)}) conditional(s32[]{:T(128)} %convert_element_type.338, () %tuple.114, (bf16[18,80,256]{2,1,0:T(8,128)(2,1)}, bf16[18,80,256]{2,1,0:T(8,128)(2,1)}, bf16[256,256]{1,0:T(8,128)(2,1)S(1)}, f32[]{:T(128)}) %tuple.211), branch_computations={%region_24.25_spmd, %region_25.27_spmd} | conditional | flops 189849600 | bytes 1660952 | solution.py:82
  112.2 1.7 multiply_reduce_fusion.5
  114.6 2.3 conditional.19
  115.2 1.7 multiply_reduce_fusion.3
  119.0 41.5 %all-reduce = (f32[]{:T(128)}, f32[]{:T(128)}) all-reduce(f32[]{:T(128)} %get-tuple-element.243, f32[]{:T(128)} %get-tuple-element.242), channel_id=1, replica_groups=mesh['band'=4,'tile'=8] {'band','tile'}, use_global_device_ids=true, to_apply=%region_1.0 | all-reduce | flops 2 | bytes 16 | tf_op jit(solution)/shard_map/psum | solution.py:103
  162.4 38.4 %psum.30 = f32[]{:T(128)} all-reduce(f32[]{:T(128)} %multiply_reduce_fusion.17), channel_id=1, replica_groups=mesh['band'=4,'tile'=8] {'band','tile'}, use_global_device_ids=true, to_apply=%region_38.39 | all-reduce | flops 1 | bytes 8 | tf_op jit(solution)/shard_map/psum | solution.py:103
  204.2 1.8 fusion.17
  206.0 3.1 %collective-permute-done.8 = f32[1,1,18,256]{3,2,1,0:T(8,128)S(1)} collective-permute-done((f32[1,1,18,256]{3,2,1,0:T(8,128)S(1)}, f32[1,1,18,256]{3,2,1,0:T(8,128)S(1)}, u32[]{:S(2)}, u32[]{:S(2)}) %collective-permute-start.8) | collective-permute-done | bytes 18464 | tf_op jit(solution)/shard_map/ppermute | solution.py:20
  212.4 2.5 conditional.30
  213.1 1.8 multiply_reduce_fusion.14
  215.8 3.2 %fusion.25 = (bf16[18,80,256]{2,1,0:T(8,128)(2,1)}, bf16[18,80,256]{2,1,0:T(8,128)(2,1)}, bf16[18,80,256]{2,1,0:T(8,128)(2,1)}) fusion(f32[18,256]{1,0:T(8,128)S(1)} %get-tuple-element.272, bf16[3,1,18,80,256]{4,3,2,1,0:T(8,128)(2,1)} %collective-permute-done.6, f32[18,256]{1,0:T(8,128)S(1)} %get-tuple-element.273, f32[18,256]{1,0:T(8,128)S(1)} %get-tuple-element.274), kind=kLoop, calls=%fused_computation.86 | loop fusion | flops 3317760 | bytes 4478976 | tf_op jit(solution)/shard_map/convert_element_type | solution.py:57
  219.8 1.6 fusion.21
  228.6 41.5 %psum.31 = f32[]{:T(128)} all-reduce(f32[]{:T(128)} %get-tuple-element.254), channel_id=1, replica_groups=mesh['band'=4,'tile'=8] {'band','tile'}, use_global_device_ids=true, to_apply=%region_65.66 | all-reduce | flops 1 | bytes 8 | tf_op jit(solution)/shard_map/psum | solution.py:103
  (129 shorter events, 34.3 us)
Async XLA Ops:
  0.6 9.1 %copy-start = (f32[63,63]{1,0:T(8,128)S(1)}, f32[63,63]{1,0:T(8,128)}, u32[]{:S(2)}) copy-start(f32[63,63]{1,0:T(8,128)} %param.58) | copy-start | bytes 47632
  0.6 15.1 %copy-start.3 = (f32[16,16,63,1]{2,1,0,3:T(8,128)S(1)}, f32[16,16,63,1]{2,1,0,3:T(8,128)}, u32[]{:S(2)}) copy-start(f32[16,16,63,1]{2,1,0,3:T(8,128)} %constant.133) | copy-start | bytes 193540
  0.7 47.3 %collective-permute-start.3 = (f32[1,1,18,256]{3,1,2,0:T(1,128)}, f32[1,1,18,256]{3,1,2,0:T(1,128)S(1)}, u32[]{:S(2)}, u32[]{:S(2)}) collective-permute-start(f32[1,1,18,256]{3,1,2,0:T(1,128)} %param.56), channel_id=1, source_target_pairs={{0,8},{8,16},{16,24},{24,0},{1,9},{9,17},{17,25},{25,1},{2,10},{10... | collective-permute-start | bytes 55304 | tf_op jit(solution)/shard_map/ppermute | solution.py:20
  3.8 45.4 %collective-permute-start.4 = (f32[1,1,18,256]{3,1,2,0:T(1,128)}, f32[1,1,18,256]{3,1,2,0:T(1,128)S(1)}, u32[]{:S(2)}, u32[]{:S(2)}) collective-permute-start(f32[1,1,18,256]{3,1,2,0:T(1,128)} %param.56), channel_id=1, source_target_pairs={{8,0},{16,8},{24,16},{0,24},{9,1},{17,9},{25,17},{1,25},{10,2},{18... | collective-permute-start | bytes 55304 | tf_op jit(solution)/shard_map/ppermute | solution.py:23
  5.9 29.8 %collective-permute-start = (bf16[1,1,18,80,256]{4,3,2,1,0:T(8,128)(2,1)}, bf16[1,1,18,80,256]{4,3,2,1,0:T(8,128)(2,1)S(1)}, u32[]{:S(2)}, u32[]{:S(2)}) collective-permute-start(bf16[1,1,18,80,256]{4,3,2,1,0:T(8,128)(2,1)} %param.55), channel_id=1, source_target_pairs={{0,8},{8,16},{16,24},{24,0},{1,9},{9,17},{17,25},{25,1},{2,10},{10... | collective-permute-start | bytes 2211848 | tf_op jit(solution)/shard_map/ppermute | solution.py:20
  5.9 34.0 %collective-permute-start.1 = (bf16[1,1,18,80,256]{4,3,2,1,0:T(8,128)(2,1)}, bf16[1,1,18,80,256]{4,3,2,1,0:T(8,128)(2,1)S(1)}, u32[]{:S(2)}, u32[]{:S(2)}) collective-permute-start(bf16[1,1,18,80,256]{4,3,2,1,0:T(8,128)(2,1)} %param.55), channel_id=1, source_target_pairs={{8,0},{16,8},{24,16},{0,24},{9,1},{17,9},{25,17},{1,25},{10,2},{18... | collective-permute-start | bytes 2211848 | tf_op jit(solution)/shard_map/ppermute | solution.py:23
  10.8 7.7 %copy-start.4 = (f32[16,16,63,1]{2,1,0,3:T(8,128)S(1)}, f32[16,16,63,1]{2,1,0,3:T(8,128)}, u32[]{:S(2)}) copy-start(f32[16,16,63,1]{2,1,0,3:T(8,128)} %constant.135) | copy-start | bytes 193540
  18.5 5.6 %copy-start.18 = (f32[16,16,63]{2,1,0:T(8,128)S(1)}, f32[16,16,63]{2,1,0:T(8,128)}, u32[]{:S(2)}) copy-start(f32[16,16,63]{2,1,0:T(8,128)} %constant.127.clone) | copy-start | bytes 193540
  18.5 5.9 %copy-start.5 = (f32[16,16,63,1]{2,1,0,3:T(8,128)S(1)}, f32[16,16,63,1]{2,1,0,3:T(8,128)}, u32[]{:S(2)}) copy-start(f32[16,16,63,1]{2,1,0,3:T(8,128)} %constant.134) | copy-start | bytes 193540
  32.9 3.9 %copy-start.6 = (bf16[1,1,18,80,256]{4,3,2,1,0:T(8,128)(2,1)S(1)}, bf16[1,1,18,80,256]{4,3,2,1,0:T(8,128)(2,1)}, u32[]{:S(2)}) copy-start(bf16[1,1,18,80,256]{4,3,2,1,0:T(8,128)(2,1)} %param.55) | copy-start | bytes 2211844
  37.7 5.5 %copy-start.14 = (f32[1,1,18,256]{3,1,2,0:T(1,128)S(1)}, f32[1,1,18,256]{3,1,2,0:T(1,128)}, u32[]{:S(2)}) copy-start(f32[1,1,18,256]{3,1,2,0:T(1,128)} %param.56) | copy-start | bytes 55300
  39.8 4.4 %copy-start.1 = (bf16[1,1,18,80,256]{4,3,2,1,0:T(8,128)(2,1)}, bf16[1,1,18,80,256]{4,3,2,1,0:T(8,128)(2,1)S(1)}, u32[]{:S(2)}) copy-start(bf16[1,1,18,80,256]{4,3,2,1,0:T(8,128)(2,1)S(1)} %collective-permute-done.1) | copy-start | bytes 2211844
  40.8 60.4 %collective-permute-start.6 = (bf16[3,1,18,80,256]{4,3,2,1,0:T(8,128)(2,1)}, bf16[3,1,18,80,256]{4,3,2,1,0:T(8,128)(2,1)}, u32[]{:S(2)}, u32[]{:S(2)}) collective-permute-start(bf16[3,1,18,80,256]{4,3,2,1,0:T(8,128)(2,1)} %constant_dynamic-update-slice_fusion), channel_id=1, source_target_pairs={{1,0},{2,1},{3,2},{4,3},{5,4},{6,5},{7,6},{0,7},{9,8},{10,9},{11,1... | collective-permute-start | bytes 6635528 | tf_op jit(solution)/shard_map/ppermute | solution.py:23
  43.2 4.1 %copy-start.23 = (s32[1,1,8]{2,1,0:T(1,128)S(1)}, s32[1,1,8]{2,1,0:T(1,128)}, u32[]{:S(2)}) copy-start(s32[1,1,8]{2,1,0:T(1,128)} %param.57) | copy-start | bytes 100
  43.2 9.2 %copy-start.24 = (f32[4]{0:T(128)S(1)}, f32[4]{0:T(128)}, u32[]{:S(2)}) copy-start(f32[4]{0:T(128)} %param.59) | copy-start | bytes 52
  44.3 0.7 copy-start.17
  47.3 62.1 %collective-permute-start.2 = (bf16[3,1,18,80,256]{4,3,2,1,0:T(8,128)(2,1)}, bf16[3,1,18,80,256]{4,3,2,1,0:T(8,128)(2,1)S(1)}, u32[]{:S(2)}, u32[]{:S(2)}) collective-permute-start(bf16[3,1,18,80,256]{4,3,2,1,0:T(8,128)(2,1)} %constant_dynamic-update-slice_fusion), channel_id=1, source_target_pairs={{0,1},{1,2},{2,3},{3,4},{4,5},{5,6},{6,7},{7,0},{8,9},{9,10},{10,1... | collective-permute-start | bytes 6635528 | tf_op jit(solution)/shard_map/ppermute | solution.py:20
  49.8 35.3 %collective-permute-start.7 = (f32[3,1,18,256]{3,1,2,0:T(1,128)}, f32[3,1,18,256]{3,1,2,0:T(1,128)S(1)}, u32[]{:S(2)}, u32[]{:S(2)}) collective-permute-start(f32[3,1,18,256]{3,1,2,0:T(1,128)} %constant_dynamic-update-slice_fusion.3), channel_id=1, source_target_pairs={{1,0},{2,1},{3,2},{4,3},{5,4},{6,5},{7,6},{0,7},{9,8},{10,9},{11,1... | collective-permute-start | bytes 165896 | tf_op jit(solution)/shard_map/ppermute | solution.py:23
  84.1 9.4 %collective-permute-start.5 = (f32[3,1,18,256]{3,1,2,0:T(1,128)}, f32[3,1,18,256]{3,1,2,0:T(1,128)S(1)}, u32[]{:S(2)}, u32[]{:S(2)}) collective-permute-start(f32[3,1,18,256]{3,1,2,0:T(1,128)} %constant_dynamic-update-slice_fusion.3), channel_id=1, source_target_pairs={{0,1},{1,2},{2,3},{3,4},{4,5},{5,6},{6,7},{7,0},{8,9},{9,10},{10,1... | collective-permute-start | bytes 165896 | tf_op jit(solution)/shard_map/ppermute | solution.py:20
  111.0 0.6 copy-start.21
  114.6 2.9 %copy-start.19 = (f32[18,256]{1,0:T(8,128)S(1)}, f32[18,256]{1,0:T(8,128)}, u32[]{:S(2)}) copy-start(f32[18,256]{1,0:T(8,128)} %get-tuple-element.301) | copy-start | bytes 55300
  114.6 2.9 %copy-start.20 = (f32[18,256]{1,0:T(8,128)S(1)}, f32[18,256]{1,0:T(8,128)}, u32[]{:S(2)}) copy-start(f32[18,256]{1,0:T(8,128)} %get-tuple-element.296) | copy-start | bytes 55300
  116.9 0.6 copy-start.22
  202.0 8.4 %copy-start.2 = (bf16[1,1,18,80,256]{4,3,2,1,0:T(8,128)(2,1)S(1)}, bf16[1,1,18,80,256]{4,3,2,1,0:T(8,128)(2,1)}, u32[]{:S(2)}) copy-start(bf16[1,1,18,80,256]{4,3,2,1,0:T(8,128)(2,1)} %copy-done.1) | copy-start | bytes 2211844
  202.0 4.0 %collective-permute-start.9 = (f32[1,1,18,256]{3,2,1,0:T(8,128)S(1)}, f32[1,1,18,256]{3,2,1,0:T(8,128)S(1)}, u32[]{:S(2)}, u32[]{:S(2)}) collective-permute-start(f32[1,1,18,256]{3,2,1,0:T(8,128)S(1)} %bitcast.285), channel_id=1, source_target_pairs={{8,0},{16,8},{24,16},{0,24},{9,1},{17,9},{25,17},{1,25},{10,2},{18... | collective-permute-start | bytes 55304 | tf_op jit(solution)/shard_map/ppermute | solution.py:23
  203.6 5.6 %collective-permute-start.8 = (f32[1,1,18,256]{3,2,1,0:T(8,128)S(1)}, f32[1,1,18,256]{3,2,1,0:T(8,128)S(1)}, u32[]{:S(2)}, u32[]{:S(2)}) collective-permute-start(f32[1,1,18,256]{3,2,1,0:T(8,128)S(1)} %bitcast.286), channel_id=1, source_target_pairs={{0,8},{8,16},{16,24},{24,0},{1,9},{9,17},{17,25},{25,1},{2,10},{10... | collective-permute-start | bytes 55304 | tf_op jit(solution)/shard_map/ppermute | solution.py:20
  209.8 5.2 %collective-permute-start.11 = (f32[3,1,18,256]{3,2,1,0:T(8,128)}, f32[3,1,18,256]{3,2,1,0:T(8,128)}, u32[]{:S(2)}, u32[]{:S(2)}) collective-permute-start(f32[3,1,18,256]{3,2,1,0:T(8,128)} %pad_maximum_fusion), channel_id=1, source_target_pairs={{1,0},{2,1},{3,2},{4,3},{5,4},{6,5},{7,6},{0,7},{9,8},{10,9},{11,1... | collective-permute-start | bytes 165896 | tf_op jit(solution)/shard_map/ppermute | solution.py:23
  209.8 9.1 %collective-permute-start.10 = (f32[3,1,18,256]{3,2,1,0:T(8,128)}, f32[3,1,18,256]{3,2,1,0:T(8,128)}, u32[]{:S(2)}, u32[]{:S(2)}) collective-permute-start(f32[3,1,18,256]{3,2,1,0:T(8,128)} %pad_maximum_fusion), channel_id=1, source_target_pairs={{0,1},{1,2},{2,3},{3,4},{4,5},{5,6},{6,7},{7,0},{8,9},{9,10},{10,1... | collective-permute-start | bytes 165896 | tf_op jit(solution)/shard_map/ppermute | solution.py:20
  212.4 2.5 copy-start.13
  219.7 1.6 copy-start.7
  221.3 1.1 copy-start.12
  221.3 1.1 copy-start.16
  222.5 1.1 copy-start.11
  222.5 1.1 copy-start.15
  223.6 1.1 copy-start.10
  224.8 1.1 copy-start.9
  225.9 1.1 copy-start.8
where the time goes:
time: 276 us; the launch traced here: 273 us
  blocking collectives  121 us (44%)
  matrix products  44.3 us (16%)
  local copies, waits for them, and re-layouts  35.5 us (13%)
  other arithmetic  26 us (9%)
  starting transfers between devices  15 us (5%)
  waiting for transfers between devices  14 us (5%)
  between operations  9.82 us (4%)
  loops' own time  6.65 us (2%)
    psum x3, blocking collectives, global_total(): return lax.psum(jnp.sum(factor_one * factor_two), ('band', 'tile'))  121 us
    dot_general x9, matrix products, local_map(): jnp.einsum('abq,cdq->acbd', by_lat, selector(SIDE, col_step), precision=l...  25.2 us
    convert_element_type x9, local copies, waits for them, and re-layouts, local_map(): return full_map.reshape(SIDE * SIDE, SIDE * SIDE).astype(jnp.bfloat16)  21.8 us
    dot_general x12, matrix products, pair_term(): lax.dot_general(weighted.reshape(levels * members, columns), matrix, (((1...  16.5 us
    convert_element_type x8, other arithmetic, weighted_block(): return (block.astype(jnp.float32) * field[:, None, :]).astype(jnp.bfloat16)  15.6 us
    ppermute x6, waiting for transfers between devices, padded(): lax.ppermute(lax.slice_in_dim(block, block.shape[dim] - width, None, axis...  11.6 us
    ppermute x6, starting transfers between devices, padded(): lax.ppermute(lax.slice_in_dim(block, 0, width, axis=dim), axis, backward)  10.7 us
    unnamed x61, local copies, waits for them, and re-layouts  8 us
  transfers between devices with their start and end apart: 12, of which 4 were waited for; matrix products, arithmetic and copies ran while one was open for 32% of the time, Pallas kernels for 0%

commit v1 on v0

--- a/solution.py
+++ b/solution.py
@@ -1,14 +1,427 @@
+import functools
+
 import jax
 import jax.numpy as jnp
 import numpy as np
 from jax import lax
+from jax.experimental import pallas as pl
+from jax.experimental.pallas import tpu as pltpu
 from jax.sharding import PartitionSpec as P
 
 SIDE = 16
 ITERS = 2
-
+GRAIN = 8
+LANES = 128
+SLOT = 32
 
 DIRECTIONS = ((-1, -1), (-1, 0), (-1, 1), (0, -1), (0, 1), (1, -1), (1, 0), (1, 1))
+ALL_STEPS = ((0, 0),) + DIRECTIONS
+
+
+class Plan:
+    def __init__(self, bands, lons, levels, members, columns):
+        self.bands, self.lons = bands, lons
+        self.levels, self.members, self.columns = levels, members, columns
+        self.count = bands * lons
+        self.depth = members // (2 * GRAIN)
+        self.rows = GRAIN * (self.depth + 1)
+        self.fits = (
+            members % (2 * GRAIN) == 0
+            and levels % (self.depth + 1) == 0
+            and levels <= SLOT
+            and lons % GRAIN == 0
+            and columns == 2 * LANES
+            and self.rows % 16 == 0
+        )
+        if not self.fits:
+            return
+        self.groups = levels // (self.depth + 1)
+        chips = self.count // 2
+        used = self.groups * self.depth
+        self.fits = used <= chips < 2 * used
+        if not self.fits:
+            return
+        across = lons // 2
+        inner = [i ^ (i >> 1) for i in range(across)]
+        if sorted(inner) != list(range(across)):
+            inner = list(range(across))
+        path = []
+        for band in range(bands):
+            path += [band * across + c for c in (inner if band % 2 == 0 else inner[::-1])]
+        self.path = path
+        self.extra = 2 * self.rows
+        self.height = self.extra + 16
+
+    def device(self, group, k, core):
+        return 2 * self.path[group * self.depth + k] + core
+
+    def owners(self):
+        for group in range(self.groups):
+            for k in range(self.depth):
+                for core in range(2):
+                    low = group * (self.depth + 1) + k
+                    yield self.device(group, k, core), k, core, low
+
+    def table(self):
+        out = np.zeros((self.count, 8), np.int32)
+        for device, k, core, low in self.owners():
+            last = k == self.depth - 1
+            out[device, :5] = (self.depth - k, core, int(core == 0), int(core == 1 and last), low)
+        return out
+
+    def onward(self):
+        pairs = []
+        for group in range(self.groups):
+            for k in range(self.depth - 1):
+                for core in range(2):
+                    pairs.append((self.device(group, k, core), self.device(group, k + 1, core)))
+        return pairs
+
+
+def in_three(x):
+    high = x.astype(jnp.bfloat16).astype(jnp.float32)
+    rest = x - high
+    middle = rest.astype(jnp.bfloat16).astype(jnp.float32)
+    return high, middle, rest - middle
+
+
+def pack_kernel(plan, tapers, code_ref, taper_ref, a_ref, f_ref, out_ref, ext_ref):
+    parts = in_three(f_ref[...])
+    lane = lax.broadcasted_iota(jnp.int32, (1, LANES), 1)
+    weights = jnp.zeros((1, LANES), jnp.float32)
+    for k in range(len(DIRECTIONS)):
+        code = code_ref[0, 0, k]
+        weight = jnp.float32(0)
+        for c in range(tapers):
+            weight = jnp.where(code == c + 1, taper_ref[c], weight)
+        weights = jnp.where(lane == k, weight, weights)
+    weights = in_three(weights / jnp.float32(plan.members - 1))
+    blank = jnp.zeros((1, LANES), jnp.float32)
+    rows, depth = plan.rows, plan.depth
+    taken = set()
+    for device, k, core, low in plan.owners():
+        taken.add(device)
+        count = GRAIN * (depth - k)
+        start = 2 * k * GRAIN + core * count
+        other = GRAIN * (k + 1)
+        for half in range(2):
+            lanes = slice(half * LANES, (half + 1) * LANES)
+            base = half * rows
+            out_ref[device, base : base + count, :] = a_ref[low, start : start + count, lanes]
+            out_ref[device, base + count : base + rows, :] = a_ref[
+                low + 1, core * other : (core + 1) * other, lanes
+            ]
+            for level in range(2):
+                for n, part in enumerate(parts):
+                    row = 6 * half + 3 * level + n
+                    ext_ref[device, row : row + 1, :] = part[low + level : low + level + 1, lanes]
+        for n, part in enumerate(weights):
+            ext_ref[device, 12 + n : 13 + n, :] = part
+        ext_ref[device, 15:16, :] = blank
+    for device in range(plan.count):
+        if device in taken:
+            out_ref[device, plan.extra : plan.extra + 16, :] = ext_ref[device].astype(jnp.bfloat16)
+        else:
+            out_ref[device] = jnp.zeros((plan.height, LANES), jnp.bfloat16)
+
+
+def build_maps(side, kernel_ref, lt_ref, by_lat_ref, turned_ref):
+    span = 4 * side - 1
+    wide = (span + 1) * side
+    square = (lax.broadcasted_iota(jnp.int32, (span, span), 0)
+              == lax.broadcasted_iota(jnp.int32, (span, span), 1))
+    table = kernel_ref[...].astype(jnp.bfloat16)
+    flipped = lax.dot_general(
+        square.astype(jnp.float32).astype(jnp.bfloat16), table, (((1,), (1,)), ((), ())),
+        preferred_element_type=jnp.float32,
+    ).astype(jnp.bfloat16)
+    block = lax.broadcasted_iota(jnp.int32, (span, wide), 1) // side
+    pick = (lax.broadcasted_iota(jnp.int32, (span, wide), 0) == span - 1 - block)
+    by_lat_ref[...] = jnp.dot(
+        flipped, pick.astype(jnp.float32).astype(jnp.bfloat16), preferred_element_type=jnp.float32
+    )
+    lane = lax.broadcasted_iota(jnp.int32, (3 * side, wide), 1) % side
+    base = jnp.zeros((3 * side, wide), jnp.float32)
+    for x in range(side):
+        base = jnp.where(lane == x, by_lat_ref[side - 1 - x : 4 * side - 1 - x, :], base)
+    turns = LANES // side
+    for turn in range(turns):
+        moved = base if turn == 0 else pltpu.roll(base, wide - turn * side, 1)
+        turned_ref[turn] = moved.astype(jnp.bfloat16)
+    for k, (p, q) in enumerate(ALL_STEPS):
+        for y in range(side):
+            start = (2 * side - 1 - p * side - y) * side
+            turn, first = (start % LANES) // side, start // LANES * LANES
+            lt_ref[k, y * side : (y + 1) * side, :] = turned_ref[
+                turn, (q + 1) * side : (q + 2) * side, first : first + side * side
+            ]
+
+
+def read_weights(plan, got_ref, wide_ref):
+    extra = got_ref[:, plan.extra : plan.extra + 16, :].astype(jnp.float32)
+    weights = extra[:, 12, :] + extra[:, 13, :] + extra[:, 14, :]
+    for k in range(len(DIRECTIONS)):
+        wide_ref[k] = jnp.broadcast_to(weights[:, k : k + 1], (plan.count, plan.columns))
+    return extra
+
+
+def forcing_of(extra, level):
+    halves = []
+    for half in range(2):
+        row = 6 * half + 3 * level
+        halves.append(extra[:, row, :] + extra[:, row + 1, :] + extra[:, row + 2, :])
+    return jnp.concatenate(halves, axis=1)
+
+
+def apply_rows(plan, low, got_ref, v_ref, lt_ref, wide_ref, w_ref, s_ref, p_ref):
+    bands, lons, rows, columns = plan.bands, plan.lons, plan.rows, plan.columns
+    grains = rows // GRAIN
+    stride = lons + 2
+
+    def weigh(band, carry):
+        for l in range(lons):
+            tile = band * lons + l
+            v_low = v_ref[0, pl.ds(tile, 1), :]
+            v_high = v_ref[1, pl.ds(tile, 1), :]
+            halves = []
+            for half in range(2):
+                lanes = slice(half * LANES, (half + 1) * LANES)
+                block = got_ref[tile, half * rows : (half + 1) * rows, :].astype(jnp.float32)
+                pieces = []
+                for g in range(grains):
+                    v = jnp.where(g < low, v_low[:, lanes], v_high[:, lanes])
+                    pieces.append(block[g * GRAIN : (g + 1) * GRAIN] * v)
+                halves.append(jnp.concatenate(pieces, axis=0))
+            weighted = jnp.concatenate(halves, axis=1).astype(jnp.bfloat16)
+            places = [l + 1] + ([0] if l == lons - 1 else []) + ([lons + 1] if l == 0 else [])
+            for place in places:
+                at = pl.multiple_of((band * stride + place) * rows, 16)
+                w_ref[pl.ds(at, rows), :] = weighted
+        return carry
+
+    lax.fori_loop(0, bands, weigh, 0)
+
+    for k, (p, q) in enumerate(ALL_STEPS):
+
+        def spread(band, carry, k=k, p=p, q=q):
+            at = pl.multiple_of(((band + p) * stride + 1 + q) * rows, 16)
+            y = jnp.dot(w_ref[pl.ds(at, lons * rows), :], lt_ref[k], preferred_element_type=jnp.float32)
+            for l in range(lons):
+                tile = band * lons + l
+                piece = y[l * rows : (l + 1) * rows]
+                if k == 0:
+                    s_ref[tile] = piece * jnp.float32(1.0 / (plan.members - 1))
+                else:
+                    s_ref[tile] += piece * wide_ref[k - 1, pl.ds(tile, 1), :]
+            return carry
+
+        lax.fori_loop(max(0, -p), min(bands, bands - p), spread, 0)
+
+    def gather(band, carry):
+        sums = [[[], []], [[], []]]
+        for l in range(lons):
+            tile = band * lons + l
+            for half in range(2):
+                lanes = slice(half * LANES, (half + 1) * LANES)
+                block = got_ref[tile, half * rows : (half + 1) * rows, :].astype(jnp.float32)
+                product = block * s_ref[tile, :, lanes]
+                lo = jnp.zeros((GRAIN, LANES), jnp.float32)
+                hi = jnp.zeros((GRAIN, LANES), jnp.float32)
+                for g in range(grains):
+                    piece = product[g * GRAIN : (g + 1) * GRAIN]
+                    share = jnp.where(g < low, jnp.float32(1), jnp.float32(0))
+                    lo = lo + piece * share
+                    hi = hi + piece * (1 - share)
+                sums[0][half].append(jnp.sum(lo, axis=0, keepdims=True))
+                sums[1][half].append(jnp.sum(hi, axis=0, keepdims=True))
+        for level in range(2):
+            p_ref[level, band] = jnp.concatenate(
+                [jnp.concatenate(sums[level][half], axis=0) for half in range(2)], axis=1
+            )
+        return carry
+
+    lax.fori_loop(0, bands, gather, 0)
+
+
+def first_kernel(plan, side, info_ref, got_ref, kernel_ref, p_ref, lt_ref,
+                 by_lat_ref, turned_ref, v_ref, wide_ref, w_ref, s_ref):
+    build_maps(side, kernel_ref, lt_ref, by_lat_ref, turned_ref)
+    extra = read_weights(plan, got_ref, wide_ref)
+    v_ref[0] = forcing_of(extra, 0)
+    v_ref[1] = forcing_of(extra, 1)
+    apply_rows(plan, info_ref[0], got_ref, v_ref, lt_ref, wide_ref, w_ref, s_ref, p_ref)
+
+
+def total(x):
+    return jnp.sum(jnp.sum(x, axis=1, keepdims=True), axis=0, keepdims=True)
+
+
+def second_kernel(plan, info_ref, got_ref, lt_ref, sum_ref, before_ref, after_ref, out_ref,
+                  v_ref, wide_ref, w_ref, s_ref, p_ref):
+    extra = read_weights(plan, got_ref, wide_ref)
+    images = (sum_ref[0] + before_ref[...], sum_ref[1] + after_ref[...])
+    lane = lax.broadcasted_iota(jnp.int32, (1, LANES), 1)
+    first = jnp.zeros((1, LANES), jnp.float32)
+    for level in range(2):
+        b = forcing_of(extra, level)
+        u = images[level]
+        bb, bu = total(b * b), total(b * u)
+        ratio = jnp.where(bb > 0, bu / jnp.where(bb > 0, bb, 1.0), 0.0)
+        rest = ratio * b - u
+        v_ref[level] = rest
+        values = (bb, total(b * rest), total(rest * rest), ratio)
+        speaks = jnp.where(info_ref[2 + level] > 0, jnp.float32(1), jnp.float32(0))
+        for n, value in enumerate(values):
+            at = lane == info_ref[4] + level + SLOT * n
+            first = first + jnp.where(at, value, 0.0) * speaks
+    apply_rows(plan, info_ref[0], got_ref, v_ref, lt_ref, wide_ref, w_ref, s_ref, p_ref)
+    second = jnp.zeros((1, LANES), jnp.float32)
+    for level in range(2):
+        b = forcing_of(extra, level)
+        t = p_ref[level].reshape(plan.count, plan.columns)
+        for n, value in enumerate((total(v_ref[level] * t), total(b * t))):
+            at = lane == info_ref[4] + level + SLOT * n
+            second = second + jnp.where(at, value, 0.0)
+    mine = jnp.where(info_ref[1] == 0, images[0], images[1])
+    for half in range(2):
+        lanes = slice(half * LANES, (half + 1) * LANES)
+        out_ref[:, half, :] = mine[:, lanes]
+        for level in range(2):
+            share = p_ref[level, :, :, lanes].reshape(plan.count, LANES)
+            out_ref[:, 2 + 2 * level + half, :] = share
+    out_ref[:, 6, :] = jnp.broadcast_to(first, (plan.count, LANES))
+    out_ref[:, 7, :] = jnp.broadcast_to(second, (plan.count, LANES))
+
+
+def last_kernel(plan, f_ref, got_ref, inc_ref, res_ref, u_ref, t_ref):
+    depth = plan.depth
+    for level in range(plan.levels):
+        group, j = divmod(level, depth + 1)
+        speaker = plan.device(group, j, 0) if j < depth else plan.device(group, depth - 1, 1)
+        for half in range(2):
+            lanes = slice(half * LANES, (half + 1) * LANES)
+            u_ref[level : level + 1, lanes] = got_ref[speaker, half : half + 1, :]
+            t = None
+            for core in range(2):
+                for part in (0, 1):
+                    k = j - part
+                    if 0 <= k < depth:
+                        row = 2 + 2 * part + half
+                        term = got_ref[plan.device(group, k, core), row : row + 1, :]
+                        t = term if t is None else t + term
+            t_ref[level : level + 1, lanes] = t
+    firsts = jnp.zeros((1, LANES), jnp.float32)
+    seconds = jnp.zeros((1, LANES), jnp.float32)
+    for device, _, _, _ in plan.owners():
+        firsts = firsts + got_ref[device, 6:7, :]
+        seconds = seconds + got_ref[device, 7:8, :]
+    lane = lax.broadcasted_iota(jnp.int32, (1, LANES), 1)
+    kept = lane < plan.levels
+
+    def slot(row, n):
+        moved = row if n == 0 else pltpu.roll(row, LANES - SLOT * n, 1)
+        return jnp.where(kept, moved, 0.0)
+
+    bb, bq, qq, ratio = (slot(firsts, n) for n in range(4))
+    qt, bt = (slot(seconds, n) for n in range(2))
+
+    def add(x):
+        return jnp.sum(x, axis=1, keepdims=True)
+
+    all_bb = add(bb)
+    all_bu = add(ratio * bb - bq)
+    whole = all_bu / all_bb
+    shift = jnp.where(kept, whole - ratio, 0.0)
+    q_q = add(shift * shift * bb + 2 * shift * bq + qq)
+    q_bq = add(shift * shift * ratio * bb - shift * shift * bq + shift * bt
+               + shift * ratio * bq - shift * qq + qt)
+    b_bq = add(shift * ratio * bb - shift * bq + bt)
+    q_u = add(shift * ratio * bb - shift * bq + ratio * bq - qq)
+    energy = all_bb + all_bu
+    step_0 = all_bb / energy
+    norm_1 = step_0 * step_0 * q_q
+    turn = norm_1 / all_bb
+    curve = (step_0 * step_0 * (q_q + q_bq) + turn * step_0 * (q_u + b_bq) + turn * turn * energy)
+    step_1 = norm_1 / curve
+
+    rows = lax.broadcasted_iota(jnp.int32, (plan.levels, LANES), 0)
+    diagonal = rows == lax.broadcasted_iota(jnp.int32, (plan.levels, LANES), 1)
+    ratio_c = add(jnp.where(diagonal, ratio, 0.0))
+    shift_c = add(jnp.where(diagonal, shift, 0.0))
+    b, u, t = f_ref[...], u_ref[...], t_ref[...]
+    q = shift_c * b + (ratio_c * b - u)
+    b_of_q = shift_c * u + t
+    direction = step_0 * q + turn * b
+    inc_ref[...] = step_0 * b + step_1 * direction
+    res_ref[...] = step_0 * q - step_1 * (step_0 * (q + b_of_q) + turn * (b + u))
+
+
+def vmem():
+    return pl.BlockSpec(memory_space=pltpu.VMEM)
+
+
+def smem():
+    return pl.BlockSpec(memory_space=pltpu.SMEM)
+
+
+def by_levels(plan, anomalies, forcing, pair_code, kernel, tile_taper):
+    axes = ("band", "tile")
+    bf16, f32 = jnp.bfloat16, jnp.float32
+    n, rows, columns = plan.count, plan.rows, plan.columns
+    side = (kernel.shape[0] + 1) // 4
+    wide = 4 * side * side
+    a, f = anomalies[0, 0], forcing[0, 0]
+    sent = pl.pallas_call(
+        functools.partial(pack_kernel, plan, tile_taper.shape[0]),
+        out_shape=jax.ShapeDtypeStruct((n, plan.height, LANES), bf16),
+        in_specs=[smem(), smem(), vmem(), vmem()],
+        out_specs=vmem(),
+        scratch_shapes=[pltpu.VMEM((n, 16, LANES), f32)],
+        name="pack",
+    )(pair_code, tile_taper, a, f)
+    got = lax.all_to_all(sent, axes, 0, 0)
+    me = lax.axis_index(axes)
+    info = lax.dynamic_slice(jnp.asarray(plan.table()), (me, 0), (1, 8))[0]
+    work = [
+        pltpu.VMEM((2, n, columns), f32),
+        pltpu.VMEM((len(DIRECTIONS), n, columns), f32),
+        pltpu.VMEM((plan.bands * (plan.lons + 2) * rows, columns), bf16),
+        pltpu.VMEM((n, rows, columns), f32),
+    ]
+    part, maps = pl.pallas_call(
+        functools.partial(first_kernel, plan, side),
+        out_shape=(jax.ShapeDtypeStruct((2, plan.bands, plan.lons, columns), f32),
+                   jax.ShapeDtypeStruct((len(ALL_STEPS), columns, columns), bf16)),
+        in_specs=[smem(), vmem(), vmem()],
+        out_specs=(vmem(), vmem()),
+        scratch_shapes=[pltpu.VMEM((4 * side - 1, wide), f32),
+                        pltpu.VMEM((LANES // side, 3 * side, wide), bf16)] + work,
+        name="first",
+    )(info, got, kernel)
+    part = part.reshape(2, n, columns)
+    swap = [(i, i ^ 1) for i in range(plan.lons)]
+    both = part + lax.ppermute(part, "tile", swap)
+    onward = plan.onward()
+    before = lax.ppermute(both[1], axes, onward)
+    after = lax.ppermute(both[0], axes, [(t, s) for s, t in onward])
+    back = pl.pallas_call(
+        functools.partial(second_kernel, plan),
+        out_shape=jax.ShapeDtypeStruct((n, 8, LANES), f32),
+        in_specs=[smem()] + [vmem()] * 5,
+        out_specs=vmem(),
+        scratch_shapes=work + [pltpu.VMEM((2, plan.bands, plan.lons, columns), f32)],
+        name="second",
+    )(info, got, maps, both, before, after)
+    home = lax.all_to_all(back, axes, 0, 0)
+    increment, residual = pl.pallas_call(
+        functools.partial(last_kernel, plan),
+        out_shape=(jax.ShapeDtypeStruct(f.shape, f32),) * 2,
+        in_specs=[vmem(), vmem()],
+        out_specs=(vmem(), vmem()),
+        scratch_shapes=[pltpu.VMEM(f.shape, f32)] * 2,
+        name="last",
+    )(f, home)
+    return increment[None, None], residual[None, None]
 
 
 def padded(block, sides, width):
@@ -124,16 +537,23 @@
 
 
 def solution(mesh):
+    specs = (
+        P("band", "tile", None, None, None),
+        P("band", "tile", None, None),
+        P("band", "tile", None),
+        P(),
+        P(),
+    )
+
+    def run(anomalies, forcing, pair_code, kernel, tile_taper):
+        plan = Plan(mesh.shape["band"], mesh.shape["tile"], *anomalies.shape[2:])
+        step = functools.partial(by_levels, plan) if plan.fits else on_device
+        return step(anomalies, forcing, pair_code, kernel, tile_taper)
+
     return jax.shard_map(
-        on_device,
+        run,
         mesh=mesh,
-        in_specs=(
-            P("band", "tile", None, None, None),
-            P("band", "tile", None, None),
-            P("band", "tile", None),
-            P(),
-            P(),
-        ),
+        in_specs=specs,
         out_specs=(P("band", "tile", None, None), P("band", "tile", None, None)),
         check_vma=False,
     )

time: 276 us -> 84.6 us (0.31)
  blocking collectives: 121 us -> 12.9 us
  matrix products: 44.3 us -> 0 us
  local copies, waits for them, and re-layouts: 35.5 us -> 6.81 us
  other arithmetic: 26 us -> 0.85 us
  Pallas kernels: 0 us -> 24.4 us
  waiting for transfers between devices: 14 us -> 25.2 us
  between operations: 9.82 us -> 0.7 us
  loops' own time: 6.65 us -> 0 us
    psum x3 -> x0, blocking collectives: 121 us -> none  [global_total(): return lax.psum(jnp.sum(factor_one * factor_two), ('band', 'tile'))]
    dot_general x24 -> x0, matrix products: 44.3 us -> none  [the longest x9 25.2 us: local_map(): jnp.einsum('abq,cdq->acbd', by_lat, selector(SIDE, col_step), precision=l...]
    pallas_call x0 -> x4, Pallas kernels: none -> 24.4 us  [the longest x1 10.3 us: by_levels(): pl.pallas_call(functools.partial(first_kernel, plan, side), out_shape=(ja...]
    all_to_all x0 -> x1, waiting for transfers between devices: none -> 22.2 us  [by_levels(): got = lax.all_to_all(sent, axes, 0, 0)]
    convert_element_type x9 -> x0, local copies, waits for them, and re-layouts: 21.8 us -> none  [local_map(): return full_map.reshape(SIDE * SIDE, SIDE * SIDE).astype(jnp.bfloat16)]
    convert_element_type x8 -> x0, other arithmetic: 15.6 us -> none  [weighted_block(): return (block.astype(jnp.float32) * field[:, None, :]).astype(jnp.bfloat16)]
    all_to_all x0 -> x1, blocking collectives: none -> 12.9 us  [by_levels(): home = lax.all_to_all(back, axes, 0, 0)]
    ppermute x12 -> x3, waiting for transfers between devices: 14 us -> 3.02 us  [the longest x1 1.56 us: by_levels(): before = lax.ppermute(both[1], axes, onward)]
  transfers between devices with their start and end apart: 12 -> 4, of which waited for: 4 -> 3; matrix products, arithmetic and copies ran while one was open for 32% -> 1% of each run, Pallas kernels for 0% -> 0%
where the time goes in v1:
time: 84.6 us; the launch traced here: 83.9 us
  waiting for transfers between devices  25.2 us (30%)
  Pallas kernels  24.4 us (29%)
  starting transfers between devices  13.2 us (16%)
  blocking collectives  12.9 us (15%)
  local copies, waits for them, and re-layouts  6.81 us (8%)
  other arithmetic  0.85 us (1%)
    all_to_all x1, waiting for transfers between devices, by_levels(): got = lax.all_to_all(sent, axes, 0, 0)  22.2 us
    all_to_all x1, blocking collectives, by_levels(): home = lax.all_to_all(back, axes, 0, 0)  12.9 us
    pallas_call x1, Pallas kernels, by_levels(): pl.pallas_call(functools.partial(first_kernel, plan, side), out_shape=(ja...  10.3 us
    pallas_call x1, Pallas kernels, by_levels(): pl.pallas_call(functools.partial(second_kernel, plan), out_shape=jax.Shap...  9.97 us
    all_to_all x1, starting transfers between devices, by_levels(): got = lax.all_to_all(sent, axes, 0, 0)  7.33 us
    unnamed x11, local copies, waits for them, and re-layouts  5.59 us
    ppermute x1, starting transfers between devices, by_levels(): before = lax.ppermute(both[1], axes, onward)  4.55 us
    pallas_call x1, Pallas kernels, by_levels(): pl.pallas_call(functools.partial(pack_kernel, plan, tile_taper.shape[0]),...  2.28 us
  transfers between devices with their start and end apart: 4, of which 3 were waited for; matrix products, arithmetic and copies ran while one was open for 1% of the time, Pallas kernels for 0%

profile of v1, /device:TPU:0, one launch (start us, length us, event | category | flops | bytes accessed | tf_op | source)
XLA Modules:
  0.0 83.9 jit_solution(12965127944216595829)
XLA Ops:
  0.6 1.3 %copy.12 = f32[1,1,18,256]{3,2,1,0:T(8,128)} copy(f32[1,1,18,256]{3,1,2,0:T(1,128)} %param.7) | data formatting | bytes 36864
  2.0 2.3 %pack.1 = bf16[32,112,128]{2,1,0:T(8,128)(2,1)} custom-call(s32[1,1,8]{2,1,0:T(1,128)} %code_ref.1, f32[4]{0:T(128)} %taper_ref.1, bf16[18,80,256]{2,1,0:T(8,128)(2,1)} %bitcast.14, f32[18,256]{1,0:T(8,128)} %bitcast.15), custom_call_target="tpu_custom_call" | custom-call | tf_op jit(solution)/shard_map/pack/pallas_call | solution.py:374
  4.2 7.3 %all-to-all-start = ((bf16[32,112,128]{2,1,0:T(8,128)(2,1)}), bf16[32,112,128]{2,1,0:T(8,128)(2,1)S(1)}, u32[]{:S(2)}, u32[]{:S(2)}) async-start(bf16[32,112,128]{2,1,0:T(8,128)(2,1)} %pack.1), calls=%async_computation | async-start | bytes 1835008 | tf_op jit(solution)/shard_map/all_to_all | solution.py:382
  11.6 1.2 %dynamic-slice_bitcast_fusion.info_ref = s32[8]{0:T(128)} fusion(s32[32,8]{1,0:T(8,128)} %constant.16.clone, s32[]{:T(128)S(6)} %select_n.3), kind=kLoop, calls=%fused_computation.3 | loop fusion | bytes 68 | tf_op jit(solution)/shard_map/squeeze | solution.py:384
  12.8 22.2 %all-to-all-done.got_ref = bf16[32,112,128]{2,1,0:T(8,128)(2,1)S(1)} async-done(((bf16[32,112,128]{2,1,0:T(8,128)(2,1)}), bf16[32,112,128]{2,1,0:T(8,128)(2,1)S(1)}, u32[]{:S(2)}, u32[]{:S(2)}) %all-to-all-start) | async-done | bytes 917536 | tf_op jit(solution)/shard_map/all_to_all | solution.py:382
  35.0 0.0 copy-start
  35.0 0.9 %copy-done = bf16[32,112,128]{2,1,0:T(8,128)(2,1)} copy-done((bf16[32,112,128]{2,1,0:T(8,128)(2,1)}, bf16[32,112,128]{2,1,0:T(8,128)(2,1)S(1)}, u32[]{:S(2)}) %copy-start) | copy-done | bytes 917528
  35.9 10.3 %first.1 = (f32[2,4,8,256]{3,2,1,0:T(8,128)}, bf16[9,256,256]{2,1,0:T(8,128)(2,1)}) custom-call(s32[8]{0:T(128)} %dynamic-slice_bitcast_fusion.info_ref, bf16[32,112,128]{2,1,0:T(8,128)(2,1)} %copy-done, f32[63,63]{1,0:T(8,128)} %kernel_ref.1), custom_call_target="tpu_custom_call" | custom-call | tf_op jit(solution)/shard_map/first/pallas_call | solution.py:391
  46.2 0.0 collective-permute-start
  46.2 1.5 %collective-permute-done = f32[2,32,256]{2,1,0:T(8,128)S(1)} collective-permute-done((f32[2,32,256]{2,1,0:T(8,128)}, f32[2,32,256]{2,1,0:T(8,128)S(1)}, u32[]{:S(2)}, u32[]{:S(2)}) %collective-permute-start) | collective-permute-done | bytes 65568 | tf_op jit(solution)/shard_map/ppermute | solution.py:403
  47.7 0.9 %bitcast_add_fusion.sum_ref = f32[2,32,256]{2,1,0:T(8,128)S(1)} fusion(f32[2,32,256]{2,1,0:T(8,128)S(1)} %collective-permute-done, f32[2,4,8,256]{3,2,1,0:T(8,128)} %get-tuple-element.7), kind=kLoop, calls=%fused_computation.4 | loop fusion | flops 16384 | bytes 196608 | tf_op jit(solution)/shard_map/add | solution.py:403
  48.5 0.0 copy-start.1
  48.5 1.3 %collective-permute-start.2 = (f32[32,256]{1,0:T(8,128)S(1)}, f32[32,256]{1,0:T(8,128)S(1)}, u32[]{:S(2)}, u32[]{:S(2)}) collective-permute-start(f32[32,256]{1,0:T(8,128)S(1)} %get-tuple-element.12), channel_id=1, source_target_pairs={{2,0},{3,1},{6,2},{7,3},{4,6},{5,7},{12,4},{13,5},{10,14},{11,15},... | collective-permute-start | bytes 98312 | tf_op jit(solution)/shard_map/ppermute | solution.py:406
  49.8 4.5 %collective-permute-start.1 = (f32[32,256]{1,0:T(8,128)S(1)}, f32[32,256]{1,0:T(8,128)S(1)}, u32[]{:S(2)}, u32[]{:S(2)}) collective-permute-start(f32[32,256]{1,0:T(8,128)S(1)} %get-tuple-element.13), channel_id=1, source_target_pairs={{0,2},{1,3},{2,6},{3,7},{6,4},{7,5},{4,12},{5,13},{14,10},{15,11},... | collective-permute-start | bytes 98312 | tf_op jit(solution)/shard_map/ppermute | solution.py:405
  54.4 0.0 collective-permute-done.2.after_ref
  54.4 0.0 copy-start.2
  54.4 1.6 %collective-permute-done.1.before_ref = f32[32,256]{1,0:T(8,128)S(1)} collective-permute-done((f32[32,256]{1,0:T(8,128)S(1)}, f32[32,256]{1,0:T(8,128)S(1)}, u32[]{:S(2)}, u32[]{:S(2)}) %collective-permute-start.1) | collective-permute-done | bytes 32800 | tf_op jit(solution)/shard_map/ppermute | solution.py:405
  56.0 0.0 copy-start.3
  56.0 0.0 copy-done.1
  56.0 0.0 copy-done.2
  56.0 0.6 copy-done.3
  56.6 10.0 %second.1 = f32[32,8,128]{2,1,0:T(8,128)} custom-call(s32[8]{0:T(128)} %dynamic-slice_bitcast_fusion.info_ref, bf16[32,112,128]{2,1,0:T(8,128)(2,1)} %copy-done, bf16[9,256,256]{2,1,0:T(8,128)(2,1)} %get-tuple-element.6.lt_ref, f32[2,32,256]{2,1,0:T(8,128)} %copy-done.1, f32[32,256]{1,0:T(8,128)} %copy-done.3, f32[32,256]{1,0:T(8,128)} %copy-done.2), custom_call_target="tpu_custom_call" | custom-call | tf_op jit(solution)/shard_map/second/pallas_call | solution.py:407
  66.5 12.9 %all_to_all.10.got_ref = f32[32,8,128]{2,1,0:T(8,128)} all-to-all(f32[32,8,128]{2,1,0:T(8,128)} %second.1), channel_id=1, replica_groups=mesh['band'=4,'tile'=8] {'band','tile'}, dimensions={0} | all-to-all | bytes 262144 | tf_op jit(solution)/shard_map/all_to_all | solution.py:415
  79.4 1.8 %last.1 = (f32[18,256]{1,0:T(8,128)}, f32[18,256]{1,0:T(8,128)}) custom-call(f32[18,256]{1,0:T(8,128)} %bitcast.16, f32[32,8,128]{2,1,0:T(8,128)} %all_to_all.10.got_ref), custom_call_target="tpu_custom_call" | custom-call | tf_op jit(solution)/shard_map/last/pallas_call | solution.py:416
  81.2 1.4 %copy.8 = f32[1,1,18,256]{3,1,2,0:T(1,128)} copy(f32[1,1,18,256]{3,2,1,0:T(8,128)} %bitcast.19) | data formatting | bytes 36864
  82.6 1.4 %copy.9 = f32[1,1,18,256]{3,1,2,0:T(1,128)} copy(f32[1,1,18,256]{3,2,1,0:T(8,128)} %bitcast.18) | data formatting | bytes 36864
  (1 shorter events, 0.0 us)
Async XLA Ops:
  4.2 30.7 %all-to-all-start = ((bf16[32,112,128]{2,1,0:T(8,128)(2,1)}), bf16[32,112,128]{2,1,0:T(8,128)(2,1)S(1)}, u32[]{:S(2)}, u32[]{:S(2)}) async-start(bf16[32,112,128]{2,1,0:T(8,128)(2,1)} %pack.1), calls=%async_computation | async-start | bytes 1835008 | tf_op jit(solution)/shard_map/all_to_all | solution.py:382
  35.0 0.9 %copy-start = (bf16[32,112,128]{2,1,0:T(8,128)(2,1)}, bf16[32,112,128]{2,1,0:T(8,128)(2,1)S(1)}, u32[]{:S(2)}) copy-start(bf16[32,112,128]{2,1,0:T(8,128)(2,1)S(1)} %all-to-all-done.got_ref) | copy-start | bytes 2752516
  46.2 1.5 %collective-permute-start = (f32[2,32,256]{2,1,0:T(8,128)}, f32[2,32,256]{2,1,0:T(8,128)S(1)}, u32[]{:S(2)}, u32[]{:S(2)}) collective-permute-start(f32[2,32,256]{2,1,0:T(8,128)} %bitcast.17), channel_id=1, source_target_pairs={{0,1},{1,0},{2,3},{3,2},{4,5},{5,4},{6,7},{7,6},{8,9},{9,8},{10,11... | collective-permute-start | bytes 196616 | tf_op jit(solution)/shard_map/ppermute | solution.py:403
  48.5 7.5 %copy-start.1 = (f32[2,32,256]{2,1,0:T(8,128)}, f32[2,32,256]{2,1,0:T(8,128)S(1)}, u32[]{:S(2)}) copy-start(f32[2,32,256]{2,1,0:T(8,128)S(1)} %bitcast_add_fusion.sum_ref) | copy-start | bytes 196612
  48.5 5.9 %collective-permute-start.2 = (f32[32,256]{1,0:T(8,128)S(1)}, f32[32,256]{1,0:T(8,128)S(1)}, u32[]{:S(2)}, u32[]{:S(2)}) collective-permute-start(f32[32,256]{1,0:T(8,128)S(1)} %get-tuple-element.12), channel_id=1, source_target_pairs={{2,0},{3,1},{6,2},{7,3},{4,6},{5,7},{12,4},{13,5},{10,14},{11,15},... | collective-permute-start | bytes 98312 | tf_op jit(solution)/shard_map/ppermute | solution.py:406
  49.8 6.1 %collective-permute-start.1 = (f32[32,256]{1,0:T(8,128)S(1)}, f32[32,256]{1,0:T(8,128)S(1)}, u32[]{:S(2)}, u32[]{:S(2)}) collective-permute-start(f32[32,256]{1,0:T(8,128)S(1)} %get-tuple-element.13), channel_id=1, source_target_pairs={{0,2},{1,3},{2,6},{3,7},{6,4},{7,5},{4,12},{5,13},{14,10},{15,11},... | collective-permute-start | bytes 98312 | tf_op jit(solution)/shard_map/ppermute | solution.py:405
  54.4 1.6 %copy-start.2 = (f32[32,256]{1,0:T(8,128)}, f32[32,256]{1,0:T(8,128)S(1)}, u32[]{:S(2)}) copy-start(f32[32,256]{1,0:T(8,128)S(1)} %collective-permute-done.2.after_ref) | copy-start | bytes 98308
  56.0 0.6 copy-start.3

commit v2 on v1

--- a/solution.py
+++ b/solution.py
@@ -86,7 +86,7 @@
 
 
 def pack_kernel(plan, tapers, code_ref, taper_ref, a_ref, f_ref, out_ref, ext_ref):
-    parts = in_three(f_ref[...])
+    parts = in_three(f_ref[:, 0, :])
     lane = lax.broadcasted_iota(jnp.int32, (1, LANES), 1)
     weights = jnp.zeros((1, LANES), jnp.float32)
     for k in range(len(DIRECTIONS)):
@@ -174,78 +174,58 @@
 
 
 def apply_rows(plan, low, got_ref, v_ref, lt_ref, wide_ref, w_ref, s_ref, p_ref):
-    bands, lons, rows, columns = plan.bands, plan.lons, plan.rows, plan.columns
+    bands, lons, rows = plan.bands, plan.lons, plan.rows
     grains = rows // GRAIN
-    stride = lons + 2
-
-    def weigh(band, carry):
-        for l in range(lons):
-            tile = band * lons + l
-            v_low = v_ref[0, pl.ds(tile, 1), :]
-            v_high = v_ref[1, pl.ds(tile, 1), :]
-            halves = []
-            for half in range(2):
-                lanes = slice(half * LANES, (half + 1) * LANES)
-                block = got_ref[tile, half * rows : (half + 1) * rows, :].astype(jnp.float32)
-                pieces = []
-                for g in range(grains):
-                    v = jnp.where(g < low, v_low[:, lanes], v_high[:, lanes])
-                    pieces.append(block[g * GRAIN : (g + 1) * GRAIN] * v)
-                halves.append(jnp.concatenate(pieces, axis=0))
-            weighted = jnp.concatenate(halves, axis=1).astype(jnp.bfloat16)
-            places = [l + 1] + ([0] if l == lons - 1 else []) + ([lons + 1] if l == 0 else [])
-            for place in places:
-                at = pl.multiple_of((band * stride + place) * rows, 16)
-                w_ref[pl.ds(at, rows), :] = weighted
-        return carry
-
-    lax.fori_loop(0, bands, weigh, 0)
+    sides = [slice(half * LANES, (half + 1) * LANES) for half in range(2)]
+
+    def block(tile, half):
+        return got_ref[tile, half * rows : (half + 1) * rows, :].astype(jnp.float32)
+
+    for tile in range(plan.count):
+        v_low, v_high = v_ref[0, tile : tile + 1, :], v_ref[1, tile : tile + 1, :]
+        for half, lanes in enumerate(sides):
+            values = block(tile, half)
+            pieces = []
+            for g in range(grains):
+                v = jnp.where(g < low, v_low[:, lanes], v_high[:, lanes])
+                pieces.append(values[g * GRAIN : (g + 1) * GRAIN] * v)
+            w_ref[tile * rows : (tile + 1) * rows, lanes] = jnp.concatenate(pieces, axis=0).astype(jnp.bfloat16)
 
     for k, (p, q) in enumerate(ALL_STEPS):
-
-        def spread(band, carry, k=k, p=p, q=q):
-            at = pl.multiple_of(((band + p) * stride + 1 + q) * rows, 16)
-            y = jnp.dot(w_ref[pl.ds(at, lons * rows), :], lt_ref[k], preferred_element_type=jnp.float32)
+        first, last = max(0, p), min(bands, bands + p)
+        y = jnp.dot(
+            w_ref[first * lons * rows : last * lons * rows, :], lt_ref[k], preferred_element_type=jnp.float32
+        )
+        for band in range(first, last):
             for l in range(lons):
-                tile = band * lons + l
-                piece = y[l * rows : (l + 1) * rows]
+                tile = (band - p) * lons + (l - q) % lons
+                at = ((band - first) * lons + l) * rows
+                piece = y[at : at + rows]
                 if k == 0:
                     s_ref[tile] = piece * jnp.float32(1.0 / (plan.members - 1))
                 else:
-                    s_ref[tile] += piece * wide_ref[k - 1, pl.ds(tile, 1), :]
-            return carry
-
-        lax.fori_loop(max(0, -p), min(bands, bands - p), spread, 0)
-
-    def gather(band, carry):
-        sums = [[[], []], [[], []]]
-        for l in range(lons):
-            tile = band * lons + l
-            for half in range(2):
-                lanes = slice(half * LANES, (half + 1) * LANES)
-                block = got_ref[tile, half * rows : (half + 1) * rows, :].astype(jnp.float32)
-                product = block * s_ref[tile, :, lanes]
+                    s_ref[tile] += piece * wide_ref[k - 1, tile : tile + 1, :]
+
+    shares = [jnp.where(g < low, jnp.float32(1), jnp.float32(0)) for g in range(grains)]
+    for band in range(bands):
+        for half, lanes in enumerate(sides):
+            sums = [[], []]
+            for l in range(lons):
+                tile = band * lons + l
+                product = block(tile, half) * s_ref[tile, :, lanes]
                 lo = jnp.zeros((GRAIN, LANES), jnp.float32)
                 hi = jnp.zeros((GRAIN, LANES), jnp.float32)
                 for g in range(grains):
                     piece = product[g * GRAIN : (g + 1) * GRAIN]
-                    share = jnp.where(g < low, jnp.float32(1), jnp.float32(0))
-                    lo = lo + piece * share
-                    hi = hi + piece * (1 - share)
-                sums[0][half].append(jnp.sum(lo, axis=0, keepdims=True))
-                sums[1][half].append(jnp.sum(hi, axis=0, keepdims=True))
-        for level in range(2):
-            p_ref[level, band] = jnp.concatenate(
-                [jnp.concatenate(sums[level][half], axis=0) for half in range(2)], axis=1
-            )
-        return carry
-
-    lax.fori_loop(0, bands, gather, 0)
-
-
-def first_kernel(plan, side, info_ref, got_ref, kernel_ref, p_ref, lt_ref,
-                 by_lat_ref, turned_ref, v_ref, wide_ref, w_ref, s_ref):
-    build_maps(side, kernel_ref, lt_ref, by_lat_ref, turned_ref)
+                    lo = lo + piece * shares[g]
+                    hi = hi + piece * (1 - shares[g])
+                sums[0].append(jnp.sum(lo, axis=0, keepdims=True))
+                sums[1].append(jnp.sum(hi, axis=0, keepdims=True))
+            for level in range(2):
+                p_ref[level, band, :, lanes] = jnp.concatenate(sums[level], axis=0)
+
+
+def first_kernel(plan, info_ref, got_ref, lt_ref, p_ref, v_ref, wide_ref, w_ref, s_ref):
     extra = read_weights(plan, got_ref, wide_ref)
     v_ref[0] = forcing_of(extra, 0)
     v_ref[1] = forcing_of(extra, 1)
@@ -348,12 +328,16 @@
     diagonal = rows == lax.broadcasted_iota(jnp.int32, (plan.levels, LANES), 1)
     ratio_c = add(jnp.where(diagonal, ratio, 0.0))
     shift_c = add(jnp.where(diagonal, shift, 0.0))
-    b, u, t = f_ref[...], u_ref[...], t_ref[...]
+    b, u, t = f_ref[:, 0, :], u_ref[...], t_ref[...]
     q = shift_c * b + (ratio_c * b - u)
     b_of_q = shift_c * u + t
     direction = step_0 * q + turn * b
-    inc_ref[...] = step_0 * b + step_1 * direction
-    res_ref[...] = step_0 * q - step_1 * (step_0 * (q + b_of_q) + turn * (b + u))
+    inc_ref[:, 0, :] = step_0 * b + step_1 * direction
+    res_ref[:, 0, :] = step_0 * q - step_1 * (step_0 * (q + b_of_q) + turn * (b + u))
+
+
+def room(mib):
+    return pltpu.CompilerParams(vmem_limit_bytes=mib << 20)
 
 
 def vmem():
@@ -370,7 +354,7 @@
     n, rows, columns = plan.count, plan.rows, plan.columns
     side = (kernel.shape[0] + 1) // 4
     wide = 4 * side * side
-    a, f = anomalies[0, 0], forcing[0, 0]
+    a, f = anomalies[0, 0], jnp.swapaxes(forcing[0], 0, 1)
     sent = pl.pallas_call(
         functools.partial(pack_kernel, plan, tile_taper.shape[0]),
         out_shape=jax.ShapeDtypeStruct((n, plan.height, LANES), bf16),
@@ -385,19 +369,29 @@
     work = [
         pltpu.VMEM((2, n, columns), f32),
         pltpu.VMEM((len(DIRECTIONS), n, columns), f32),
-        pltpu.VMEM((plan.bands * (plan.lons + 2) * rows, columns), bf16),
+        pltpu.VMEM((n * rows, columns), bf16),
         pltpu.VMEM((n, rows, columns), f32),
     ]
-    part, maps = pl.pallas_call(
-        functools.partial(first_kernel, plan, side),
-        out_shape=(jax.ShapeDtypeStruct((2, plan.bands, plan.lons, columns), f32),
-                   jax.ShapeDtypeStruct((len(ALL_STEPS), columns, columns), bf16)),
+    maps = pl.pallas_call(
+        functools.partial(build_maps, side),
+        out_shape=jax.ShapeDtypeStruct((len(ALL_STEPS), columns, columns), bf16),
+        in_specs=[vmem()],
+        out_specs=vmem(),
+        scratch_shapes=[pltpu.VMEM((4 * side - 1, wide), f32),
+                        pltpu.VMEM((LANES // side, 3 * side, wide), bf16)],
+        cost_estimate=pl.CostEstimate(flops=200_000_000, bytes_accessed=2_000_000, transcendentals=0),
+        compiler_params=room(12),
+        name="maps",
+    )(kernel)
+    part = pl.pallas_call(
+        functools.partial(first_kernel, plan),
+        out_shape=jax.ShapeDtypeStruct((2, plan.bands, plan.lons, columns), f32),
         in_specs=[smem(), vmem(), vmem()],
-        out_specs=(vmem(), vmem()),
-        scratch_shapes=[pltpu.VMEM((4 * side - 1, wide), f32),
-                        pltpu.VMEM((LANES // side, 3 * side, wide), bf16)] + work,
+        out_specs=vmem(),
+        scratch_shapes=work,
+        compiler_params=room(20),
         name="first",
-    )(info, got, kernel)
+    )(info, got, maps)
     part = part.reshape(2, n, columns)
     swap = [(i, i ^ 1) for i in range(plan.lons)]
     both = part + lax.ppermute(part, "tile", swap)
@@ -410,6 +404,7 @@
         in_specs=[smem()] + [vmem()] * 5,
         out_specs=vmem(),
         scratch_shapes=work + [pltpu.VMEM((2, plan.bands, plan.lons, columns), f32)],
+        compiler_params=room(20),
         name="second",
     )(info, got, maps, both, before, after)
     home = lax.all_to_all(back, axes, 0, 0)
@@ -418,10 +413,11 @@
         out_shape=(jax.ShapeDtypeStruct(f.shape, f32),) * 2,
         in_specs=[vmem(), vmem()],
         out_specs=(vmem(), vmem()),
-        scratch_shapes=[pltpu.VMEM(f.shape, f32)] * 2,
+        scratch_shapes=[pltpu.VMEM((plan.levels, columns), f32)] * 2,
+        compiler_params=room(8),
         name="last",
     )(f, home)
-    return increment[None, None], residual[None, None]
+    return jnp.swapaxes(increment, 0, 1)[None], jnp.swapaxes(residual, 0, 1)[None]
 
 
 def padded(block, sides, width):

time: 84.6 us -> 62.1 us (0.73)
  Pallas kernels: 24.4 us -> 9.89 us
  local copies, waits for them, and re-layouts: 6.81 us -> 0.72 us
    pallas_call x1, Pallas kernels: 9.97 us -> 3.05 us  [by_levels(): pl.pallas_call(functools.partial(second_kernel, plan), out_shape=jax.Shap...]
    pallas_call x1 -> x2, Pallas kernels: 10.3 us -> 3.6 us  [the longest x1 2.75 us: by_levels(): pl.pallas_call(functools.partial(first_kernel, plan), out_shape=jax.Shape...]
    unnamed x11 -> x4, local copies, waits for them, and re-layouts: 5.59 us -> 0.01 us
    pallas_call x1, Pallas kernels: 1.83 us -> 0.91 us  [by_levels(): pl.pallas_call(functools.partial(last_kernel, plan), out_shape=(jax.Shape...]
  transfers between devices with their start and end apart: 4 -> 4, of which waited for: 3 -> 3; matrix products, arithmetic and copies ran while one was open for 1% -> 1% of each run, Pallas kernels for 0% -> 1%
where the time goes in v2:
time: 62.1 us; the launch traced here: 61.7 us
  waiting for transfers between devices  24.6 us (40%)
  starting transfers between devices  13.2 us (21%)
  blocking collectives  12.5 us (20%)
  Pallas kernels  9.89 us (16%)
  between operations  0.73 us (1%)
  local copies, waits for them, and re-layouts  0.72 us (1%)
    all_to_all x1, waiting for transfers between devices, by_levels(): got = lax.all_to_all(sent, axes, 0, 0)  21.8 us
    all_to_all x1, blocking collectives, by_levels(): home = lax.all_to_all(back, axes, 0, 0)  12.5 us
    all_to_all x1, starting transfers between devices, by_levels(): got = lax.all_to_all(sent, axes, 0, 0)  7.33 us
    ppermute x1, starting transfers between devices, by_levels(): before = lax.ppermute(both[1], axes, onward)  4.55 us
    pallas_call x1, Pallas kernels, by_levels(): pl.pallas_call(functools.partial(second_kernel, plan), out_shape=jax.Shap...  3.05 us
    pallas_call x1, Pallas kernels, by_levels(): pl.pallas_call(functools.partial(first_kernel, plan), out_shape=jax.Shape...  2.75 us
    pallas_call x1, Pallas kernels, by_levels(): pl.pallas_call(functools.partial(pack_kernel, plan, tile_taper.shape[0]),...  2.33 us
    ppermute x1, waiting for transfers between devices, by_levels(): before = lax.ppermute(both[1], axes, onward)  1.57 us
  transfers between devices with their start and end apart: 4, of which 3 were waited for; matrix products, arithmetic and copies ran while one was open for 1% of the time, Pallas kernels for 1%

profile of v2, /device:TPU:0, one launch (start us, length us, event | category | flops | bytes accessed | tf_op | source)
XLA Modules:
  0.0 61.7 jit_solution(4475873882394480335)
XLA Ops:
  0.6 2.3 %pack.1 = bf16[32,112,128]{2,1,0:T(8,128)(2,1)} custom-call(s32[1,1,8]{2,1,0:T(1,128)} %code_ref.1, f32[4]{0:T(128)} %taper_ref.1, bf16[18,80,256]{2,1,0:T(8,128)(2,1)} %bitcast.19, f32[18,1,256]{2,1,0:T(1,128)} %bitcast.17), custom_call_target="tpu_custom_call" | custom-call | tf_op jit(solution)/shard_map/pack/pallas_call | solution.py:358
  3.0 0.0 copy-start.1
  3.0 7.3 %all-to-all-start = ((bf16[32,112,128]{2,1,0:T(8,128)(2,1)}), bf16[32,112,128]{2,1,0:T(8,128)(2,1)S(1)}, u32[]{:S(2)}, u32[]{:S(2)}) async-start(bf16[32,112,128]{2,1,0:T(8,128)(2,1)} %pack.1), calls=%async_computation | async-start | bytes 1835008 | tf_op jit(solution)/shard_map/all_to_all | solution.py:366
  10.3 0.0 copy-done.1
  10.3 0.9 %maps.1.lt_ref = bf16[9,256,256]{2,1,0:T(8,128)(2,1)S(1)} custom-call(f32[63,63]{1,0:T(8,128)S(1)} %copy-done.1), custom_call_target="tpu_custom_call" | custom-call | flops 200000000 | bytes 2000000 | tf_op jit(solution)/shard_map/maps/pallas_call | solution.py:375
  11.2 0.7 %dynamic-slice_bitcast_fusion.info_ref = s32[8]{0:T(128)S(1)} fusion(s32[32,8]{1,0:T(8,128)} %constant.16.clone, s32[]{:T(128)S(6)} %select_n.3), kind=kLoop, calls=%fused_computation.2 | loop fusion | bytes 68 | tf_op jit(solution)/shard_map/squeeze | solution.py:368
  11.9 21.8 %all-to-all-done.got_ref = bf16[32,112,128]{2,1,0:T(8,128)(2,1)S(1)} async-done(((bf16[32,112,128]{2,1,0:T(8,128)(2,1)}), bf16[32,112,128]{2,1,0:T(8,128)(2,1)S(1)}, u32[]{:S(2)}, u32[]{:S(2)}) %all-to-all-start) | async-done | bytes 917536 | tf_op jit(solution)/shard_map/all_to_all | solution.py:366
  33.7 2.8 %first.1 = f32[2,4,8,256]{3,2,1,0:T(8,128)S(1)} custom-call(s32[8]{0:T(128)S(1)} %dynamic-slice_bitcast_fusion.info_ref, bf16[32,112,128]{2,1,0:T(8,128)(2,1)S(1)} %all-to-all-done.got_ref, bf16[9,256,256]{2,1,0:T(8,128)(2,1)S(1)} %maps.1.lt_ref), custom_call_target="tpu_custom_call" | custom-call | tf_op jit(solution)/shard_map/first/pallas_call | solution.py:386
  36.4 0.1 collective-permute-start
  36.5 1.2 %collective-permute-done = f32[2,32,256]{2,1,0:T(8,128)S(1)} collective-permute-done((f32[2,32,256]{2,1,0:T(8,128)S(1)}, f32[2,32,256]{2,1,0:T(8,128)S(1)}, u32[]{:S(2)}, u32[]{:S(2)}) %collective-permute-start) | collective-permute-done | bytes 65568 | tf_op jit(solution)/shard_map/ppermute | solution.py:397
  37.8 1.3 %collective-permute-start.2 = (f32[32,256]{1,0:T(8,128)S(1)}, f32[32,256]{1,0:T(8,128)S(1)}, u32[]{:S(2)}, u32[]{:S(2)}) collective-permute-start(f32[32,256]{1,0:T(8,128)S(1)} %get-tuple-element.8), channel_id=1, source_target_pairs={{2,0},{3,1},{6,2},{7,3},{4,6},{5,7},{12,4},{13,5},{10,14},{11,15},... | collective-permute-start | bytes 98312 | tf_op jit(solution)/shard_map/ppermute | solution.py:400
  39.1 0.0 copy-start
  39.1 4.5 %collective-permute-start.1 = (f32[32,256]{1,0:T(8,128)S(1)}, f32[32,256]{1,0:T(8,128)S(1)}, u32[]{:S(2)}, u32[]{:S(2)}) collective-permute-start(f32[32,256]{1,0:T(8,128)S(1)} %get-tuple-element.9), channel_id=1, source_target_pairs={{0,2},{1,3},{2,6},{3,7},{6,4},{7,5},{4,12},{5,13},{14,10},{15,11},... | collective-permute-start | bytes 98312 | tf_op jit(solution)/shard_map/ppermute | solution.py:399
  43.7 0.0 collective-permute-done.2.after_ref
  43.7 1.6 %collective-permute-done.1.before_ref = f32[32,256]{1,0:T(8,128)S(1)} collective-permute-done((f32[32,256]{1,0:T(8,128)S(1)}, f32[32,256]{1,0:T(8,128)S(1)}, u32[]{:S(2)}, u32[]{:S(2)}) %collective-permute-start.1) | collective-permute-done | bytes 32800 | tf_op jit(solution)/shard_map/ppermute | solution.py:399
  45.2 3.0 %second.1 = f32[32,8,128]{2,1,0:T(8,128)S(1)} custom-call(s32[8]{0:T(128)S(1)} %dynamic-slice_bitcast_fusion.info_ref, bf16[32,112,128]{2,1,0:T(8,128)(2,1)S(1)} %all-to-all-done.got_ref, bf16[9,256,256]{2,1,0:T(8,128)(2,1)S(1)} %maps.1.lt_ref, f32[2,32,256]{2,1,0:T(8,128)S(1)} %bitcast_add_fusion.sum_ref, f32[32,256]{1,0:T(8,128)S(1)} %collective-permute-done.1.before_ref, ...), custom_call_target="tpu_custom_call" | custom-call | tf_op jit(solution)/shard_map/second/pallas_call | solution.py:401
  48.3 12.5 %all_to_all.10.got_ref = f32[32,8,128]{2,1,0:T(8,128)S(1)} all-to-all(f32[32,8,128]{2,1,0:T(8,128)S(1)} %second.1), channel_id=1, replica_groups=mesh['band'=4,'tile'=8] {'band','tile'}, dimensions={0} | all-to-all | bytes 262144 | tf_op jit(solution)/shard_map/all_to_all | solution.py:410
  60.8 0.0 copy-done
  60.8 0.9 %last.1 = (f32[18,1,256]{2,1,0:T(1,128)}, f32[18,1,256]{2,1,0:T(1,128)}) custom-call(f32[18,1,256]{2,1,0:T(1,128)S(1)} %bitcast.18, f32[32,8,128]{2,1,0:T(8,128)S(1)} %all_to_all.10.got_ref), custom_call_target="tpu_custom_call" | custom-call | tf_op jit(solution)/shard_map/last/pallas_call | solution.py:411
  (2 shorter events, 0.0 us)
Async XLA Ops:
  3.0 7.3 %copy-start.1 = (f32[63,63]{1,0:T(8,128)S(1)}, f32[63,63]{1,0:T(8,128)}, u32[]{:S(2)}) copy-start(f32[63,63]{1,0:T(8,128)} %kernel_ref.1) | copy-start | bytes 47632
  3.0 30.7 %all-to-all-start = ((bf16[32,112,128]{2,1,0:T(8,128)(2,1)}), bf16[32,112,128]{2,1,0:T(8,128)(2,1)S(1)}, u32[]{:S(2)}, u32[]{:S(2)}) async-start(bf16[32,112,128]{2,1,0:T(8,128)(2,1)} %pack.1), calls=%async_computation | async-start | bytes 1835008 | tf_op jit(solution)/shard_map/all_to_all | solution.py:366
  36.4 1.3 %collective-permute-start = (f32[2,32,256]{2,1,0:T(8,128)S(1)}, f32[2,32,256]{2,1,0:T(8,128)S(1)}, u32[]{:S(2)}, u32[]{:S(2)}) collective-permute-start(f32[2,32,256]{2,1,0:T(8,128)S(1)} %bitcast.16), channel_id=1, source_target_pairs={{0,1},{1,0},{2,3},{3,2},{4,5},{5,4},{6,7},{7,6},{8,9},{9,8},{10,11... | collective-permute-start | bytes 196616 | tf_op jit(solution)/shard_map/ppermute | solution.py:397
  37.8 5.9 %collective-permute-start.2 = (f32[32,256]{1,0:T(8,128)S(1)}, f32[32,256]{1,0:T(8,128)S(1)}, u32[]{:S(2)}, u32[]{:S(2)}) collective-permute-start(f32[32,256]{1,0:T(8,128)S(1)} %get-tuple-element.8), channel_id=1, source_target_pairs={{2,0},{3,1},{6,2},{7,3},{4,6},{5,7},{12,4},{13,5},{10,14},{11,15},... | collective-permute-start | bytes 98312 | tf_op jit(solution)/shard_map/ppermute | solution.py:400
  39.1 21.7 %copy-start = (f32[1,1,18,256]{3,1,2,0:T(1,128)S(1)}, f32[1,1,18,256]{3,1,2,0:T(1,128)}, u32[]{:S(2)}) copy-start(f32[1,1,18,256]{3,1,2,0:T(1,128)} %param.7) | copy-start | bytes 55300
  39.1 6.1 %collective-permute-start.1 = (f32[32,256]{1,0:T(8,128)S(1)}, f32[32,256]{1,0:T(8,128)S(1)}, u32[]{:S(2)}, u32[]{:S(2)}) collective-permute-start(f32[32,256]{1,0:T(8,128)S(1)} %get-tuple-element.9), channel_id=1, source_target_pairs={{0,2},{1,3},{2,6},{3,7},{6,4},{7,5},{4,12},{5,13},{14,10},{15,11},... | collective-permute-start | bytes 98312 | tf_op jit(solution)/shard_map/ppermute | solution.py:399

commit v3 on v2

--- a/solution.py
+++ b/solution.py
@@ -23,24 +23,24 @@
         self.bands, self.lons = bands, lons
         self.levels, self.members, self.columns = levels, members, columns
         self.count = bands * lons
-        self.depth = members // (2 * GRAIN)
-        self.rows = GRAIN * (self.depth + 1)
+        self.rows = levels * members // self.count
+        self.step = 2 * self.rows - members
         self.fits = (
-            members % (2 * GRAIN) == 0
-            and levels % (self.depth + 1) == 0
+            levels * members % self.count == 0
+            and members % 2 == 0
+            and 0 < self.step < members
+            and members % self.step == 0
             and levels <= SLOT
             and lons % GRAIN == 0
             and columns == 2 * LANES
-            and self.rows % 16 == 0
         )
         if not self.fits:
             return
-        self.groups = levels // (self.depth + 1)
-        chips = self.count // 2
-        used = self.groups * self.depth
-        self.fits = used <= chips < 2 * used
+        self.depth = members // self.step
+        self.fits = levels % (self.depth + 1) == 0
         if not self.fits:
             return
+        self.groups = levels // (self.depth + 1)
         across = lons // 2
         inner = [i ^ (i >> 1) for i in range(across)]
         if sorted(inner) != list(range(across)):
@@ -49,8 +49,11 @@
         for band in range(bands):
             path += [band * across + c for c in (inner if band % 2 == 0 else inner[::-1])]
         self.path = path
-        self.extra = 2 * self.rows
-        self.height = self.extra + 16
+        self.block = -(-(self.rows + 3) // 16) * 16
+        self.height = 2 * self.block + GRAIN
+
+    def low_rows(self, k):
+        return (self.members - k * self.step) // 2
 
     def device(self, group, k, core):
         return 2 * self.path[group * self.depth + k] + core
@@ -66,7 +69,7 @@
         out = np.zeros((self.count, 8), np.int32)
         for device, k, core, low in self.owners():
             last = k == self.depth - 1
-            out[device, :5] = (self.depth - k, core, int(core == 0), int(core == 1 and last), low)
+            out[device, :5] = (self.low_rows(k), core, int(core == 0), int(core == 1 and last), low)
         return out
 
     def onward(self):
@@ -82,11 +85,13 @@
     high = x.astype(jnp.bfloat16).astype(jnp.float32)
     rest = x - high
     middle = rest.astype(jnp.bfloat16).astype(jnp.float32)
-    return high, middle, rest - middle
-
-
-def pack_kernel(plan, tapers, code_ref, taper_ref, a_ref, f_ref, out_ref, ext_ref):
-    parts = in_three(f_ref[:, 0, :])
+    return [high, middle, rest - middle]
+
+
+def pack_kernel(plan, tapers, code_ref, taper_ref, a_ref, f_ref, out_ref, wide_ref):
+    for level in range(plan.levels):
+        wide_ref[level * plan.members : (level + 1) * plan.members, :] = a_ref[level].astype(jnp.float32)
+    forcing = in_three(f_ref[:, 0, :])
     lane = lax.broadcasted_iota(jnp.int32, (1, LANES), 1)
     weights = jnp.zeros((1, LANES), jnp.float32)
     for k in range(len(DIRECTIONS)):
@@ -95,34 +100,25 @@
         for c in range(tapers):
             weight = jnp.where(code == c + 1, taper_ref[c], weight)
         weights = jnp.where(lane == k, weight, weights)
-    weights = in_three(weights / jnp.float32(plan.members - 1))
-    blank = jnp.zeros((1, LANES), jnp.float32)
-    rows, depth = plan.rows, plan.depth
-    taken = set()
+    weights = weights / jnp.float32(plan.members - 1)
+    high, middle, _ = in_three(weights)
     for device, k, core, low in plan.owners():
-        taken.add(device)
-        count = GRAIN * (depth - k)
-        start = 2 * k * GRAIN + core * count
-        other = GRAIN * (k + 1)
+        count, other = plan.low_rows(k), plan.rows - plan.low_rows(k)
+        start = low * plan.members + k * plan.step + core * count
+        after = (low + 1) * plan.members + core * other
         for half in range(2):
             lanes = slice(half * LANES, (half + 1) * LANES)
-            base = half * rows
-            out_ref[device, base : base + count, :] = a_ref[low, start : start + count, lanes]
-            out_ref[device, base + count : base + rows, :] = a_ref[
-                low + 1, core * other : (core + 1) * other, lanes
-            ]
-            for level in range(2):
-                for n, part in enumerate(parts):
-                    row = 6 * half + 3 * level + n
-                    ext_ref[device, row : row + 1, :] = part[low + level : low + level + 1, lanes]
-        for n, part in enumerate(weights):
-            ext_ref[device, 12 + n : 13 + n, :] = part
-        ext_ref[device, 15:16, :] = blank
-    for device in range(plan.count):
-        if device in taken:
-            out_ref[device, plan.extra : plan.extra + 16, :] = ext_ref[device].astype(jnp.bfloat16)
-        else:
-            out_ref[device] = jnp.zeros((plan.height, LANES), jnp.bfloat16)
+            pieces = [wide_ref[start : start + count, lanes], wide_ref[after : after + other, lanes]]
+            pieces += [part[low : low + 1, lanes] for part in forcing]
+            spare = plan.block - plan.rows - 3
+            if spare:
+                pieces.append(jnp.zeros((spare, LANES), jnp.float32))
+            out_ref[device, half * plan.block : (half + 1) * plan.block, :] = jnp.concatenate(
+                pieces, axis=0
+            ).astype(jnp.bfloat16)
+        pieces = [part[low + 1 : low + 2, :LANES] for part in forcing]
+        pieces += [part[low + 1 : low + 2, LANES:] for part in forcing]
+        out_ref[device, 2 * plan.block :, :] = jnp.concatenate(pieces + [high, middle], axis=0).astype(jnp.bfloat16)
 
 
 def build_maps(side, kernel_ref, lt_ref, by_lat_ref, turned_ref):
@@ -157,25 +153,25 @@
             ]
 
 
-def read_weights(plan, got_ref, wide_ref):
-    extra = got_ref[:, plan.extra : plan.extra + 16, :].astype(jnp.float32)
-    weights = extra[:, 12, :] + extra[:, 13, :] + extra[:, 14, :]
+def read_extra(plan, got_ref, wide_ref):
+    first = plan.rows // 16 * 16
+    at = plan.rows - first
+    tail = got_ref[:, 2 * plan.block :, :].astype(jnp.float32)
+    weights = tail[:, 6, :] + tail[:, 7, :]
     for k in range(len(DIRECTIONS)):
         wide_ref[k] = jnp.broadcast_to(weights[:, k : k + 1], (plan.count, plan.columns))
-    return extra
-
-
-def forcing_of(extra, level):
-    halves = []
+    low, high = [], []
     for half in range(2):
-        row = 6 * half + 3 * level
-        halves.append(extra[:, row, :] + extra[:, row + 1, :] + extra[:, row + 2, :])
-    return jnp.concatenate(halves, axis=1)
+        slab = got_ref[:, half * plan.block + first : (half + 1) * plan.block, :].astype(jnp.float32)
+        low.append(slab[:, at, :] + slab[:, at + 1, :] + slab[:, at + 2, :])
+        high.append(tail[:, 3 * half, :] + tail[:, 3 * half + 1, :] + tail[:, 3 * half + 2, :])
+    return [jnp.concatenate(low, axis=1), jnp.concatenate(high, axis=1)]
 
 
 def apply_rows(plan, low, got_ref, v_ref, lt_ref, wide_ref, w_ref, s_ref, p_ref):
-    bands, lons, rows = plan.bands, plan.lons, plan.rows
-    grains = rows // GRAIN
+    bands, lons, rows = plan.bands, plan.lons, plan.block
+    place = lax.broadcasted_iota(jnp.int32, (rows, LANES), 0)
+    is_low = place < low
     sides = [slice(half * LANES, (half + 1) * LANES) for half in range(2)]
 
     def block(tile, half):
@@ -184,12 +180,8 @@
     for tile in range(plan.count):
         v_low, v_high = v_ref[0, tile : tile + 1, :], v_ref[1, tile : tile + 1, :]
         for half, lanes in enumerate(sides):
-            values = block(tile, half)
-            pieces = []
-            for g in range(grains):
-                v = jnp.where(g < low, v_low[:, lanes], v_high[:, lanes])
-                pieces.append(values[g * GRAIN : (g + 1) * GRAIN] * v)
-            w_ref[tile * rows : (tile + 1) * rows, lanes] = jnp.concatenate(pieces, axis=0).astype(jnp.bfloat16)
+            v = jnp.where(is_low, v_low[:, lanes], v_high[:, lanes])
+            w_ref[tile * rows : (tile + 1) * rows, lanes] = (block(tile, half) * v).astype(jnp.bfloat16)
 
     for k, (p, q) in enumerate(ALL_STEPS):
         first, last = max(0, p), min(bands, bands + p)
@@ -206,29 +198,22 @@
                 else:
                     s_ref[tile] += piece * wide_ref[k - 1, tile : tile + 1, :]
 
-    shares = [jnp.where(g < low, jnp.float32(1), jnp.float32(0)) for g in range(grains)]
+    low_share = jnp.where(is_low, jnp.float32(1), jnp.float32(0))
+    high_share = jnp.where(is_low | (place >= plan.rows), jnp.float32(0), jnp.float32(1))
     for band in range(bands):
         for half, lanes in enumerate(sides):
             sums = [[], []]
             for l in range(lons):
                 tile = band * lons + l
                 product = block(tile, half) * s_ref[tile, :, lanes]
-                lo = jnp.zeros((GRAIN, LANES), jnp.float32)
-                hi = jnp.zeros((GRAIN, LANES), jnp.float32)
-                for g in range(grains):
-                    piece = product[g * GRAIN : (g + 1) * GRAIN]
-                    lo = lo + piece * shares[g]
-                    hi = hi + piece * (1 - shares[g])
-                sums[0].append(jnp.sum(lo, axis=0, keepdims=True))
-                sums[1].append(jnp.sum(hi, axis=0, keepdims=True))
+                sums[0].append(jnp.sum(product * low_share, axis=0, keepdims=True))
+                sums[1].append(jnp.sum(product * high_share, axis=0, keepdims=True))
             for level in range(2):
                 p_ref[level, band, :, lanes] = jnp.concatenate(sums[level], axis=0)
 
 
 def first_kernel(plan, info_ref, got_ref, lt_ref, p_ref, v_ref, wide_ref, w_ref, s_ref):
-    extra = read_weights(plan, got_ref, wide_ref)
-    v_ref[0] = forcing_of(extra, 0)
-    v_ref[1] = forcing_of(extra, 1)
+    v_ref[0], v_ref[1] = read_extra(plan, got_ref, wide_ref)
     apply_rows(plan, info_ref[0], got_ref, v_ref, lt_ref, wide_ref, w_ref, s_ref, p_ref)
 
 
@@ -238,12 +223,12 @@
 
 def second_kernel(plan, info_ref, got_ref, lt_ref, sum_ref, before_ref, after_ref, out_ref,
                   v_ref, wide_ref, w_ref, s_ref, p_ref):
-    extra = read_weights(plan, got_ref, wide_ref)
+    forcing = read_extra(plan, got_ref, wide_ref)
     images = (sum_ref[0] + before_ref[...], sum_ref[1] + after_ref[...])
     lane = lax.broadcasted_iota(jnp.int32, (1, LANES), 1)
     first = jnp.zeros((1, LANES), jnp.float32)
     for level in range(2):
-        b = forcing_of(extra, level)
+        b = forcing[level]
         u = images[level]
         bb, bu = total(b * b), total(b * u)
         ratio = jnp.where(bb > 0, bu / jnp.where(bb > 0, bb, 1.0), 0.0)
@@ -257,7 +242,7 @@
     apply_rows(plan, info_ref[0], got_ref, v_ref, lt_ref, wide_ref, w_ref, s_ref, p_ref)
     second = jnp.zeros((1, LANES), jnp.float32)
     for level in range(2):
-        b = forcing_of(extra, level)
+        b = forcing[level]
         t = p_ref[level].reshape(plan.count, plan.columns)
         for n, value in enumerate((total(v_ref[level] * t), total(b * t))):
             at = lane == info_ref[4] + level + SLOT * n
@@ -351,7 +336,7 @@
 def by_levels(plan, anomalies, forcing, pair_code, kernel, tile_taper):
     axes = ("band", "tile")
     bf16, f32 = jnp.bfloat16, jnp.float32
-    n, rows, columns = plan.count, plan.rows, plan.columns
+    n, rows, columns = plan.count, plan.block, plan.columns
     side = (kernel.shape[0] + 1) // 4
     wide = 4 * side * side
     a, f = anomalies[0, 0], jnp.swapaxes(forcing[0], 0, 1)
@@ -360,7 +345,7 @@
         out_shape=jax.ShapeDtypeStruct((n, plan.height, LANES), bf16),
         in_specs=[smem(), smem(), vmem(), vmem()],
         out_specs=vmem(),
-        scratch_shapes=[pltpu.VMEM((n, 16, LANES), f32)],
+        scratch_shapes=[pltpu.VMEM((plan.levels * plan.members, columns), f32)],
         name="pack",
     )(pair_code, tile_taper, a, f)
     got = lax.all_to_all(sent, axes, 0, 0)

time: 62.1 us -> 60.7 us (0.977)
  waiting for transfers between devices: 24.6 us -> 23.2 us
    all_to_all x1, waiting for transfers between devices: 21.8 us -> 20.4 us  [by_levels(): got = lax.all_to_all(sent, axes, 0, 0)]
where the time goes in v3:
time: 60.7 us; the launch traced here: 60.3 us
  waiting for transfers between devices  23.2 us (38%)
  starting transfers between devices  13.2 us (22%)
  blocking collectives  12.5 us (21%)
  Pallas kernels  9.83 us (16%)
  between operations  0.73 us (1%)
  local copies, waits for them, and re-layouts  0.72 us (1%)
    all_to_all x1, waiting for transfers between devices, by_levels(): got = lax.all_to_all(sent, axes, 0, 0)  20.4 us
    all_to_all x1, blocking collectives, by_levels(): home = lax.all_to_all(back, axes, 0, 0)  12.5 us
    all_to_all x1, starting transfers between devices, by_levels(): got = lax.all_to_all(sent, axes, 0, 0)  7.33 us
    ppermute x1, starting transfers between devices, by_levels(): before = lax.ppermute(both[1], axes, onward)  4.55 us
    pallas_call x1, Pallas kernels, by_levels(): pl.pallas_call(functools.partial(second_kernel, plan), out_shape=jax.Shap...  3.02 us
    pallas_call x1, Pallas kernels, by_levels(): pl.pallas_call(functools.partial(first_kernel, plan), out_shape=jax.Shape...  2.69 us
    pallas_call x1, Pallas kernels, by_levels(): pl.pallas_call(functools.partial(pack_kernel, plan, tile_taper.shape[0]),...  2.36 us
    ppermute x1, waiting for transfers between devices, by_levels(): before = lax.ppermute(both[1], axes, onward)  1.57 us
  transfers between devices with their start and end apart: 4, of which 3 were waited for; matrix products, arithmetic and copies ran while one was open for 1% of the time, Pallas kernels for 1%

profile of v3, /device:TPU:0, one launch (start us, length us, event | category | flops | bytes accessed | tf_op | source)
XLA Modules:
  0.0 60.3 jit_solution(11862276127262637493)
XLA Ops:
  0.6 2.4 %pack.1 = bf16[32,104,128]{2,1,0:T(8,128)(2,1)} custom-call(s32[1,1,8]{2,1,0:T(1,128)} %code_ref.1, f32[4]{0:T(128)} %taper_ref.1, bf16[18,80,256]{2,1,0:T(8,128)(2,1)} %bitcast.19, f32[18,1,256]{2,1,0:T(1,128)} %bitcast.17), custom_call_target="tpu_custom_call" | custom-call | tf_op jit(solution)/shard_map/pack/pallas_call | solution.py:343
  3.0 0.0 copy-start.1
  3.0 7.3 %all-to-all-start = ((bf16[32,104,128]{2,1,0:T(8,128)(2,1)}), bf16[32,104,128]{2,1,0:T(8,128)(2,1)S(1)}, u32[]{:S(2)}, u32[]{:S(2)}) async-start(bf16[32,104,128]{2,1,0:T(8,128)(2,1)} %pack.1), calls=%async_computation | async-start | bytes 1703936 | tf_op jit(solution)/shard_map/all_to_all | solution.py:351
  10.3 0.0 copy-done.1
  10.3 0.9 %maps.1.lt_ref = bf16[9,256,256]{2,1,0:T(8,128)(2,1)S(1)} custom-call(f32[63,63]{1,0:T(8,128)S(1)} %copy-done.1), custom_call_target="tpu_custom_call" | custom-call | flops 200000000 | bytes 2000000 | tf_op jit(solution)/shard_map/maps/pallas_call | solution.py:360
  11.2 0.7 %dynamic-slice_bitcast_fusion.info_ref = s32[8]{0:T(128)S(1)} fusion(s32[32,8]{1,0:T(8,128)} %constant.16.clone, s32[]{:T(128)S(6)} %select_n.3), kind=kLoop, calls=%fused_computation.2 | loop fusion | bytes 68 | tf_op jit(solution)/shard_map/squeeze | solution.py:353
  11.9 20.4 %all-to-all-done.got_ref = bf16[32,104,128]{2,1,0:T(8,128)(2,1)S(1)} async-done(((bf16[32,104,128]{2,1,0:T(8,128)(2,1)}), bf16[32,104,128]{2,1,0:T(8,128)(2,1)S(1)}, u32[]{:S(2)}, u32[]{:S(2)}) %all-to-all-start) | async-done | bytes 852000 | tf_op jit(solution)/shard_map/all_to_all | solution.py:351
  32.3 2.7 %first.1 = f32[2,4,8,256]{3,2,1,0:T(8,128)S(1)} custom-call(s32[8]{0:T(128)S(1)} %dynamic-slice_bitcast_fusion.info_ref, bf16[32,104,128]{2,1,0:T(8,128)(2,1)S(1)} %all-to-all-done.got_ref, bf16[9,256,256]{2,1,0:T(8,128)(2,1)S(1)} %maps.1.lt_ref), custom_call_target="tpu_custom_call" | custom-call | tf_op jit(solution)/shard_map/first/pallas_call | solution.py:371
  35.0 0.1 collective-permute-start
  35.1 1.2 %collective-permute-done = f32[2,32,256]{2,1,0:T(8,128)S(1)} collective-permute-done((f32[2,32,256]{2,1,0:T(8,128)S(1)}, f32[2,32,256]{2,1,0:T(8,128)S(1)}, u32[]{:S(2)}, u32[]{:S(2)}) %collective-permute-start) | collective-permute-done | bytes 65568 | tf_op jit(solution)/shard_map/ppermute | solution.py:382
  36.4 1.3 %collective-permute-start.2 = (f32[32,256]{1,0:T(8,128)S(1)}, f32[32,256]{1,0:T(8,128)S(1)}, u32[]{:S(2)}, u32[]{:S(2)}) collective-permute-start(f32[32,256]{1,0:T(8,128)S(1)} %get-tuple-element.8), channel_id=1, source_target_pairs={{2,0},{3,1},{6,2},{7,3},{4,6},{5,7},{12,4},{13,5},{14,12},{15,13},... | collective-permute-start | bytes 98312 | tf_op jit(solution)/shard_map/ppermute | solution.py:385
  37.7 0.0 copy-start
  37.7 4.5 %collective-permute-start.1 = (f32[32,256]{1,0:T(8,128)S(1)}, f32[32,256]{1,0:T(8,128)S(1)}, u32[]{:S(2)}, u32[]{:S(2)}) collective-permute-start(f32[32,256]{1,0:T(8,128)S(1)} %get-tuple-element.9), channel_id=1, source_target_pairs={{0,2},{1,3},{2,6},{3,7},{6,4},{7,5},{4,12},{5,13},{12,14},{13,15},... | collective-permute-start | bytes 98312 | tf_op jit(solution)/shard_map/ppermute | solution.py:384
  42.2 0.0 collective-permute-done.2.after_ref
  42.2 1.6 %collective-permute-done.1.before_ref = f32[32,256]{1,0:T(8,128)S(1)} collective-permute-done((f32[32,256]{1,0:T(8,128)S(1)}, f32[32,256]{1,0:T(8,128)S(1)}, u32[]{:S(2)}, u32[]{:S(2)}) %collective-permute-start.1) | collective-permute-done | bytes 32800 | tf_op jit(solution)/shard_map/ppermute | solution.py:384
  43.8 3.0 %second.1 = f32[32,8,128]{2,1,0:T(8,128)S(1)} custom-call(s32[8]{0:T(128)S(1)} %dynamic-slice_bitcast_fusion.info_ref, bf16[32,104,128]{2,1,0:T(8,128)(2,1)S(1)} %all-to-all-done.got_ref, bf16[9,256,256]{2,1,0:T(8,128)(2,1)S(1)} %maps.1.lt_ref, f32[2,32,256]{2,1,0:T(8,128)S(1)} %bitcast_add_fusion.sum_ref, f32[32,256]{1,0:T(8,128)S(1)} %collective-permute-done.1.before_ref, ...), custom_call_target="tpu_custom_call" | custom-call | tf_op jit(solution)/shard_map/second/pallas_call | solution.py:386
  46.8 12.5 %all_to_all.10.got_ref = f32[32,8,128]{2,1,0:T(8,128)S(1)} all-to-all(f32[32,8,128]{2,1,0:T(8,128)S(1)} %second.1), channel_id=1, replica_groups=mesh['band'=4,'tile'=8] {'band','tile'}, dimensions={0} | all-to-all | bytes 262144 | tf_op jit(solution)/shard_map/all_to_all | solution.py:395
  59.4 0.0 copy-done
  59.4 0.9 %last.1 = (f32[18,1,256]{2,1,0:T(1,128)}, f32[18,1,256]{2,1,0:T(1,128)}) custom-call(f32[18,1,256]{2,1,0:T(1,128)S(1)} %bitcast.18, f32[32,8,128]{2,1,0:T(8,128)S(1)} %all_to_all.10.got_ref), custom_call_target="tpu_custom_call" | custom-call | tf_op jit(solution)/shard_map/last/pallas_call | solution.py:396
  (2 shorter events, 0.0 us)
Async XLA Ops:
  3.0 7.3 %copy-start.1 = (f32[63,63]{1,0:T(8,128)S(1)}, f32[63,63]{1,0:T(8,128)}, u32[]{:S(2)}) copy-start(f32[63,63]{1,0:T(8,128)} %kernel_ref.1) | copy-start | bytes 47632
  3.0 29.3 %all-to-all-start = ((bf16[32,104,128]{2,1,0:T(8,128)(2,1)}), bf16[32,104,128]{2,1,0:T(8,128)(2,1)S(1)}, u32[]{:S(2)}, u32[]{:S(2)}) async-start(bf16[32,104,128]{2,1,0:T(8,128)(2,1)} %pack.1), calls=%async_computation | async-start | bytes 1703936 | tf_op jit(solution)/shard_map/all_to_all | solution.py:351
  35.0 1.3 %collective-permute-start = (f32[2,32,256]{2,1,0:T(8,128)S(1)}, f32[2,32,256]{2,1,0:T(8,128)S(1)}, u32[]{:S(2)}, u32[]{:S(2)}) collective-permute-start(f32[2,32,256]{2,1,0:T(8,128)S(1)} %bitcast.16), channel_id=1, source_target_pairs={{0,1},{1,0},{2,3},{3,2},{4,5},{5,4},{6,7},{7,6},{8,9},{9,8},{10,11... | collective-permute-start | bytes 196616 | tf_op jit(solution)/shard_map/ppermute | solution.py:382
  36.4 5.9 %collective-permute-start.2 = (f32[32,256]{1,0:T(8,128)S(1)}, f32[32,256]{1,0:T(8,128)S(1)}, u32[]{:S(2)}, u32[]{:S(2)}) collective-permute-start(f32[32,256]{1,0:T(8,128)S(1)} %get-tuple-element.8), channel_id=1, source_target_pairs={{2,0},{3,1},{6,2},{7,3},{4,6},{5,7},{12,4},{13,5},{14,12},{15,13},... | collective-permute-start | bytes 98312 | tf_op jit(solution)/shard_map/ppermute | solution.py:385
  37.7 21.7 %copy-start = (f32[1,1,18,256]{3,1,2,0:T(1,128)S(1)}, f32[1,1,18,256]{3,1,2,0:T(1,128)}, u32[]{:S(2)}) copy-start(f32[1,1,18,256]{3,1,2,0:T(1,128)} %param.7) | copy-start | bytes 55300
  37.7 6.1 %collective-permute-start.1 = (f32[32,256]{1,0:T(8,128)S(1)}, f32[32,256]{1,0:T(8,128)S(1)}, u32[]{:S(2)}, u32[]{:S(2)}) collective-permute-start(f32[32,256]{1,0:T(8,128)S(1)} %get-tuple-element.9), channel_id=1, source_target_pairs={{0,2},{1,3},{2,6},{3,7},{6,4},{7,5},{4,12},{5,13},{12,14},{13,15},... | collective-permute-start | bytes 98312 | tf_op jit(solution)/shard_map/ppermute | solution.py:384

commit v4 on v3

--- a/solution.py
+++ b/solution.py
@@ -72,12 +72,12 @@
             out[device, :5] = (self.low_rows(k), core, int(core == 0), int(core == 1 and last), low)
         return out
 
-    def onward(self):
+    def outward(self):
         pairs = []
         for group in range(self.groups):
-            for k in range(self.depth - 1):
-                for core in range(2):
-                    pairs.append((self.device(group, k, core), self.device(group, k + 1, core)))
+            for k in range(1, self.depth):
+                pairs.append((self.device(group, k, 0), self.device(group, k - 1, 0)))
+                pairs.append((self.device(group, k - 1, 1), self.device(group, k, 1)))
         return pairs
 
 
@@ -168,7 +168,7 @@
     return [jnp.concatenate(low, axis=1), jnp.concatenate(high, axis=1)]
 
 
-def apply_rows(plan, low, got_ref, v_ref, lt_ref, wide_ref, w_ref, s_ref, p_ref):
+def apply_rows(plan, low, order, got_ref, v_ref, lt_ref, wide_ref, w_ref, s_ref, p_ref):
     bands, lons, rows = plan.bands, plan.lons, plan.block
     place = lax.broadcasted_iota(jnp.int32, (rows, LANES), 0)
     is_low = place < low
@@ -209,22 +209,26 @@
                 sums[0].append(jnp.sum(product * low_share, axis=0, keepdims=True))
                 sums[1].append(jnp.sum(product * high_share, axis=0, keepdims=True))
             for level in range(2):
-                p_ref[level, band, :, lanes] = jnp.concatenate(sums[level], axis=0)
+                p_ref[order[level], band, :, lanes] = jnp.concatenate(sums[level], axis=0)
 
 
 def first_kernel(plan, info_ref, got_ref, lt_ref, p_ref, v_ref, wide_ref, w_ref, s_ref):
     v_ref[0], v_ref[1] = read_extra(plan, got_ref, wide_ref)
-    apply_rows(plan, info_ref[0], got_ref, v_ref, lt_ref, wide_ref, w_ref, s_ref, p_ref)
+    order = (info_ref[1], 1 - info_ref[1])
+    apply_rows(plan, info_ref[0], order, got_ref, v_ref, lt_ref, wide_ref, w_ref, s_ref, p_ref)
 
 
 def total(x):
     return jnp.sum(jnp.sum(x, axis=1, keepdims=True), axis=0, keepdims=True)
 
 
-def second_kernel(plan, info_ref, got_ref, lt_ref, sum_ref, before_ref, after_ref, out_ref,
+def second_kernel(plan, info_ref, got_ref, lt_ref, own_ref, other_ref, far_ref, far_other_ref, out_ref,
                   v_ref, wide_ref, w_ref, s_ref, p_ref):
     forcing = read_extra(plan, got_ref, wide_ref)
-    images = (sum_ref[0] + before_ref[...], sum_ref[1] + after_ref[...])
+    mine = (own_ref[0] + other_ref[1]) + far_other_ref[...]
+    rest = (own_ref[1] + other_ref[0]) + far_ref[...]
+    first_core = info_ref[1] == 0
+    images = (jnp.where(first_core, mine, rest), jnp.where(first_core, rest, mine))
     lane = lax.broadcasted_iota(jnp.int32, (1, LANES), 1)
     first = jnp.zeros((1, LANES), jnp.float32)
     for level in range(2):
@@ -232,14 +236,14 @@
         u = images[level]
         bb, bu = total(b * b), total(b * u)
         ratio = jnp.where(bb > 0, bu / jnp.where(bb > 0, bb, 1.0), 0.0)
-        rest = ratio * b - u
-        v_ref[level] = rest
-        values = (bb, total(b * rest), total(rest * rest), ratio)
+        q = ratio * b - u
+        v_ref[level] = q
+        values = (bb, total(b * q), total(q * q), ratio)
         speaks = jnp.where(info_ref[2 + level] > 0, jnp.float32(1), jnp.float32(0))
         for n, value in enumerate(values):
             at = lane == info_ref[4] + level + SLOT * n
             first = first + jnp.where(at, value, 0.0) * speaks
-    apply_rows(plan, info_ref[0], got_ref, v_ref, lt_ref, wide_ref, w_ref, s_ref, p_ref)
+    apply_rows(plan, info_ref[0], (0, 1), got_ref, v_ref, lt_ref, wide_ref, w_ref, s_ref, p_ref)
     second = jnp.zeros((1, LANES), jnp.float32)
     for level in range(2):
         b = forcing[level]
@@ -247,7 +251,6 @@
         for n, value in enumerate((total(v_ref[level] * t), total(b * t))):
             at = lane == info_ref[4] + level + SLOT * n
             second = second + jnp.where(at, value, 0.0)
-    mine = jnp.where(info_ref[1] == 0, images[0], images[1])
     for half in range(2):
         lanes = slice(half * LANES, (half + 1) * LANES)
         out_ref[:, half, :] = mine[:, lanes]
@@ -379,19 +382,18 @@
     )(info, got, maps)
     part = part.reshape(2, n, columns)
     swap = [(i, i ^ 1) for i in range(plan.lons)]
-    both = part + lax.ppermute(part, "tile", swap)
-    onward = plan.onward()
-    before = lax.ppermute(both[1], axes, onward)
-    after = lax.ppermute(both[0], axes, [(t, s) for s, t in onward])
+    other = lax.ppermute(part, "tile", swap)
+    far = lax.ppermute(part[0] + other[1], axes, plan.outward())
+    far_other = lax.ppermute(far, "tile", swap)
     back = pl.pallas_call(
         functools.partial(second_kernel, plan),
         out_shape=jax.ShapeDtypeStruct((n, 8, LANES), f32),
-        in_specs=[smem()] + [vmem()] * 5,
+        in_specs=[smem()] + [vmem()] * 6,
         out_specs=vmem(),
         scratch_shapes=work + [pltpu.VMEM((2, plan.bands, plan.lons, columns), f32)],
         compiler_params=room(20),
         name="second",
-    )(info, got, maps, both, before, after)
+    )(info, got, maps, part, other, far, far_other)
     home = lax.all_to_all(back, axes, 0, 0)
     increment, residual = pl.pallas_call(
         functools.partial(last_kernel, plan),

time: 60.7 us -> 59.4 us (0.979)
  starting transfers between devices: 13.2 us -> 8.69 us
  waiting for transfers between devices: 23.2 us -> 27.4 us
  blocking collectives: 12.5 us -> 11.6 us
    ppermute x3, starting transfers between devices: 5.91 us -> 1.37 us  [the longest x1 1.29 us: by_levels(): far = lax.ppermute(part[0] + other[1], axes, plan.outward())]
    ppermute x3, waiting for transfers between devices: 2.81 us -> 6.95 us  [the longest x1 4.51 us: by_levels(): far = lax.ppermute(part[0] + other[1], axes, plan.outward())]
    all_to_all x1, blocking collectives: 12.5 us -> 11.6 us  [by_levels(): home = lax.all_to_all(back, axes, 0, 0)]
  transfers between devices with their start and end apart: 4 -> 4, of which waited for: 3 -> 4; matrix products, arithmetic and copies ran while one was open for 1% -> 1% of each run, Pallas kernels for 1% -> 1%
where the time goes in v4:
time: 59.4 us; the launch traced here: 59 us
  waiting for transfers between devices  27.4 us (46%)
  blocking collectives  11.6 us (20%)
  Pallas kernels  9.88 us (17%)
  starting transfers between devices  8.69 us (15%)
  local copies, waits for them, and re-layouts  0.71 us (1%)
  between operations  0.7 us (1%)
    all_to_all x1, waiting for transfers between devices, by_levels(): got = lax.all_to_all(sent, axes, 0, 0)  20.4 us
    all_to_all x1, blocking collectives, by_levels(): home = lax.all_to_all(back, axes, 0, 0)  11.6 us
    all_to_all x1, starting transfers between devices, by_levels(): got = lax.all_to_all(sent, axes, 0, 0)  7.33 us
    ppermute x1, waiting for transfers between devices, by_levels(): far = lax.ppermute(part[0] + other[1], axes, plan.outward())  4.51 us
    pallas_call x1, Pallas kernels, by_levels(): pl.pallas_call(functools.partial(second_kernel, plan), out_shape=jax.Shap...  3.04 us
    pallas_call x1, Pallas kernels, by_levels(): pl.pallas_call(functools.partial(first_kernel, plan), out_shape=jax.Shape...  2.7 us
    pallas_call x1, Pallas kernels, by_levels(): pl.pallas_call(functools.partial(pack_kernel, plan, tile_taper.shape[0]),...  2.37 us
    ppermute x1, starting transfers between devices, by_levels(): far = lax.ppermute(part[0] + other[1], axes, plan.outward())  1.29 us
  transfers between devices with their start and end apart: 4, of which 4 were waited for; matrix products, arithmetic and copies ran while one was open for 1% of the time, Pallas kernels for 1%

profile of v4, /device:TPU:0, one launch (start us, length us, event | category | flops | bytes accessed | tf_op | source)
XLA Modules:
  0.0 59.0 jit_solution(7863635118336713174)
XLA Ops:
  0.6 2.4 %pack.1 = bf16[32,104,128]{2,1,0:T(8,128)(2,1)} custom-call(s32[1,1,8]{2,1,0:T(1,128)} %code_ref.1, f32[4]{0:T(128)} %taper_ref.1, bf16[18,80,256]{2,1,0:T(8,128)(2,1)} %bitcast.23, f32[18,1,256]{2,1,0:T(1,128)} %bitcast.21), custom_call_target="tpu_custom_call" | custom-call | tf_op jit(solution)/shard_map/pack/pallas_call | solution.py:346
  3.0 0.0 copy-start.1
  3.0 7.3 %all-to-all-start = ((bf16[32,104,128]{2,1,0:T(8,128)(2,1)}), bf16[32,104,128]{2,1,0:T(8,128)(2,1)S(1)}, u32[]{:S(2)}, u32[]{:S(2)}) async-start(bf16[32,104,128]{2,1,0:T(8,128)(2,1)} %pack.1), calls=%async_computation | async-start | bytes 1703936 | tf_op jit(solution)/shard_map/all_to_all | solution.py:354
  10.3 0.0 copy-done.1
  10.3 0.9 %maps.1.lt_ref = bf16[9,256,256]{2,1,0:T(8,128)(2,1)S(1)} custom-call(f32[63,63]{1,0:T(8,128)S(1)} %copy-done.1), custom_call_target="tpu_custom_call" | custom-call | flops 200000000 | bytes 2000000 | tf_op jit(solution)/shard_map/maps/pallas_call | solution.py:363
  11.2 0.7 %dynamic-slice_bitcast_fusion.info_ref = s32[8]{0:T(128)S(1)} fusion(s32[32,8]{1,0:T(8,128)} %constant.16.clone, s32[]{:T(128)S(6)} %select_n.3), kind=kLoop, calls=%fused_computation.3 | loop fusion | bytes 68 | tf_op jit(solution)/shard_map/squeeze | solution.py:356
  11.9 20.4 %all-to-all-done.got_ref = bf16[32,104,128]{2,1,0:T(8,128)(2,1)S(1)} async-done(((bf16[32,104,128]{2,1,0:T(8,128)(2,1)}), bf16[32,104,128]{2,1,0:T(8,128)(2,1)S(1)}, u32[]{:S(2)}, u32[]{:S(2)}) %all-to-all-start) | async-done | bytes 852000 | tf_op jit(solution)/shard_map/all_to_all | solution.py:354
  32.3 2.7 %first.1 = f32[2,4,8,256]{3,2,1,0:T(8,128)S(1)} custom-call(s32[8]{0:T(128)S(1)} %dynamic-slice_bitcast_fusion.info_ref, bf16[32,104,128]{2,1,0:T(8,128)(2,1)S(1)} %all-to-all-done.got_ref, bf16[9,256,256]{2,1,0:T(8,128)(2,1)S(1)} %maps.1.lt_ref), custom_call_target="tpu_custom_call" | custom-call | tf_op jit(solution)/shard_map/first/pallas_call | solution.py:374
  35.0 0.1 collective-permute-start
  35.1 1.2 %collective-permute-done.other_ref = f32[2,32,256]{2,1,0:T(8,128)S(1)} collective-permute-done((f32[2,32,256]{2,1,0:T(8,128)S(1)}, f32[2,32,256]{2,1,0:T(8,128)S(1)}, u32[]{:S(2)}, u32[]{:S(2)}) %collective-permute-start) | collective-permute-done | bytes 65568 | tf_op jit(solution)/shard_map/ppermute | solution.py:385
  36.4 0.0 copy-start
  36.4 1.3 %collective-permute-start.1 = (f32[32,256]{1,0:T(8,128)S(1)}, f32[32,256]{1,0:T(8,128)S(1)}, u32[]{:S(2)}, u32[]{:S(2)}) collective-permute-start(f32[32,256]{1,0:T(8,128)S(1)} %fusion), channel_id=1, source_target_pairs={{2,0},{1,3},{6,2},{3,7},{4,6},{7,5},{12,4},{5,13},{14,12},{13,15},... | collective-permute-start | bytes 98312 | tf_op jit(solution)/shard_map/ppermute | solution.py:386
  37.7 4.5 %collective-permute-done.1.far_ref = f32[32,256]{1,0:T(8,128)S(1)} collective-permute-done((f32[32,256]{1,0:T(8,128)S(1)}, f32[32,256]{1,0:T(8,128)S(1)}, u32[]{:S(2)}, u32[]{:S(2)}) %collective-permute-start.1) | collective-permute-done | bytes 32800 | tf_op jit(solution)/shard_map/ppermute | solution.py:386
  42.2 0.0 collective-permute-start.2
  42.2 1.2 %collective-permute-done.2.far_other_ref = f32[32,256]{1,0:T(8,128)S(1)} collective-permute-done((f32[32,256]{1,0:T(8,128)S(1)}, f32[32,256]{1,0:T(8,128)S(1)}, u32[]{:S(2)}, u32[]{:S(2)}) %collective-permute-start.2) | collective-permute-done | bytes 32800 | tf_op jit(solution)/shard_map/ppermute | solution.py:387
  43.4 3.0 %second.1 = f32[32,8,128]{2,1,0:T(8,128)S(1)} custom-call(s32[8]{0:T(128)S(1)} %dynamic-slice_bitcast_fusion.info_ref, bf16[32,104,128]{2,1,0:T(8,128)(2,1)S(1)} %all-to-all-done.got_ref, bf16[9,256,256]{2,1,0:T(8,128)(2,1)S(1)} %maps.1.lt_ref, f32[2,32,256]{2,1,0:T(8,128)S(1)} %bitcast.20, f32[2,32,256]{2,1,0:T(8,128)S(1)} %collective-permute-done.other_ref, ...), custom_call_target="tpu_custom_call" | custom-call | tf_op jit(solution)/shard_map/second/pallas_call | solution.py:388
  46.4 11.6 %all_to_all.10.got_ref = f32[32,8,128]{2,1,0:T(8,128)S(1)} all-to-all(f32[32,8,128]{2,1,0:T(8,128)S(1)} %second.1), channel_id=1, replica_groups=mesh['band'=4,'tile'=8] {'band','tile'}, dimensions={0} | all-to-all | bytes 262144 | tf_op jit(solution)/shard_map/all_to_all | solution.py:397
  58.1 0.0 copy-done
  58.1 0.9 %last.1 = (f32[18,1,256]{2,1,0:T(1,128)}, f32[18,1,256]{2,1,0:T(1,128)}) custom-call(f32[18,1,256]{2,1,0:T(1,128)S(1)} %bitcast.22, f32[32,8,128]{2,1,0:T(8,128)S(1)} %all_to_all.10.got_ref), custom_call_target="tpu_custom_call" | custom-call | tf_op jit(solution)/shard_map/last/pallas_call | solution.py:398
  (1 shorter events, 0.0 us)
Async XLA Ops:
  3.0 7.3 %copy-start.1 = (f32[63,63]{1,0:T(8,128)S(1)}, f32[63,63]{1,0:T(8,128)}, u32[]{:S(2)}) copy-start(f32[63,63]{1,0:T(8,128)} %kernel_ref.1) | copy-start | bytes 47632
  3.0 29.3 %all-to-all-start = ((bf16[32,104,128]{2,1,0:T(8,128)(2,1)}), bf16[32,104,128]{2,1,0:T(8,128)(2,1)S(1)}, u32[]{:S(2)}, u32[]{:S(2)}) async-start(bf16[32,104,128]{2,1,0:T(8,128)(2,1)} %pack.1), calls=%async_computation | async-start | bytes 1703936 | tf_op jit(solution)/shard_map/all_to_all | solution.py:354
  35.0 1.3 %collective-permute-start = (f32[2,32,256]{2,1,0:T(8,128)S(1)}, f32[2,32,256]{2,1,0:T(8,128)S(1)}, u32[]{:S(2)}, u32[]{:S(2)}) collective-permute-start(f32[2,32,256]{2,1,0:T(8,128)S(1)} %bitcast.19), channel_id=1, source_target_pairs={{0,1},{1,0},{2,3},{3,2},{4,5},{5,4},{6,7},{7,6},{8,9},{9,8},{10,11... | collective-permute-start | bytes 196616 | tf_op jit(solution)/shard_map/ppermute | solution.py:385
  36.4 21.7 %copy-start = (f32[1,1,18,256]{3,1,2,0:T(1,128)S(1)}, f32[1,1,18,256]{3,1,2,0:T(1,128)}, u32[]{:S(2)}) copy-start(f32[1,1,18,256]{3,1,2,0:T(1,128)} %param.7) | copy-start | bytes 55300
  36.4 5.8 %collective-permute-start.1 = (f32[32,256]{1,0:T(8,128)S(1)}, f32[32,256]{1,0:T(8,128)S(1)}, u32[]{:S(2)}, u32[]{:S(2)}) collective-permute-start(f32[32,256]{1,0:T(8,128)S(1)} %fusion), channel_id=1, source_target_pairs={{2,0},{1,3},{6,2},{3,7},{4,6},{7,5},{12,4},{5,13},{14,12},{13,15},... | collective-permute-start | bytes 98312 | tf_op jit(solution)/shard_map/ppermute | solution.py:386
  42.2 1.2 %collective-permute-start.2 = (f32[32,256]{1,0:T(8,128)S(1)}, f32[32,256]{1,0:T(8,128)S(1)}, u32[]{:S(2)}, u32[]{:S(2)}) collective-permute-start(f32[32,256]{1,0:T(8,128)S(1)} %collective-permute-done.1.far_ref), channel_id=1, source_target_pairs={{0,1},{1,0},{2,3},{3,2},{4,5},{5,4},{6,7},{7,6},{8,9},{9,8},{10,11... | collective-permute-start | bytes 98312 | tf_op jit(solution)/shard_map/ppermute | solution.py:387

commit v5 on v4

--- a/solution.py
+++ b/solution.py
@@ -13,6 +13,7 @@
 GRAIN = 8
 LANES = 128
 SLOT = 32
+CHUNK = 1
 
 DIRECTIONS = ((-1, -1), (-1, 0), (-1, 1), (0, -1), (0, 1), (1, -1), (1, 0), (1, 1))
 ALL_STEPS = ((0, 0),) + DIRECTIONS
@@ -88,9 +89,24 @@
     return [high, middle, rest - middle]
 
 
-def pack_kernel(plan, tapers, code_ref, taper_ref, a_ref, f_ref, out_ref, wide_ref):
-    for level in range(plan.levels):
-        wide_ref[level * plan.members : (level + 1) * plan.members, :] = a_ref[level].astype(jnp.float32)
+def pack_kernel(plan, tapers, code_hbm, taper_hbm, a_ref, f_hbm, out_ref,
+                code_ref, taper_ref, f_ref, near_ref, wide_ref, sent_ref, small_sem, in_sem, out_sem):
+    share, size = plan.depth + 1, plan.count // plan.groups
+
+    def fetch(group):
+        run = pl.ds(group * share, share)
+        return pltpu.make_async_copy(a_ref.at[run], near_ref.at[run], in_sem.at[group])
+
+    small = [
+        pltpu.make_async_copy(source, target, small_sem.at[n])
+        for n, (source, target) in enumerate(((code_hbm, code_ref), (taper_hbm, taper_ref), (f_hbm, f_ref)))
+    ]
+    for copy in small:
+        copy.start()
+    for group in range(plan.groups):
+        fetch(group).start()
+    for copy in small:
+        copy.wait()
     forcing = in_three(f_ref[:, 0, :])
     lane = lax.broadcasted_iota(jnp.int32, (1, LANES), 1)
     weights = jnp.zeros((1, LANES), jnp.float32)
@@ -102,7 +118,14 @@
         weights = jnp.where(lane == k, weight, weights)
     weights = weights / jnp.float32(plan.members - 1)
     high, middle, _ = in_three(weights)
+    here = 0
+    copies = []
     for device, k, core, low in plan.owners():
+        if low % share == 0 and core == 0:
+            fetch(low // share).wait()
+        while here < low + 2:
+            wide_ref[here * plan.members : (here + 1) * plan.members, :] = near_ref[here].astype(jnp.float32)
+            here += 1
         count, other = plan.low_rows(k), plan.rows - plan.low_rows(k)
         start = low * plan.members + k * plan.step + core * count
         after = (low + 1) * plan.members + core * other
@@ -113,12 +136,18 @@
             spare = plan.block - plan.rows - 3
             if spare:
                 pieces.append(jnp.zeros((spare, LANES), jnp.float32))
-            out_ref[device, half * plan.block : (half + 1) * plan.block, :] = jnp.concatenate(
+            sent_ref[device, half * plan.block : (half + 1) * plan.block, :] = jnp.concatenate(
                 pieces, axis=0
             ).astype(jnp.bfloat16)
         pieces = [part[low + 1 : low + 2, :LANES] for part in forcing]
         pieces += [part[low + 1 : low + 2, LANES:] for part in forcing]
-        out_ref[device, 2 * plan.block :, :] = jnp.concatenate(pieces + [high, middle], axis=0).astype(jnp.bfloat16)
+        sent_ref[device, 2 * plan.block :, :] = jnp.concatenate(pieces + [high, middle], axis=0).astype(jnp.bfloat16)
+        if k == plan.depth - 1 and core == 1:
+            run = pl.ds(len(copies) * size, size)
+            copies.append(pltpu.make_async_copy(sent_ref.at[run], out_ref.at[run], out_sem.at[len(copies)]))
+            copies[-1].start()
+    for copy in copies:
+        copy.wait()
 
 
 def build_maps(side, kernel_ref, lt_ref, by_lat_ref, turned_ref):
@@ -183,33 +212,48 @@
             v = jnp.where(is_low, v_low[:, lanes], v_high[:, lanes])
             w_ref[tile * rows : (tile + 1) * rows, lanes] = (block(tile, half) * v).astype(jnp.bfloat16)
 
-    for k, (p, q) in enumerate(ALL_STEPS):
-        first, last = max(0, p), min(bands, bands + p)
-        y = jnp.dot(
-            w_ref[first * lons * rows : last * lons * rows, :], lt_ref[k], preferred_element_type=jnp.float32
-        )
-        for band in range(first, last):
-            for l in range(lons):
-                tile = (band - p) * lons + (l - q) % lons
-                at = ((band - first) * lons + l) * rows
-                piece = y[at : at + rows]
-                if k == 0:
-                    s_ref[tile] = piece * jnp.float32(1.0 / (plan.members - 1))
-                else:
-                    s_ref[tile] += piece * wide_ref[k - 1, tile : tile + 1, :]
-
     low_share = jnp.where(is_low, jnp.float32(1), jnp.float32(0))
     high_share = jnp.where(is_low | (place >= plan.rows), jnp.float32(0), jnp.float32(1))
-    for band in range(bands):
+    sums = {}
+
+    def finish(tile, spread):
         for half, lanes in enumerate(sides):
-            sums = [[], []]
-            for l in range(lons):
-                tile = band * lons + l
-                product = block(tile, half) * s_ref[tile, :, lanes]
-                sums[0].append(jnp.sum(product * low_share, axis=0, keepdims=True))
-                sums[1].append(jnp.sum(product * high_share, axis=0, keepdims=True))
-            for level in range(2):
-                p_ref[order[level], band, :, lanes] = jnp.concatenate(sums[level], axis=0)
+            product = block(tile, half) * spread[:, lanes]
+            for level, share in enumerate((low_share, high_share)):
+                sums[tile, level, half] = jnp.sum(product * share, axis=0, keepdims=True)
+
+    touched = set()
+    steps = sorted(ALL_STEPS, key=lambda step: (step[0] == 0, step == (0, 0)))
+    for start in range(0, bands, CHUNK):
+        stop = min(start + CHUNK, bands)
+        for p, q in steps:
+            first, last = max(0, start + p), min(bands, stop + p)
+            if first >= last:
+                continue
+            k = ALL_STEPS.index((p, q))
+            y = jnp.dot(
+                w_ref[first * lons * rows : last * lons * rows, :], lt_ref[k], preferred_element_type=jnp.float32
+            )
+            for band in range(first, last):
+                for l in range(lons):
+                    tile = (band - p) * lons + (l - q) % lons
+                    at = ((band - first) * lons + l) * rows
+                    term = y[at : at + rows]
+                    if k == 0:
+                        finish(tile, s_ref[tile] + term * jnp.float32(1.0 / (plan.members - 1)))
+                        continue
+                    term = term * wide_ref[k - 1, tile : tile + 1, :]
+                    if tile in touched:
+                        s_ref[tile] += term
+                    else:
+                        s_ref[tile] = term
+                        touched.add(tile)
+                if k == 0:
+                    for level in range(2):
+                        for half, lanes in enumerate(sides):
+                            p_ref[order[level], band, :, lanes] = jnp.concatenate(
+                                [sums[band * lons + l, level, half] for l in range(lons)], axis=0
+                            )
 
 
 def first_kernel(plan, info_ref, got_ref, lt_ref, p_ref, v_ref, wide_ref, w_ref, s_ref):
@@ -222,9 +266,8 @@
     return jnp.sum(jnp.sum(x, axis=1, keepdims=True), axis=0, keepdims=True)
 
 
-def second_kernel(plan, info_ref, got_ref, lt_ref, own_ref, other_ref, far_ref, far_other_ref, out_ref,
-                  v_ref, wide_ref, w_ref, s_ref, p_ref):
-    forcing = read_extra(plan, got_ref, wide_ref)
+def second_kernel(plan, info_ref, got_ref, lt_ref, b_ref, wide_ref, own_ref, other_ref, far_ref, far_other_ref,
+                  out_ref, v_ref, w_ref, s_ref, p_ref):
     mine = (own_ref[0] + other_ref[1]) + far_other_ref[...]
     rest = (own_ref[1] + other_ref[0]) + far_ref[...]
     first_core = info_ref[1] == 0
@@ -232,7 +275,7 @@
     lane = lax.broadcasted_iota(jnp.int32, (1, LANES), 1)
     first = jnp.zeros((1, LANES), jnp.float32)
     for level in range(2):
-        b = forcing[level]
+        b = b_ref[level]
         u = images[level]
         bb, bu = total(b * b), total(b * u)
         ratio = jnp.where(bb > 0, bu / jnp.where(bb > 0, bb, 1.0), 0.0)
@@ -246,7 +289,7 @@
     apply_rows(plan, info_ref[0], (0, 1), got_ref, v_ref, lt_ref, wide_ref, w_ref, s_ref, p_ref)
     second = jnp.zeros((1, LANES), jnp.float32)
     for level in range(2):
-        b = forcing[level]
+        b = b_ref[level]
         t = p_ref[level].reshape(plan.count, plan.columns)
         for n, value in enumerate((total(v_ref[level] * t), total(b * t))):
             at = lane == info_ref[4] + level + SLOT * n
@@ -346,20 +389,26 @@
     sent = pl.pallas_call(
         functools.partial(pack_kernel, plan, tile_taper.shape[0]),
         out_shape=jax.ShapeDtypeStruct((n, plan.height, LANES), bf16),
-        in_specs=[smem(), smem(), vmem(), vmem()],
-        out_specs=vmem(),
-        scratch_shapes=[pltpu.VMEM((plan.levels * plan.members, columns), f32)],
+        in_specs=[pl.BlockSpec(memory_space=pl.ANY)] * 4,
+        out_specs=pl.BlockSpec(memory_space=pl.ANY),
+        scratch_shapes=[pltpu.SMEM(pair_code.shape, jnp.int32),
+                        pltpu.SMEM(tile_taper.shape, f32),
+                        pltpu.VMEM(f.shape, f32),
+                        pltpu.VMEM(a.shape, bf16),
+                        pltpu.VMEM((plan.levels * plan.members, columns), f32),
+                        pltpu.VMEM((n, plan.height, LANES), bf16),
+                        pltpu.SemaphoreType.DMA((3,)),
+                        pltpu.SemaphoreType.DMA((plan.groups,)),
+                        pltpu.SemaphoreType.DMA((plan.groups,))],
         name="pack",
     )(pair_code, tile_taper, a, f)
     got = lax.all_to_all(sent, axes, 0, 0)
     me = lax.axis_index(axes)
     info = lax.dynamic_slice(jnp.asarray(plan.table()), (me, 0), (1, 8))[0]
-    work = [
-        pltpu.VMEM((2, n, columns), f32),
-        pltpu.VMEM((len(DIRECTIONS), n, columns), f32),
-        pltpu.VMEM((n * rows, columns), bf16),
-        pltpu.VMEM((n, rows, columns), f32),
-    ]
+    both = jax.ShapeDtypeStruct((2, n, columns), f32)
+    shares = jax.ShapeDtypeStruct((2, plan.bands, plan.lons, columns), f32)
+    weights = jax.ShapeDtypeStruct((len(DIRECTIONS), n, columns), f32)
+    work = [pltpu.VMEM((n * rows, columns), bf16), pltpu.VMEM((n, rows, columns), f32)]
     maps = pl.pallas_call(
         functools.partial(build_maps, side),
         out_shape=jax.ShapeDtypeStruct((len(ALL_STEPS), columns, columns), bf16),
@@ -371,11 +420,11 @@
         compiler_params=room(12),
         name="maps",
     )(kernel)
-    part = pl.pallas_call(
+    part, b, wide_weights = pl.pallas_call(
         functools.partial(first_kernel, plan),
-        out_shape=jax.ShapeDtypeStruct((2, plan.bands, plan.lons, columns), f32),
+        out_shape=(shares, both, weights),
         in_specs=[smem(), vmem(), vmem()],
-        out_specs=vmem(),
+        out_specs=(vmem(),) * 3,
         scratch_shapes=work,
         compiler_params=room(20),
         name="first",
@@ -388,12 +437,12 @@
     back = pl.pallas_call(
         functools.partial(second_kernel, plan),
         out_shape=jax.ShapeDtypeStruct((n, 8, LANES), f32),
-        in_specs=[smem()] + [vmem()] * 6,
+        in_specs=[smem()] + [vmem()] * 8,
         out_specs=vmem(),
-        scratch_shapes=work + [pltpu.VMEM((2, plan.bands, plan.lons, columns), f32)],
+        scratch_shapes=[pltpu.VMEM(both.shape, f32)] + work + [pltpu.VMEM(shares.shape, f32)],
         compiler_params=room(20),
         name="second",
-    )(info, got, maps, part, other, far, far_other)
+    )(info, got, maps, b, wide_weights, part, other, far, far_other)
     home = lax.all_to_all(back, axes, 0, 0)
     increment, residual = pl.pallas_call(
         functools.partial(last_kernel, plan),

time: 59.4 us -> 58.7 us (0.988)
  Pallas kernels: 9.88 us -> 9.27 us
where the time goes in v5:
time: 58.7 us; the launch traced here: 58.4 us
  waiting for transfers between devices  27.4 us (47%)
  blocking collectives  11.6 us (20%)
  Pallas kernels  9.27 us (16%)
  starting transfers between devices  8.69 us (15%)
  local copies, waits for them, and re-layouts  0.71 us (1%)
  between operations  0.71 us (1%)
    all_to_all x1, waiting for transfers between devices, by_levels(): got = lax.all_to_all(sent, axes, 0, 0)  20.4 us
    all_to_all x1, blocking collectives, by_levels(): home = lax.all_to_all(back, axes, 0, 0)  11.6 us
    all_to_all x1, starting transfers between devices, by_levels(): got = lax.all_to_all(sent, axes, 0, 0)  7.33 us
    ppermute x1, waiting for transfers between devices, by_levels(): far = lax.ppermute(part[0] + other[1], axes, plan.outward())  4.51 us
    pallas_call x1, Pallas kernels, by_levels(): pl.pallas_call(functools.partial(second_kernel, plan), out_shape=jax.Shap...  2.74 us
    pallas_call x1, Pallas kernels, by_levels(): pl.pallas_call(functools.partial(first_kernel, plan), out_shape=(shares,...  2.69 us
    pallas_call x1, Pallas kernels, by_levels(): pl.pallas_call(functools.partial(pack_kernel, plan, tile_taper.shape[0]),...  2.08 us
    ppermute x1, starting transfers between devices, by_levels(): far = lax.ppermute(part[0] + other[1], axes, plan.outward())  1.28 us
  transfers between devices with their start and end apart: 4, of which 4 were waited for; matrix products, arithmetic and copies ran while one was open for 1% of the time, Pallas kernels for 1%

profile of v5, /device:TPU:0, one launch (start us, length us, event | category | flops | bytes accessed | tf_op | source)
XLA Modules:
  0.0 58.4 jit_solution(16882910197257286416)
XLA Ops:
  0.6 2.1 %pack.1 = bf16[32,104,128]{2,1,0:T(8,128)(2,1)} custom-call(s32[1,1,8]{2,1,0:T(1,128)} %code_hbm.1, f32[4]{0:T(128)} %taper_hbm.1, bf16[18,80,256]{2,1,0:T(8,128)(2,1)} %bitcast.21, f32[18,1,256]{2,1,0:T(1,128)} %bitcast.19), custom_call_target="tpu_custom_call" | custom-call | tf_op jit(solution)/shard_map/pack/pallas_call | solution.py:389
  2.7 0.0 copy-start.1
  2.7 7.3 %all-to-all-start = ((bf16[32,104,128]{2,1,0:T(8,128)(2,1)}), bf16[32,104,128]{2,1,0:T(8,128)(2,1)S(1)}, u32[]{:S(2)}, u32[]{:S(2)}) async-start(bf16[32,104,128]{2,1,0:T(8,128)(2,1)} %pack.1), calls=%async_computation | async-start | bytes 1703936 | tf_op jit(solution)/shard_map/all_to_all | solution.py:405
  10.1 0.0 copy-done.1
  10.1 0.9 %maps.1.lt_ref = bf16[9,256,256]{2,1,0:T(8,128)(2,1)S(1)} custom-call(f32[63,63]{1,0:T(8,128)S(1)} %copy-done.1), custom_call_target="tpu_custom_call" | custom-call | flops 200000000 | bytes 2000000 | tf_op jit(solution)/shard_map/maps/pallas_call | solution.py:412
  10.9 0.7 %dynamic-slice_bitcast_fusion.info_ref = s32[8]{0:T(128)S(1)} fusion(s32[32,8]{1,0:T(8,128)} %constant.16.clone, s32[]{:T(128)S(6)} %select_n.3), kind=kLoop, calls=%fused_computation.2 | loop fusion | bytes 68 | tf_op jit(solution)/shard_map/squeeze | solution.py:407
  11.6 20.4 %all-to-all-done.got_ref = bf16[32,104,128]{2,1,0:T(8,128)(2,1)S(1)} async-done(((bf16[32,104,128]{2,1,0:T(8,128)(2,1)}), bf16[32,104,128]{2,1,0:T(8,128)(2,1)S(1)}, u32[]{:S(2)}, u32[]{:S(2)}) %all-to-all-start) | async-done | bytes 852000 | tf_op jit(solution)/shard_map/all_to_all | solution.py:405
  32.1 2.7 %first.1 = (f32[2,4,8,256]{3,2,1,0:T(8,128)S(1)}, f32[2,32,256]{2,1,0:T(8,128)S(1)}, f32[8,32,256]{2,1,0:T(8,128)S(1)}) custom-call(s32[8]{0:T(128)S(1)} %dynamic-slice_bitcast_fusion.info_ref, bf16[32,104,128]{2,1,0:T(8,128)(2,1)S(1)} %all-to-all-done.got_ref, bf16[9,256,256]{2,1,0:T(8,128)(2,1)S(1)} %maps.1.lt_ref), custom_call_target="tpu_custom_call" | custom-call | tf_op jit(solution)/shard_map/first/pallas_call | solution.py:423
  34.8 0.1 collective-permute-start
  34.8 1.2 %collective-permute-done.other_ref = f32[2,32,256]{2,1,0:T(8,128)S(1)} collective-permute-done((f32[2,32,256]{2,1,0:T(8,128)S(1)}, f32[2,32,256]{2,1,0:T(8,128)S(1)}, u32[]{:S(2)}, u32[]{:S(2)}) %collective-permute-start) | collective-permute-done | bytes 65568 | tf_op jit(solution)/shard_map/ppermute | solution.py:434
  36.1 1.3 %collective-permute-start.1 = (f32[32,256]{1,0:T(8,128)S(1)}, f32[32,256]{1,0:T(8,128)S(1)}, u32[]{:S(2)}, u32[]{:S(2)}) collective-permute-start(f32[32,256]{1,0:T(8,128)S(1)} %fusion), channel_id=1, source_target_pairs={{2,0},{1,3},{6,2},{3,7},{4,6},{7,5},{12,4},{5,13},{14,12},{13,15},... | collective-permute-start | bytes 98312 | tf_op jit(solution)/shard_map/ppermute | solution.py:435
  37.4 4.5 %collective-permute-done.1.far_ref = f32[32,256]{1,0:T(8,128)S(1)} collective-permute-done((f32[32,256]{1,0:T(8,128)S(1)}, f32[32,256]{1,0:T(8,128)S(1)}, u32[]{:S(2)}, u32[]{:S(2)}) %collective-permute-start.1) | collective-permute-done | bytes 32800 | tf_op jit(solution)/shard_map/ppermute | solution.py:435
  41.9 0.0 collective-permute-start.2
  41.9 1.2 %collective-permute-done.2.far_other_ref = f32[32,256]{1,0:T(8,128)S(1)} collective-permute-done((f32[32,256]{1,0:T(8,128)S(1)}, f32[32,256]{1,0:T(8,128)S(1)}, u32[]{:S(2)}, u32[]{:S(2)}) %collective-permute-start.2) | collective-permute-done | bytes 32800 | tf_op jit(solution)/shard_map/ppermute | solution.py:436
  43.1 0.0 copy-start
  43.1 2.7 %second.1 = f32[32,8,128]{2,1,0:T(8,128)S(1)} custom-call(s32[8]{0:T(128)S(1)} %dynamic-slice_bitcast_fusion.info_ref, bf16[32,104,128]{2,1,0:T(8,128)(2,1)S(1)} %all-to-all-done.got_ref, bf16[9,256,256]{2,1,0:T(8,128)(2,1)S(1)} %maps.1.lt_ref, f32[2,32,256]{2,1,0:T(8,128)S(1)} %get-tuple-element.7.b_ref, f32[8,32,256]{2,1,0:T(8,128)S(1)} %get-tuple-element.8.wide_ref, ...), custom_call_target="tpu_custom_call" | custom-call | tf_op jit(solution)/shard_map/second/pallas_call | solution.py:437
  45.8 11.6 %all_to_all.10.got_ref = f32[32,8,128]{2,1,0:T(8,128)S(1)} all-to-all(f32[32,8,128]{2,1,0:T(8,128)S(1)} %second.1), channel_id=1, replica_groups=mesh['band'=4,'tile'=8] {'band','tile'}, dimensions={0} | all-to-all | bytes 262144 | tf_op jit(solution)/shard_map/all_to_all | solution.py:446
  57.5 0.0 copy-done
  57.5 0.9 %last.1 = (f32[18,1,256]{2,1,0:T(1,128)}, f32[18,1,256]{2,1,0:T(1,128)}) custom-call(f32[18,1,256]{2,1,0:T(1,128)S(1)} %bitcast.20, f32[32,8,128]{2,1,0:T(8,128)S(1)} %all_to_all.10.got_ref), custom_call_target="tpu_custom_call" | custom-call | tf_op jit(solution)/shard_map/last/pallas_call | solution.py:447
  (1 shorter events, 0.0 us)
Async XLA Ops:
  2.7 7.4 %copy-start.1 = (f32[63,63]{1,0:T(8,128)S(1)}, f32[63,63]{1,0:T(8,128)}, u32[]{:S(2)}) copy-start(f32[63,63]{1,0:T(8,128)} %kernel_ref.1) | copy-start | bytes 47632
  2.7 29.3 %all-to-all-start = ((bf16[32,104,128]{2,1,0:T(8,128)(2,1)}), bf16[32,104,128]{2,1,0:T(8,128)(2,1)S(1)}, u32[]{:S(2)}, u32[]{:S(2)}) async-start(bf16[32,104,128]{2,1,0:T(8,128)(2,1)} %pack.1), calls=%async_computation | async-start | bytes 1703936 | tf_op jit(solution)/shard_map/all_to_all | solution.py:405
  34.8 1.3 %collective-permute-start = (f32[2,32,256]{2,1,0:T(8,128)S(1)}, f32[2,32,256]{2,1,0:T(8,128)S(1)}, u32[]{:S(2)}, u32[]{:S(2)}) collective-permute-start(f32[2,32,256]{2,1,0:T(8,128)S(1)} %bitcast.17), channel_id=1, source_target_pairs={{0,1},{1,0},{2,3},{3,2},{4,5},{5,4},{6,7},{7,6},{8,9},{9,8},{10,11... | collective-permute-start | bytes 196616 | tf_op jit(solution)/shard_map/ppermute | solution.py:434
  36.1 5.8 %collective-permute-start.1 = (f32[32,256]{1,0:T(8,128)S(1)}, f32[32,256]{1,0:T(8,128)S(1)}, u32[]{:S(2)}, u32[]{:S(2)}) collective-permute-start(f32[32,256]{1,0:T(8,128)S(1)} %fusion), channel_id=1, source_target_pairs={{2,0},{1,3},{6,2},{3,7},{4,6},{7,5},{12,4},{5,13},{14,12},{13,15},... | collective-permute-start | bytes 98312 | tf_op jit(solution)/shard_map/ppermute | solution.py:435
  41.9 1.2 %collective-permute-start.2 = (f32[32,256]{1,0:T(8,128)S(1)}, f32[32,256]{1,0:T(8,128)S(1)}, u32[]{:S(2)}, u32[]{:S(2)}) collective-permute-start(f32[32,256]{1,0:T(8,128)S(1)} %collective-permute-done.1.far_ref), channel_id=1, source_target_pairs={{0,1},{1,0},{2,3},{3,2},{4,5},{5,4},{6,7},{7,6},{8,9},{9,8},{10,11... | collective-permute-start | bytes 98312 | tf_op jit(solution)/shard_map/ppermute | solution.py:436
  43.1 14.4 %copy-start = (f32[1,1,18,256]{3,1,2,0:T(1,128)S(1)}, f32[1,1,18,256]{3,1,2,0:T(1,128)}, u32[]{:S(2)}) copy-start(f32[1,1,18,256]{3,1,2,0:T(1,128)} %param.7) | copy-start | bytes 55300

commit v6 on v5

--- a/solution.py
+++ b/solution.py
@@ -70,15 +70,17 @@
         out = np.zeros((self.count, 8), np.int32)
         for device, k, core, low in self.owners():
             last = k == self.depth - 1
+            joined = (int(not last), int(k > 0))
             out[device, :5] = (self.low_rows(k), core, int(core == 0), int(core == 1 and last), low)
+            out[device, 5:7] = (joined[core], joined[1 - core])
         return out
 
     def outward(self):
         pairs = []
         for group in range(self.groups):
-            for k in range(1, self.depth):
-                pairs.append((self.device(group, k, 0), self.device(group, k - 1, 0)))
-                pairs.append((self.device(group, k - 1, 1), self.device(group, k, 1)))
+            for k in range(self.depth):
+                pairs.append((self.device(group, k, 0), self.device(group, (k - 1) % self.depth, 0)))
+                pairs.append((self.device(group, k, 1), self.device(group, (k + 1) % self.depth, 1)))
         return pairs
 
 
@@ -116,7 +118,6 @@
         for c in range(tapers):
             weight = jnp.where(code == c + 1, taper_ref[c], weight)
         weights = jnp.where(lane == k, weight, weights)
-    weights = weights / jnp.float32(plan.members - 1)
     high, middle, _ = in_three(weights)
     here = 0
     copies = []
@@ -212,15 +213,17 @@
             v = jnp.where(is_low, v_low[:, lanes], v_high[:, lanes])
             w_ref[tile * rows : (tile + 1) * rows, lanes] = (block(tile, half) * v).astype(jnp.bfloat16)
 
-    low_share = jnp.where(is_low, jnp.float32(1), jnp.float32(0))
-    high_share = jnp.where(is_low | (place >= plan.rows), jnp.float32(0), jnp.float32(1))
+    scale = jnp.float32(1.0 / (plan.members - 1))
+    low_share = jnp.where(is_low, scale, jnp.float32(0))
+    high_share = jnp.where(is_low | (place >= plan.rows), jnp.float32(0), scale)
+    low_end = min(-(-plan.low_rows(0) // GRAIN) * GRAIN, rows)
     sums = {}
 
     def finish(tile, spread):
         for half, lanes in enumerate(sides):
             product = block(tile, half) * spread[:, lanes]
-            for level, share in enumerate((low_share, high_share)):
-                sums[tile, level, half] = jnp.sum(product * share, axis=0, keepdims=True)
+            sums[tile, 0, half] = jnp.sum(product[:low_end] * low_share[:low_end], axis=0, keepdims=True)
+            sums[tile, 1, half] = jnp.sum(product * high_share, axis=0, keepdims=True)
 
     touched = set()
     steps = sorted(ALL_STEPS, key=lambda step: (step[0] == 0, step == (0, 0)))
@@ -240,7 +243,7 @@
                     at = ((band - first) * lons + l) * rows
                     term = y[at : at + rows]
                     if k == 0:
-                        finish(tile, s_ref[tile] + term * jnp.float32(1.0 / (plan.members - 1)))
+                        finish(tile, s_ref[tile] + term)
                         continue
                     term = term * wide_ref[k - 1, tile : tile + 1, :]
                     if tile in touched:
@@ -268,8 +271,8 @@
 
 def second_kernel(plan, info_ref, got_ref, lt_ref, b_ref, wide_ref, own_ref, other_ref, far_ref, far_other_ref,
                   out_ref, v_ref, w_ref, s_ref, p_ref):
-    mine = (own_ref[0] + other_ref[1]) + far_other_ref[...]
-    rest = (own_ref[1] + other_ref[0]) + far_ref[...]
+    mine = (own_ref[0] + other_ref[1]) + jnp.where(info_ref[6] > 0, far_other_ref[...], 0.0)
+    rest = (own_ref[1] + other_ref[0]) + jnp.where(info_ref[5] > 0, far_ref[...], 0.0)
     first_core = info_ref[1] == 0
     images = (jnp.where(first_core, mine, rest), jnp.where(first_core, rest, mine))
     lane = lax.broadcasted_iota(jnp.int32, (1, LANES), 1)

time: 58.7 us -> 56.7 us (0.966)
  waiting for transfers between devices: 27.4 us -> 25.4 us
    ppermute x1, waiting for transfers between devices: 4.51 us -> 2.52 us  [by_levels(): far = lax.ppermute(part[0] + other[1], axes, plan.outward())]
  transfers between devices with their start and end apart: 4 -> 4, of which waited for: 4 -> 4; matrix products, arithmetic and copies ran while one was open for 1% -> 1% of each run, Pallas kernels for 1% -> 2%
where the time goes in v6:
time: 56.7 us; the launch traced here: 56.4 us
  waiting for transfers between devices  25.4 us (45%)
  blocking collectives  11.6 us (20%)
  Pallas kernels  9.18 us (16%)
  starting transfers between devices  8.8 us (16%)
  local copies, waits for them, and re-layouts  0.71 us (1%)
  between operations  0.7 us (1%)
    all_to_all x1, waiting for transfers between devices, by_levels(): got = lax.all_to_all(sent, axes, 0, 0)  20.4 us
    all_to_all x1, blocking collectives, by_levels(): home = lax.all_to_all(back, axes, 0, 0)  11.6 us
    all_to_all x1, starting transfers between devices, by_levels(): got = lax.all_to_all(sent, axes, 0, 0)  7.33 us
    pallas_call x1, Pallas kernels, by_levels(): pl.pallas_call(functools.partial(second_kernel, plan), out_shape=jax.Shap...  2.7 us
    pallas_call x1, Pallas kernels, by_levels(): pl.pallas_call(functools.partial(first_kernel, plan), out_shape=(shares,...  2.64 us
    ppermute x1, waiting for transfers between devices, by_levels(): far = lax.ppermute(part[0] + other[1], axes, plan.outward())  2.52 us
    pallas_call x1, Pallas kernels, by_levels(): pl.pallas_call(functools.partial(pack_kernel, plan, tile_taper.shape[0]),...  2.08 us
    ppermute x1, starting transfers between devices, by_levels(): far = lax.ppermute(part[0] + other[1], axes, plan.outward())  1.39 us
  transfers between devices with their start and end apart: 4, of which 4 were waited for; matrix products, arithmetic and copies ran while one was open for 1% of the time, Pallas kernels for 2%

profile of v6, /device:TPU:0, one launch (start us, length us, event | category | flops | bytes accessed | tf_op | source)
XLA Modules:
  0.0 56.4 jit_solution(4913366420221399563)
XLA Ops:
  0.6 2.1 %pack.1 = bf16[32,104,128]{2,1,0:T(8,128)(2,1)} custom-call(s32[1,1,8]{2,1,0:T(1,128)} %code_hbm.1, f32[4]{0:T(128)} %taper_hbm.1, bf16[18,80,256]{2,1,0:T(8,128)(2,1)} %bitcast.21, f32[18,1,256]{2,1,0:T(1,128)} %bitcast.19), custom_call_target="tpu_custom_call" | custom-call | tf_op jit(solution)/shard_map/pack/pallas_call | solution.py:392
  2.7 0.0 copy-start.1
  2.7 7.3 %all-to-all-start = ((bf16[32,104,128]{2,1,0:T(8,128)(2,1)}), bf16[32,104,128]{2,1,0:T(8,128)(2,1)S(1)}, u32[]{:S(2)}, u32[]{:S(2)}) async-start(bf16[32,104,128]{2,1,0:T(8,128)(2,1)} %pack.1), calls=%async_computation | async-start | bytes 1703936 | tf_op jit(solution)/shard_map/all_to_all | solution.py:408
  10.1 0.0 copy-done.1
  10.1 0.9 %maps.1.lt_ref = bf16[9,256,256]{2,1,0:T(8,128)(2,1)S(1)} custom-call(f32[63,63]{1,0:T(8,128)S(1)} %copy-done.1), custom_call_target="tpu_custom_call" | custom-call | flops 200000000 | bytes 2000000 | tf_op jit(solution)/shard_map/maps/pallas_call | solution.py:415
  10.9 0.7 %dynamic-slice_bitcast_fusion.info_ref = s32[8]{0:T(128)S(1)} fusion(s32[32,8]{1,0:T(8,128)} %constant.16.clone, s32[]{:T(128)S(6)} %select_n.3), kind=kLoop, calls=%fused_computation.2 | loop fusion | bytes 68 | tf_op jit(solution)/shard_map/squeeze | solution.py:410
  11.6 20.4 %all-to-all-done.got_ref = bf16[32,104,128]{2,1,0:T(8,128)(2,1)S(1)} async-done(((bf16[32,104,128]{2,1,0:T(8,128)(2,1)}), bf16[32,104,128]{2,1,0:T(8,128)(2,1)S(1)}, u32[]{:S(2)}, u32[]{:S(2)}) %all-to-all-start) | async-done | bytes 852000 | tf_op jit(solution)/shard_map/all_to_all | solution.py:408
  32.1 2.6 %first.1 = (f32[2,4,8,256]{3,2,1,0:T(8,128)S(1)}, f32[2,32,256]{2,1,0:T(8,128)S(1)}, f32[8,32,256]{2,1,0:T(8,128)S(1)}) custom-call(s32[8]{0:T(128)S(1)} %dynamic-slice_bitcast_fusion.info_ref, bf16[32,104,128]{2,1,0:T(8,128)(2,1)S(1)} %all-to-all-done.got_ref, bf16[9,256,256]{2,1,0:T(8,128)(2,1)S(1)} %maps.1.lt_ref), custom_call_target="tpu_custom_call" | custom-call | tf_op jit(solution)/shard_map/first/pallas_call | solution.py:426
  34.7 0.1 collective-permute-start
  34.8 1.2 %collective-permute-done.other_ref = f32[2,32,256]{2,1,0:T(8,128)S(1)} collective-permute-done((f32[2,32,256]{2,1,0:T(8,128)S(1)}, f32[2,32,256]{2,1,0:T(8,128)S(1)}, u32[]{:S(2)}, u32[]{:S(2)}) %collective-permute-start) | collective-permute-done | bytes 65568 | tf_op jit(solution)/shard_map/ppermute | solution.py:437
  36.0 1.4 %collective-permute-start.1 = (f32[32,256]{1,0:T(8,128)S(1)}, f32[32,256]{1,0:T(8,128)S(1)}, u32[]{:S(2)}, u32[]{:S(2)}) collective-permute-start(f32[32,256]{1,0:T(8,128)S(1)} %fusion), channel_id=1, source_target_pairs={{0,8},{1,3},{2,0},{3,7},{6,2},{7,5},{4,6},{5,13},{12,4},{13,15},{1... | collective-permute-start | bytes 98312 | tf_op jit(solution)/shard_map/ppermute | solution.py:438
  37.4 2.5 %collective-permute-done.1.far_ref = f32[32,256]{1,0:T(8,128)S(1)} collective-permute-done((f32[32,256]{1,0:T(8,128)S(1)}, f32[32,256]{1,0:T(8,128)S(1)}, u32[]{:S(2)}, u32[]{:S(2)}) %collective-permute-start.1) | collective-permute-done | bytes 32800 | tf_op jit(solution)/shard_map/ppermute | solution.py:438
  40.0 0.0 collective-permute-start.2
  40.0 1.2 %collective-permute-done.2.far_other_ref = f32[32,256]{1,0:T(8,128)S(1)} collective-permute-done((f32[32,256]{1,0:T(8,128)S(1)}, f32[32,256]{1,0:T(8,128)S(1)}, u32[]{:S(2)}, u32[]{:S(2)}) %collective-permute-start.2) | collective-permute-done | bytes 32800 | tf_op jit(solution)/shard_map/ppermute | solution.py:439
  41.2 0.0 copy-start
  41.2 2.7 %second.1 = f32[32,8,128]{2,1,0:T(8,128)S(1)} custom-call(s32[8]{0:T(128)S(1)} %dynamic-slice_bitcast_fusion.info_ref, bf16[32,104,128]{2,1,0:T(8,128)(2,1)S(1)} %all-to-all-done.got_ref, bf16[9,256,256]{2,1,0:T(8,128)(2,1)S(1)} %maps.1.lt_ref, f32[2,32,256]{2,1,0:T(8,128)S(1)} %get-tuple-element.7.b_ref, f32[8,32,256]{2,1,0:T(8,128)S(1)} %get-tuple-element.8.wide_ref, ...), custom_call_target="tpu_custom_call" | custom-call | tf_op jit(solution)/shard_map/second/pallas_call | solution.py:440
  43.9 11.6 %all_to_all.10.got_ref = f32[32,8,128]{2,1,0:T(8,128)S(1)} all-to-all(f32[32,8,128]{2,1,0:T(8,128)S(1)} %second.1), channel_id=1, replica_groups=mesh['band'=4,'tile'=8] {'band','tile'}, dimensions={0} | all-to-all | bytes 262144 | tf_op jit(solution)/shard_map/all_to_all | solution.py:449
  55.5 0.0 copy-done
  55.5 0.9 %last.1 = (f32[18,1,256]{2,1,0:T(1,128)}, f32[18,1,256]{2,1,0:T(1,128)}) custom-call(f32[18,1,256]{2,1,0:T(1,128)S(1)} %bitcast.20, f32[32,8,128]{2,1,0:T(8,128)S(1)} %all_to_all.10.got_ref), custom_call_target="tpu_custom_call" | custom-call | tf_op jit(solution)/shard_map/last/pallas_call | solution.py:450
  (1 shorter events, 0.0 us)
Async XLA Ops:
  2.7 7.4 %copy-start.1 = (f32[63,63]{1,0:T(8,128)S(1)}, f32[63,63]{1,0:T(8,128)}, u32[]{:S(2)}) copy-start(f32[63,63]{1,0:T(8,128)} %kernel_ref.1) | copy-start | bytes 47632
  2.7 29.3 %all-to-all-start = ((bf16[32,104,128]{2,1,0:T(8,128)(2,1)}), bf16[32,104,128]{2,1,0:T(8,128)(2,1)S(1)}, u32[]{:S(2)}, u32[]{:S(2)}) async-start(bf16[32,104,128]{2,1,0:T(8,128)(2,1)} %pack.1), calls=%async_computation | async-start | bytes 1703936 | tf_op jit(solution)/shard_map/all_to_all | solution.py:408
  34.7 1.3 %collective-permute-start = (f32[2,32,256]{2,1,0:T(8,128)S(1)}, f32[2,32,256]{2,1,0:T(8,128)S(1)}, u32[]{:S(2)}, u32[]{:S(2)}) collective-permute-start(f32[2,32,256]{2,1,0:T(8,128)S(1)} %bitcast.17), channel_id=1, source_target_pairs={{0,1},{1,0},{2,3},{3,2},{4,5},{5,4},{6,7},{7,6},{8,9},{9,8},{10,11... | collective-permute-start | bytes 196616 | tf_op jit(solution)/shard_map/ppermute | solution.py:437
  36.0 3.9 %collective-permute-start.1 = (f32[32,256]{1,0:T(8,128)S(1)}, f32[32,256]{1,0:T(8,128)S(1)}, u32[]{:S(2)}, u32[]{:S(2)}) collective-permute-start(f32[32,256]{1,0:T(8,128)S(1)} %fusion), channel_id=1, source_target_pairs={{0,8},{1,3},{2,0},{3,7},{6,2},{7,5},{4,6},{5,13},{12,4},{13,15},{1... | collective-permute-start | bytes 98312 | tf_op jit(solution)/shard_map/ppermute | solution.py:438
  40.0 1.2 %collective-permute-start.2 = (f32[32,256]{1,0:T(8,128)S(1)}, f32[32,256]{1,0:T(8,128)S(1)}, u32[]{:S(2)}, u32[]{:S(2)}) collective-permute-start(f32[32,256]{1,0:T(8,128)S(1)} %collective-permute-done.1.far_ref), channel_id=1, source_target_pairs={{0,1},{1,0},{2,3},{3,2},{4,5},{5,4},{6,7},{7,6},{8,9},{9,8},{10,11... | collective-permute-start | bytes 98312 | tf_op jit(solution)/shard_map/ppermute | solution.py:439
  41.2 14.3 %copy-start = (f32[1,1,18,256]{3,1,2,0:T(1,128)S(1)}, f32[1,1,18,256]{3,1,2,0:T(1,128)}, u32[]{:S(2)}) copy-start(f32[1,1,18,256]{3,1,2,0:T(1,128)} %param.7) | copy-start | bytes 55300

commit v7 on v6

--- a/solution.py
+++ b/solution.py
@@ -435,8 +435,9 @@
     part = part.reshape(2, n, columns)
     swap = [(i, i ^ 1) for i in range(plan.lons)]
     other = lax.ppermute(part, "tile", swap)
-    far = lax.ppermute(part[0] + other[1], axes, plan.outward())
-    far_other = lax.ppermute(far, "tile", swap)
+    outward = plan.outward()
+    far = lax.ppermute(part[0] + other[1], axes, outward)
+    far_other = lax.ppermute(part[1] + other[0], axes, [(target, source) for source, target in outward])
     back = pl.pallas_call(
         functools.partial(second_kernel, plan),
         out_shape=jax.ShapeDtypeStruct((n, 8, LANES), f32),

time: 56.7 us -> 56.2 us (level)
  blocking collectives: 11.6 us -> 10.7 us
  starting transfers between devices: 8.8 us -> 9.48 us
    all_to_all x1, blocking collectives: 11.6 us -> 10.7 us  [by_levels(): home = lax.all_to_all(back, axes, 0, 0)]
    ppermute x2, starting transfers between devices: 1.39 us -> 2.08 us  [the longest x1 1.53 us: by_levels(): lax.ppermute(part[1] + other[0], axes, [(target, source) for source, targ...]
where the time goes in v7:
time: 56.2 us; the launch traced here: 55.9 us
  waiting for transfers between devices  25 us (44%)
  blocking collectives  10.7 us (19%)
  starting transfers between devices  9.48 us (17%)
  Pallas kernels  9.19 us (16%)
  local copies, waits for them, and re-layouts  0.71 us (1%)
  between operations  0.71 us (1%)
    all_to_all x1, waiting for transfers between devices, by_levels(): got = lax.all_to_all(sent, axes, 0, 0)  20.4 us
    all_to_all x1, blocking collectives, by_levels(): home = lax.all_to_all(back, axes, 0, 0)  10.7 us
    all_to_all x1, starting transfers between devices, by_levels(): got = lax.all_to_all(sent, axes, 0, 0)  7.33 us
    pallas_call x1, Pallas kernels, by_levels(): pl.pallas_call(functools.partial(second_kernel, plan), out_shape=jax.Shap...  2.7 us
    pallas_call x1, Pallas kernels, by_levels(): pl.pallas_call(functools.partial(first_kernel, plan), out_shape=(shares,...  2.64 us
    pallas_call x1, Pallas kernels, by_levels(): pl.pallas_call(functools.partial(pack_kernel, plan, tile_taper.shape[0]),...  2.1 us
    ppermute x1, waiting for transfers between devices, by_levels(): lax.ppermute(part[1] + other[0], axes, [(target, source) for source, targ...  1.93 us
    ppermute x1, starting transfers between devices, by_levels(): lax.ppermute(part[1] + other[0], axes, [(target, source) for source, targ...  1.53 us
  transfers between devices with their start and end apart: 4, of which 4 were waited for; matrix products, arithmetic and copies ran while one was open for 1% of the time, Pallas kernels for 2%

profile of v7, /device:TPU:0, one launch (start us, length us, event | category | flops | bytes accessed | tf_op | source)
XLA Modules:
  0.0 55.9 jit_solution(3372375337182645434)
XLA Ops:
  0.6 2.1 %pack.1 = bf16[32,104,128]{2,1,0:T(8,128)(2,1)} custom-call(s32[1,1,8]{2,1,0:T(1,128)} %code_hbm.1, f32[4]{0:T(128)} %taper_hbm.1, bf16[18,80,256]{2,1,0:T(8,128)(2,1)} %bitcast.27, f32[18,1,256]{2,1,0:T(1,128)} %bitcast.25), custom_call_target="tpu_custom_call" | custom-call | tf_op jit(solution)/shard_map/pack/pallas_call | solution.py:392
  2.7 0.0 copy-start.1
  2.7 7.3 %all-to-all-start = ((bf16[32,104,128]{2,1,0:T(8,128)(2,1)}), bf16[32,104,128]{2,1,0:T(8,128)(2,1)S(1)}, u32[]{:S(2)}, u32[]{:S(2)}) async-start(bf16[32,104,128]{2,1,0:T(8,128)(2,1)} %pack.1), calls=%async_computation | async-start | bytes 1703936 | tf_op jit(solution)/shard_map/all_to_all | solution.py:408
  10.1 0.0 copy-done.1
  10.1 0.9 %maps.1.lt_ref = bf16[9,256,256]{2,1,0:T(8,128)(2,1)S(1)} custom-call(f32[63,63]{1,0:T(8,128)S(1)} %copy-done.1), custom_call_target="tpu_custom_call" | custom-call | flops 200000000 | bytes 2000000 | tf_op jit(solution)/shard_map/maps/pallas_call | solution.py:415
  11.0 0.7 %dynamic-slice_bitcast_fusion.info_ref = s32[8]{0:T(128)S(1)} fusion(s32[32,8]{1,0:T(8,128)} %constant.16.clone, s32[]{:T(128)S(6)} %select_n.3), kind=kLoop, calls=%fused_computation.4 | loop fusion | bytes 68 | tf_op jit(solution)/shard_map/squeeze | solution.py:410
  11.7 20.4 %all-to-all-done.got_ref = bf16[32,104,128]{2,1,0:T(8,128)(2,1)S(1)} async-done(((bf16[32,104,128]{2,1,0:T(8,128)(2,1)}), bf16[32,104,128]{2,1,0:T(8,128)(2,1)S(1)}, u32[]{:S(2)}, u32[]{:S(2)}) %all-to-all-start) | async-done | bytes 852000 | tf_op jit(solution)/shard_map/all_to_all | solution.py:408
  32.1 2.6 %first.1 = (f32[2,4,8,256]{3,2,1,0:T(8,128)S(1)}, f32[2,32,256]{2,1,0:T(8,128)S(1)}, f32[8,32,256]{2,1,0:T(8,128)S(1)}) custom-call(s32[8]{0:T(128)S(1)} %dynamic-slice_bitcast_fusion.info_ref, bf16[32,104,128]{2,1,0:T(8,128)(2,1)S(1)} %all-to-all-done.got_ref, bf16[9,256,256]{2,1,0:T(8,128)(2,1)S(1)} %maps.1.lt_ref), custom_call_target="tpu_custom_call" | custom-call | tf_op jit(solution)/shard_map/first/pallas_call | solution.py:426
  34.7 0.1 collective-permute-start
  34.8 1.2 %collective-permute-done.other_ref = f32[2,32,256]{2,1,0:T(8,128)S(1)} collective-permute-done((f32[2,32,256]{2,1,0:T(8,128)S(1)}, f32[2,32,256]{2,1,0:T(8,128)S(1)}, u32[]{:S(2)}, u32[]{:S(2)}) %collective-permute-start) | collective-permute-done | bytes 65568 | tf_op jit(solution)/shard_map/ppermute | solution.py:437
  36.1 1.5 %collective-permute-start.2 = (f32[32,256]{1,0:T(8,128)S(1)}, f32[32,256]{1,0:T(8,128)S(1)}, u32[]{:S(2)}, u32[]{:S(2)}) collective-permute-start(f32[32,256]{1,0:T(8,128)S(1)} %get-tuple-element.14), channel_id=1, source_target_pairs={{8,0},{3,1},{0,2},{7,3},{2,6},{5,7},{6,4},{13,5},{4,12},{15,13},{1... | collective-permute-start | bytes 98312 | tf_op jit(solution)/shard_map/ppermute | solution.py:440
  37.6 0.5 collective-permute-start.1
  38.1 1.9 %collective-permute-done.2.far_other_ref = f32[32,256]{1,0:T(8,128)S(1)} collective-permute-done((f32[32,256]{1,0:T(8,128)S(1)}, f32[32,256]{1,0:T(8,128)S(1)}, u32[]{:S(2)}, u32[]{:S(2)}) %collective-permute-start.2) | collective-permute-done | bytes 32800 | tf_op jit(solution)/shard_map/ppermute | solution.py:440
  40.1 1.4 %collective-permute-done.1.far_ref = f32[32,256]{1,0:T(8,128)S(1)} collective-permute-done((f32[32,256]{1,0:T(8,128)S(1)}, f32[32,256]{1,0:T(8,128)S(1)}, u32[]{:S(2)}, u32[]{:S(2)}) %collective-permute-start.1) | collective-permute-done | bytes 32800 | tf_op jit(solution)/shard_map/ppermute | solution.py:439
  41.5 0.0 copy-start
  41.5 2.7 %second.1 = f32[32,8,128]{2,1,0:T(8,128)S(1)} custom-call(s32[8]{0:T(128)S(1)} %dynamic-slice_bitcast_fusion.info_ref, bf16[32,104,128]{2,1,0:T(8,128)(2,1)S(1)} %all-to-all-done.got_ref, bf16[9,256,256]{2,1,0:T(8,128)(2,1)S(1)} %maps.1.lt_ref, f32[2,32,256]{2,1,0:T(8,128)S(1)} %get-tuple-element.7.b_ref, f32[8,32,256]{2,1,0:T(8,128)S(1)} %get-tuple-element.8.wide_ref, ...), custom_call_target="tpu_custom_call" | custom-call | tf_op jit(solution)/shard_map/second/pallas_call | solution.py:441
  44.2 10.7 %all_to_all.10.got_ref = f32[32,8,128]{2,1,0:T(8,128)S(1)} all-to-all(f32[32,8,128]{2,1,0:T(8,128)S(1)} %second.1), channel_id=1, replica_groups=mesh['band'=4,'tile'=8] {'band','tile'}, dimensions={0} | all-to-all | bytes 262144 | tf_op jit(solution)/shard_map/all_to_all | solution.py:450
  54.9 0.0 copy-done
  54.9 0.9 %last.1 = (f32[18,1,256]{2,1,0:T(1,128)}, f32[18,1,256]{2,1,0:T(1,128)}) custom-call(f32[18,1,256]{2,1,0:T(1,128)S(1)} %bitcast.26, f32[32,8,128]{2,1,0:T(8,128)S(1)} %all_to_all.10.got_ref), custom_call_target="tpu_custom_call" | custom-call | tf_op jit(solution)/shard_map/last/pallas_call | solution.py:451
  (1 shorter events, 0.0 us)
Async XLA Ops:
  2.7 7.4 %copy-start.1 = (f32[63,63]{1,0:T(8,128)S(1)}, f32[63,63]{1,0:T(8,128)}, u32[]{:S(2)}) copy-start(f32[63,63]{1,0:T(8,128)} %kernel_ref.1) | copy-start | bytes 47632
  2.7 29.3 %all-to-all-start = ((bf16[32,104,128]{2,1,0:T(8,128)(2,1)}), bf16[32,104,128]{2,1,0:T(8,128)(2,1)S(1)}, u32[]{:S(2)}, u32[]{:S(2)}) async-start(bf16[32,104,128]{2,1,0:T(8,128)(2,1)} %pack.1), calls=%async_computation | async-start | bytes 1703936 | tf_op jit(solution)/shard_map/all_to_all | solution.py:408
  34.7 1.3 %collective-permute-start = (f32[2,32,256]{2,1,0:T(8,128)S(1)}, f32[2,32,256]{2,1,0:T(8,128)S(1)}, u32[]{:S(2)}, u32[]{:S(2)}) collective-permute-start(f32[2,32,256]{2,1,0:T(8,128)S(1)} %bitcast.23), channel_id=1, source_target_pairs={{0,1},{1,0},{2,3},{3,2},{4,5},{5,4},{6,7},{7,6},{8,9},{9,8},{10,11... | collective-permute-start | bytes 196616 | tf_op jit(solution)/shard_map/ppermute | solution.py:437
  36.1 4.0 %collective-permute-start.2 = (f32[32,256]{1,0:T(8,128)S(1)}, f32[32,256]{1,0:T(8,128)S(1)}, u32[]{:S(2)}, u32[]{:S(2)}) collective-permute-start(f32[32,256]{1,0:T(8,128)S(1)} %get-tuple-element.14), channel_id=1, source_target_pairs={{8,0},{3,1},{0,2},{7,3},{2,6},{5,7},{6,4},{13,5},{4,12},{15,13},{1... | collective-permute-start | bytes 98312 | tf_op jit(solution)/shard_map/ppermute | solution.py:440
  37.6 3.9 %collective-permute-start.1 = (f32[32,256]{1,0:T(8,128)S(1)}, f32[32,256]{1,0:T(8,128)S(1)}, u32[]{:S(2)}, u32[]{:S(2)}) collective-permute-start(f32[32,256]{1,0:T(8,128)S(1)} %get-tuple-element.15), channel_id=1, source_target_pairs={{0,8},{1,3},{2,0},{3,7},{6,2},{7,5},{4,6},{5,13},{12,4},{13,15},{1... | collective-permute-start | bytes 98312 | tf_op jit(solution)/shard_map/ppermute | solution.py:439
  41.5 13.4 %copy-start = (f32[1,1,18,256]{3,1,2,0:T(1,128)S(1)}, f32[1,1,18,256]{3,1,2,0:T(1,128)}, u32[]{:S(2)}) copy-start(f32[1,1,18,256]{3,1,2,0:T(1,128)} %param.7) | copy-start | bytes 55300

commit v8 on v7

--- a/solution.py
+++ b/solution.py
@@ -92,7 +92,7 @@
 
 
 def pack_kernel(plan, tapers, code_hbm, taper_hbm, a_ref, f_hbm, out_ref,
-                code_ref, taper_ref, f_ref, near_ref, wide_ref, sent_ref, small_sem, in_sem, out_sem):
+                code_ref, taper_ref, f_ref, near_ref, sent_ref, small_sem, in_sem, out_sem):
     share, size = plan.depth + 1, plan.count // plan.groups
 
     def fetch(group):
@@ -119,20 +119,18 @@
             weight = jnp.where(code == c + 1, taper_ref[c], weight)
         weights = jnp.where(lane == k, weight, weights)
     high, middle, _ = in_three(weights)
-    here = 0
     copies = []
     for device, k, core, low in plan.owners():
         if low % share == 0 and core == 0:
             fetch(low // share).wait()
-        while here < low + 2:
-            wide_ref[here * plan.members : (here + 1) * plan.members, :] = near_ref[here].astype(jnp.float32)
-            here += 1
         count, other = plan.low_rows(k), plan.rows - plan.low_rows(k)
-        start = low * plan.members + k * plan.step + core * count
-        after = (low + 1) * plan.members + core * other
+        start, after = k * plan.step + core * count, core * other
         for half in range(2):
             lanes = slice(half * LANES, (half + 1) * LANES)
-            pieces = [wide_ref[start : start + count, lanes], wide_ref[after : after + other, lanes]]
+            pieces = [
+                near_ref[low, start : start + count, lanes].astype(jnp.float32),
+                near_ref[low + 1, after : after + other, lanes].astype(jnp.float32),
+            ]
             pieces += [part[low : low + 1, lanes] for part in forcing]
             spare = plan.block - plan.rows - 3
             if spare:
@@ -398,7 +396,6 @@
                         pltpu.SMEM(tile_taper.shape, f32),
                         pltpu.VMEM(f.shape, f32),
                         pltpu.VMEM(a.shape, bf16),
-                        pltpu.VMEM((plan.levels * plan.members, columns), f32),
                         pltpu.VMEM((n, plan.height, LANES), bf16),
                         pltpu.SemaphoreType.DMA((3,)),
                         pltpu.SemaphoreType.DMA((plan.groups,)),

time: 56.2 us -> 56.2 us (level)
  no operation moved by 1% of the time
where the time goes in v8:
time: 56.2 us; the launch traced here: 55.8 us
  waiting for transfers between devices  25 us (44%)
  blocking collectives  10.7 us (19%)
  starting transfers between devices  9.48 us (17%)
  Pallas kernels  9.19 us (16%)
  local copies, waits for them, and re-layouts  0.71 us (1%)
  between operations  0.71 us (1%)
    all_to_all x1, waiting for transfers between devices, by_levels(): got = lax.all_to_all(sent, axes, 0, 0)  20.4 us
    all_to_all x1, blocking collectives, by_levels(): home = lax.all_to_all(back, axes, 0, 0)  10.7 us
    all_to_all x1, starting transfers between devices, by_levels(): got = lax.all_to_all(sent, axes, 0, 0)  7.33 us
    pallas_call x1, Pallas kernels, by_levels(): pl.pallas_call(functools.partial(second_kernel, plan), out_shape=jax.Shap...  2.7 us
    pallas_call x1, Pallas kernels, by_levels(): pl.pallas_call(functools.partial(first_kernel, plan), out_shape=(shares,...  2.64 us
    pallas_call x1, Pallas kernels, by_levels(): pl.pallas_call(functools.partial(pack_kernel, plan, tile_taper.shape[0]),...  2.09 us
    ppermute x1, waiting for transfers between devices, by_levels(): lax.ppermute(part[1] + other[0], axes, [(target, source) for source, targ...  1.94 us
    ppermute x1, starting transfers between devices, by_levels(): lax.ppermute(part[1] + other[0], axes, [(target, source) for source, targ...  1.51 us
  transfers between devices with their start and end apart: 4, of which 4 were waited for; matrix products, arithmetic and copies ran while one was open for 1% of the time, Pallas kernels for 2%

profile of v8, /device:TPU:0, one launch (start us, length us, event | category | flops | bytes accessed | tf_op | source)
XLA Modules:
  0.0 55.8 jit_solution(9299363819289036613)
XLA Ops:
  0.6 2.1 %pack.1 = bf16[32,104,128]{2,1,0:T(8,128)(2,1)} custom-call(s32[1,1,8]{2,1,0:T(1,128)} %code_hbm.1, f32[4]{0:T(128)} %taper_hbm.1, bf16[18,80,256]{2,1,0:T(8,128)(2,1)} %bitcast.27, f32[18,1,256]{2,1,0:T(1,128)} %bitcast.25), custom_call_target="tpu_custom_call" | custom-call | tf_op jit(solution)/shard_map/pack/pallas_call | solution.py:390
  2.7 0.0 copy-start.1
  2.7 7.3 %all-to-all-start = ((bf16[32,104,128]{2,1,0:T(8,128)(2,1)}), bf16[32,104,128]{2,1,0:T(8,128)(2,1)S(1)}, u32[]{:S(2)}, u32[]{:S(2)}) async-start(bf16[32,104,128]{2,1,0:T(8,128)(2,1)} %pack.1), calls=%async_computation | async-start | bytes 1703936 | tf_op jit(solution)/shard_map/all_to_all | solution.py:405
  10.1 0.0 copy-done.1
  10.1 0.8 %maps.1.lt_ref = bf16[9,256,256]{2,1,0:T(8,128)(2,1)S(1)} custom-call(f32[63,63]{1,0:T(8,128)S(1)} %copy-done.1), custom_call_target="tpu_custom_call" | custom-call | flops 200000000 | bytes 2000000 | tf_op jit(solution)/shard_map/maps/pallas_call | solution.py:412
  11.0 0.7 %dynamic-slice_bitcast_fusion.info_ref = s32[8]{0:T(128)S(1)} fusion(s32[32,8]{1,0:T(8,128)} %constant.16.clone, s32[]{:T(128)S(6)} %select_n.3), kind=kLoop, calls=%fused_computation.4 | loop fusion | bytes 68 | tf_op jit(solution)/shard_map/squeeze | solution.py:407
  11.7 20.4 %all-to-all-done.got_ref = bf16[32,104,128]{2,1,0:T(8,128)(2,1)S(1)} async-done(((bf16[32,104,128]{2,1,0:T(8,128)(2,1)}), bf16[32,104,128]{2,1,0:T(8,128)(2,1)S(1)}, u32[]{:S(2)}, u32[]{:S(2)}) %all-to-all-start) | async-done | bytes 852000 | tf_op jit(solution)/shard_map/all_to_all | solution.py:405
  32.1 2.6 %first.1 = (f32[2,4,8,256]{3,2,1,0:T(8,128)S(1)}, f32[2,32,256]{2,1,0:T(8,128)S(1)}, f32[8,32,256]{2,1,0:T(8,128)S(1)}) custom-call(s32[8]{0:T(128)S(1)} %dynamic-slice_bitcast_fusion.info_ref, bf16[32,104,128]{2,1,0:T(8,128)(2,1)S(1)} %all-to-all-done.got_ref, bf16[9,256,256]{2,1,0:T(8,128)(2,1)S(1)} %maps.1.lt_ref), custom_call_target="tpu_custom_call" | custom-call | tf_op jit(solution)/shard_map/first/pallas_call | solution.py:423
  34.7 0.1 collective-permute-start
  34.8 1.2 %collective-permute-done.other_ref = f32[2,32,256]{2,1,0:T(8,128)S(1)} collective-permute-done((f32[2,32,256]{2,1,0:T(8,128)S(1)}, f32[2,32,256]{2,1,0:T(8,128)S(1)}, u32[]{:S(2)}, u32[]{:S(2)}) %collective-permute-start) | collective-permute-done | bytes 65568 | tf_op jit(solution)/shard_map/ppermute | solution.py:434
  36.1 1.5 %collective-permute-start.2 = (f32[32,256]{1,0:T(8,128)S(1)}, f32[32,256]{1,0:T(8,128)S(1)}, u32[]{:S(2)}, u32[]{:S(2)}) collective-permute-start(f32[32,256]{1,0:T(8,128)S(1)} %get-tuple-element.14), channel_id=1, source_target_pairs={{8,0},{3,1},{0,2},{7,3},{2,6},{5,7},{6,4},{13,5},{4,12},{15,13},{1... | collective-permute-start | bytes 98312 | tf_op jit(solution)/shard_map/ppermute | solution.py:437
  37.6 0.6 %collective-permute-start.1 = (f32[32,256]{1,0:T(8,128)S(1)}, f32[32,256]{1,0:T(8,128)S(1)}, u32[]{:S(2)}, u32[]{:S(2)}) collective-permute-start(f32[32,256]{1,0:T(8,128)S(1)} %get-tuple-element.15), channel_id=1, source_target_pairs={{0,8},{1,3},{2,0},{3,7},{6,2},{7,5},{4,6},{5,13},{12,4},{13,15},{1... | collective-permute-start | bytes 98312 | tf_op jit(solution)/shard_map/ppermute | solution.py:436
  38.1 1.9 %collective-permute-done.2.far_other_ref = f32[32,256]{1,0:T(8,128)S(1)} collective-permute-done((f32[32,256]{1,0:T(8,128)S(1)}, f32[32,256]{1,0:T(8,128)S(1)}, u32[]{:S(2)}, u32[]{:S(2)}) %collective-permute-start.2) | collective-permute-done | bytes 32800 | tf_op jit(solution)/shard_map/ppermute | solution.py:437
  40.1 1.4 %collective-permute-done.1.far_ref = f32[32,256]{1,0:T(8,128)S(1)} collective-permute-done((f32[32,256]{1,0:T(8,128)S(1)}, f32[32,256]{1,0:T(8,128)S(1)}, u32[]{:S(2)}, u32[]{:S(2)}) %collective-permute-start.1) | collective-permute-done | bytes 32800 | tf_op jit(solution)/shard_map/ppermute | solution.py:436
  41.5 0.0 copy-start
  41.5 2.7 %second.1 = f32[32,8,128]{2,1,0:T(8,128)S(1)} custom-call(s32[8]{0:T(128)S(1)} %dynamic-slice_bitcast_fusion.info_ref, bf16[32,104,128]{2,1,0:T(8,128)(2,1)S(1)} %all-to-all-done.got_ref, bf16[9,256,256]{2,1,0:T(8,128)(2,1)S(1)} %maps.1.lt_ref, f32[2,32,256]{2,1,0:T(8,128)S(1)} %get-tuple-element.7.b_ref, f32[8,32,256]{2,1,0:T(8,128)S(1)} %get-tuple-element.8.wide_ref, ...), custom_call_target="tpu_custom_call" | custom-call | tf_op jit(solution)/shard_map/second/pallas_call | solution.py:438
  44.2 10.7 %all_to_all.10.got_ref = f32[32,8,128]{2,1,0:T(8,128)S(1)} all-to-all(f32[32,8,128]{2,1,0:T(8,128)S(1)} %second.1), channel_id=1, replica_groups=mesh['band'=4,'tile'=8] {'band','tile'}, dimensions={0} | all-to-all | bytes 262144 | tf_op jit(solution)/shard_map/all_to_all | solution.py:447
  54.9 0.0 copy-done
  54.9 0.9 %last.1 = (f32[18,1,256]{2,1,0:T(1,128)}, f32[18,1,256]{2,1,0:T(1,128)}) custom-call(f32[18,1,256]{2,1,0:T(1,128)S(1)} %bitcast.26, f32[32,8,128]{2,1,0:T(8,128)S(1)} %all_to_all.10.got_ref), custom_call_target="tpu_custom_call" | custom-call | tf_op jit(solution)/shard_map/last/pallas_call | solution.py:448
  (1 shorter events, 0.0 us)
Async XLA Ops:
  2.7 7.4 %copy-start.1 = (f32[63,63]{1,0:T(8,128)S(1)}, f32[63,63]{1,0:T(8,128)}, u32[]{:S(2)}) copy-start(f32[63,63]{1,0:T(8,128)} %kernel_ref.1) | copy-start | bytes 47632
  2.7 29.3 %all-to-all-start = ((bf16[32,104,128]{2,1,0:T(8,128)(2,1)}), bf16[32,104,128]{2,1,0:T(8,128)(2,1)S(1)}, u32[]{:S(2)}, u32[]{:S(2)}) async-start(bf16[32,104,128]{2,1,0:T(8,128)(2,1)} %pack.1), calls=%async_computation | async-start | bytes 1703936 | tf_op jit(solution)/shard_map/all_to_all | solution.py:405
  34.7 1.3 %collective-permute-start = (f32[2,32,256]{2,1,0:T(8,128)S(1)}, f32[2,32,256]{2,1,0:T(8,128)S(1)}, u32[]{:S(2)}, u32[]{:S(2)}) collective-permute-start(f32[2,32,256]{2,1,0:T(8,128)S(1)} %bitcast.23), channel_id=1, source_target_pairs={{0,1},{1,0},{2,3},{3,2},{4,5},{5,4},{6,7},{7,6},{8,9},{9,8},{10,11... | collective-permute-start | bytes 196616 | tf_op jit(solution)/shard_map/ppermute | solution.py:434
  36.1 4.0 %collective-permute-start.2 = (f32[32,256]{1,0:T(8,128)S(1)}, f32[32,256]{1,0:T(8,128)S(1)}, u32[]{:S(2)}, u32[]{:S(2)}) collective-permute-start(f32[32,256]{1,0:T(8,128)S(1)} %get-tuple-element.14), channel_id=1, source_target_pairs={{8,0},{3,1},{0,2},{7,3},{2,6},{5,7},{6,4},{13,5},{4,12},{15,13},{1... | collective-permute-start | bytes 98312 | tf_op jit(solution)/shard_map/ppermute | solution.py:437
  37.6 3.9 %collective-permute-start.1 = (f32[32,256]{1,0:T(8,128)S(1)}, f32[32,256]{1,0:T(8,128)S(1)}, u32[]{:S(2)}, u32[]{:S(2)}) collective-permute-start(f32[32,256]{1,0:T(8,128)S(1)} %get-tuple-element.15), channel_id=1, source_target_pairs={{0,8},{1,3},{2,0},{3,7},{6,2},{7,5},{4,6},{5,13},{12,4},{13,15},{1... | collective-permute-start | bytes 98312 | tf_op jit(solution)/shard_map/ppermute | solution.py:436
  41.5 13.4 %copy-start = (f32[1,1,18,256]{3,1,2,0:T(1,128)S(1)}, f32[1,1,18,256]{3,1,2,0:T(1,128)}, u32[]{:S(2)}) copy-start(f32[1,1,18,256]{3,1,2,0:T(1,128)} %param.7) | copy-start | bytes 55300
